TPU v7x, 512 devices: a whole 4x8x8 slice. The times are simulated.
512 devices in a mesh: dom: 16 (over y, core), aux: 32 (over x, z).
Axes of the slice: x: 4, y: 8, z: 8, core: 2. Of those that a mesh axis runs over, the one named last changes fastest.
Arguments:
- integrals: bfloat16 [16, 1024, 512, 128], P('dom', 'aux'), may hold values from -0.25 to 0.25
- density: bfloat16 [16, 4, 128, 128], P('dom'), may hold values from -0.25 to 0.25
- dens_cols: int32 [16, 4], replicated, may hold values from 0 to 15, as said below
- neighbours: int32 [16, 4], replicated, may hold values from 0 to 15, as said below
- metric: bfloat16 [16, 1024, 1024], P('dom', 'aux'), may hold values from -0.5 to 2.5, as said below
Outputs:
- exchange: float32 [16, 128, 128], P('dom')
Inputs may be any that keep to these rules, and one draw needn't show every extreme that they name: `neighbours`: in each row the entries are distinct; position 0 holds the row's own block, the others are blocks within cyclic distance 2 of it, both blocks at distance 1 among them. `dens_cols`: in each row the entries are distinct; position 0 holds the row's own block, the others are blocks within cyclic distance 2 of it, both blocks at distance 1 among them. `metric`: each domain's matrix is symmetric.
All inputs are finite; a program needn't handle non-finite values.
Results may differ from a plain program's by a relative error of at most 0.004.
Values may be sent and summed in bfloat16 or wider, within the bound.
No kernel may reach another device: no remote copies, remote signals or barrier semaphores. Data moves between devices by JAX's collectives and lax.ppermute only.
A program may use at most 64 MiB of HBM per device.

v0:
```python
import jax
import jax.numpy as jnp
from jax import lax
from jax.sharding import PartitionSpec as P

RAD = 2


def passed_along(block, axis, distance):
    devices = range(lax.axis_size(axis))
    route = [((i - distance) % len(devices), i) for i in devices]
    return lax.ppermute(block, axis, route)


def body(integrals, density, dens_cols, neighbours, metric):
    domain_count = lax.axis_size("dom")
    my_domain = lax.axis_index("dom")
    block_size = density.shape[2]
    neigh_count = neighbours.shape[1]
    my_blocks = lax.dynamic_index_in_dim(neighbours, my_domain, 0, keepdims=False)
    slab_list = []
    for offset in range(-RAD, RAD + 1):
        if offset == 0:
            slab_list.append(density[0])
        else:
            slab_list.append(passed_along(density, "dom", -offset)[0])
    row_slabs = jnp.stack(slab_list)
    slot_index = (my_blocks - my_domain + RAD) % domain_count
    picked = jnp.take(row_slabs, slot_index, axis=0)
    tile_cols = jnp.take(dens_cols, my_blocks, axis=0)
    matches = (tile_cols[:, None, :] == my_blocks[None, :, None]).astype(jnp.bfloat16)
    dense_tiles = jnp.einsum("jsk,jkab->jasb", matches, picked, preferred_element_type=jnp.float32)
    density_local = dense_tiles.astype(jnp.bfloat16).reshape(
        neigh_count * block_size, neigh_count * block_size
    )
    half_product = jnp.einsum(
        "ls,plm->psm", density_local, integrals[0], preferred_element_type=jnp.float32
    ).astype(jnp.bfloat16)
    half_moved, ints_moved = (
        lax.all_to_all(half_product[None], "aux", split_axis=2, concat_axis=1, tiled=True),
        lax.all_to_all(integrals, "aux", split_axis=2, concat_axis=1, tiled=True),
    )
    columns = ints_moved[0].reshape(ints_moved.shape[1], -1)
    fitted = jnp.dot(
        lax.all_gather(metric, "aux", axis=1, tiled=True)[0],
        columns,
        preferred_element_type=jnp.float32,
    ).astype(jnp.bfloat16)
    fitted = fitted.reshape(half_moved.shape[1:])
    partial_value = jnp.einsum(
        "psm,psn->mn", half_moved[0], fitted, preferred_element_type=jnp.float32
    )
    summed = lax.psum(partial_value, "aux")
    return summed[None]


def solution(mesh):
    return jax.shard_map(
        body,
        mesh=mesh,
        in_specs=(
            P("dom", "aux", None, None),
            P("dom", None, None, None),
            P(),
            P(),
            P("dom", "aux", None),
        ),
        out_specs=P("dom", None, None),
        check_vma=False,
    )
```

profile of v0, /device:TPU:16, one launch (start us, length us, event | category | flops | bytes accessed | tf_op | source)
XLA Modules:
  0.0 421.3 jit_solution(17828483009210059733)
XLA Ops:
  6.5 0.0 copy-start
  6.5 6.9 %copy.30 = bf16[1,32,512,128]{3,1,0,2:T(8,128)(2,1)} copy(bf16[1,32,512,128]{3,2,1,0:T(8,128)(2,1)} %param.5) | data formatting | bytes 8388608 | tf_op args[0]
  13.4 0.0 copy-start.2
  13.4 0.0 copy-start.3
  13.4 13.4 %all-to-all-start.1 = ((bf16[1,32,512,128]{3,1,0,2:T(8,128)(2,1)}), bf16[1,32,512,128]{3,1,0,2:T(8,128)(2,1)}, u32[]{:S(2)}, u32[]{:S(2)}) async-start(bf16[1,32,512,128]{3,1,0,2:T(8,128)(2,1)} %copy.30), calls=%async_computation.1 | async-start | bytes 8388608 | tf_op jit(solution)/shard_map/all_to_all | solution.py:41
  26.8 0.0 copy-done.2
  26.9 3.5 collective-permute-start
  30.3 0.0 collective-permute-start.1
  30.4 1.7 collective-permute-start.2
  32.1 2.3 collective-permute-start.3
  34.5 0.0 copy-done.3
  34.5 0.1 copy.24
  34.6 0.0 copy-done
  34.6 0.2 dynamic-slice_reduce_fusion
  34.8 0.6 gather_fusion.1
  35.4 0.1 broadcast_select_fusion.1
  35.4 0.0 collective-permute-done
  35.5 0.0 collective-permute-done.1
  35.5 0.0 collective-permute-done.2
  35.6 5.1 %collective-permute-done.3 = bf16[1,4,128,128]{3,2,1,0:T(8,128)(2,1)S(1)} collective-permute-done((bf16[1,4,128,128]{3,2,1,0:T(8,128)(2,1)S(1)}, bf16[1,4,128,128]{3,2,1,0:T(8,128)(2,1)S(1)}, u32[]{:S(2)}, u32[]{:S(2)}) %collective-permute-start.3) | collective-permute-done | bytes 131104 | tf_op jit(solution)/shard_map/ppermute | solution.py:12
  40.7 0.6 gather_fusion
  41.3 0.1 broadcast_select_fusion
  41.4 0.6 convolution_convert_fusion
  42.0 4.6 %convert_bitcast_fusion.1 = bf16[1,32,512,128]{3,2,1,0:T(8,128)(2,1)S(1)} fusion(bf16[1,32,512,128]{3,2,1,0:T(8,128)(2,1)} %param.5, bf16[64,8,4,128]{3,2,1,0:T(4,128)(2,1)S(1)} %bitcast.62), kind=kOutput, calls=%fused_computation.8 | convolution fusion | flops 2149580800 | bytes 8912896 | tf_op jit(solution)/shard_map/ls,plm->psm/dot_general | solution.py:36
  46.6 4.6 %copy.27 = bf16[1,32,512,128]{3,1,0,2:T(8,128)(2,1)} copy(bf16[1,32,512,128]{3,2,1,0:T(8,128)(2,1)S(1)} %convert_bitcast_fusion.1) | data formatting | bytes 8388608 | tf_op jit(solution)/shard_map/broadcast_in_dim | solution.py:40
  51.2 72.6 %all-to-all-done.1 = bf16[1,32,512,128]{3,1,0,2:T(8,128)(2,1)} async-done(((bf16[1,32,512,128]{3,1,0,2:T(8,128)(2,1)}), bf16[1,32,512,128]{3,1,0,2:T(8,128)(2,1)}, u32[]{:S(2)}, u32[]{:S(2)}) %all-to-all-start.1) | async-done | bytes 4194336 | tf_op jit(solution)/shard_map/all_to_all | solution.py:41
  123.8 5.1 %all-to-all-start = ((bf16[1,32,512,128]{3,1,0,2:T(8,128)(2,1)}), bf16[1,32,512,128]{3,1,0,2:T(8,128)(2,1)}, u32[]{:S(2)}, u32[]{:S(2)}) async-start(bf16[1,32,512,128]{3,1,0,2:T(8,128)(2,1)} %copy.27), calls=%async_computation | async-start | bytes 8388608 | tf_op jit(solution)/shard_map/all_to_all | solution.py:40
  128.9 0.0 all-gather.2.cloned.1.call-start
  129.0 0.7 all-gather.2.cloned.1.call-update
  129.7 0.2 all-reduce.2.cloned.1.call-start
  129.9 6.1 %copy.31 = bf16[1,32,32,16,128]{4,3,1,2,0:T(8,128)(2,1)} copy(bf16[1,32,32,16,128]{4,1,3,2,0:T(8,128)(2,1)} %bitcast.13) | data formatting | bytes 8388608 | tf_op jit(solution)/shard_map/all_to_all | solution.py:41
  136.0 106.7 %all-gather.2.cloned.1.call-done = bf16[1,1024,1024]{2,1,0:T(8,128)(2,1)} async-done(((bf16[1,32,1024]{2,1,0:T(8,128)(2,1)}), bf16[1,1024,1024]{2,1,0:T(8,128)(2,1)}) %all-gather.2.cloned.1.call-update) | async-done | bytes 2097168 | tf_op jit(solution)/shard_map/all_gather | solution.py:45
  242.6 7.3 %convert_bitcast_fusion = bf16[128,8,16,128]{3,1,2,0:T(8,128)(2,1)S(1)} fusion(bf16[128,8,16,128]{3,2,1,0:T(8,128)(2,1)} %bitcast.60, bf16[1,1024,1024]{2,1,0:T(8,128)(2,1)} %all-gather.2.cloned.1.call-done), kind=kOutput, calls=%fused_computation.7 | convolution fusion | flops 4297064448 | bytes 10485760 | tf_op jit(solution)/shard_map/dot_general | solution.py:44
  250.0 3.4 copy.37
  253.4 0.0 all-to-all-done
  253.4 3.8 copy.28
  257.2 0.0 copy-start.1
  257.2 1.2 copy.29
  258.4 1.0 copy-done.1
  259.4 1.9 convolution_bitcast_fusion
  261.3 0.0 all-reduce.2.cloned.1.call-update
  261.3 151.7 %all-reduce.2.cloned.1.call-done = f32[1,128,128]{2,1,0:T(8,128)} async-done(((f32[1,128,128]{2,1,0:T(8,128)}), f32[1,128,128]{2,1,0:T(8,128)}) %all-reduce.2.cloned.1.call-update) | async-done | bytes 65552 | tf_op jit(solution)/shard_map/psum | solution.py:53
  413.0 1.5 copy.55
  (9 shorter events, 0.1 us)
Async XLA Ops:
  6.5 28.0 %copy-start = (s32[16,4]{0,1:T(4,128)S(1)}, s32[16,4]{0,1:T(4,128)}, u32[]{:S(2)}) copy-start(s32[16,4]{0,1:T(4,128)} %param.8) | copy-start | bytes 772
  13.4 13.4 %copy-start.2 = (bf16[1,4,128,128]{3,2,1,0:T(8,128)(2,1)S(1)}, bf16[1,4,128,128]{3,2,1,0:T(8,128)(2,1)}, u32[]{:S(2)}) copy-start(bf16[1,4,128,128]{3,2,1,0:T(8,128)(2,1)} %param.6) | copy-start | bytes 393220
  13.4 21.1 %copy-start.3 = (s32[16,4]{0,1:T(4,128)S(1)}, s32[16,4]{0,1:T(4,128)}, u32[]{:S(2)}) copy-start(s32[16,4]{0,1:T(4,128)} %param.7) | copy-start | bytes 772
  13.4 110.4 %all-to-all-start.1 = ((bf16[1,32,512,128]{3,1,0,2:T(8,128)(2,1)}), bf16[1,32,512,128]{3,1,0,2:T(8,128)(2,1)}, u32[]{:S(2)}, u32[]{:S(2)}) async-start(bf16[1,32,512,128]{3,1,0,2:T(8,128)(2,1)} %copy.30), calls=%async_computation.1 | async-start | bytes 8388608 | tf_op jit(solution)/shard_map/all_to_all | solution.py:41
  26.9 8.6 %collective-permute-start = (bf16[1,4,128,128]{3,2,1,0:T(8,128)(2,1)S(1)}, bf16[1,4,128,128]{3,2,1,0:T(8,128)(2,1)S(1)}, u32[]{:S(2)}, u32[]{:S(2)}) collective-permute-start(bf16[1,4,128,128]{3,2,1,0:T(8,128)(2,1)S(1)} %copy-done.2), channel_id=1, source_target_pairs={{448,0},{480,32},{0,64},{32,96},{64,128},{96,160},{128,192},{160,2... | collective-permute-start | bytes 393224 | tf_op jit(solution)/shard_map/ppermute | solution.py:12
  30.3 5.1 %collective-permute-start.1 = (bf16[1,4,128,128]{3,2,1,0:T(8,128)(2,1)S(1)}, bf16[1,4,128,128]{3,2,1,0:T(8,128)(2,1)S(1)}, u32[]{:S(2)}, u32[]{:S(2)}) collective-permute-start(bf16[1,4,128,128]{3,2,1,0:T(8,128)(2,1)S(1)} %copy-done.2), channel_id=1, source_target_pairs={{480,0},{0,32},{32,64},{64,96},{96,128},{128,160},{160,192},{192,2... | collective-permute-start | bytes 393224 | tf_op jit(solution)/shard_map/ppermute | solution.py:12
  30.4 5.2 %collective-permute-start.2 = (bf16[1,4,128,128]{3,2,1,0:T(8,128)(2,1)S(1)}, bf16[1,4,128,128]{3,2,1,0:T(8,128)(2,1)S(1)}, u32[]{:S(2)}, u32[]{:S(2)}) collective-permute-start(bf16[1,4,128,128]{3,2,1,0:T(8,128)(2,1)S(1)} %copy-done.2), channel_id=1, source_target_pairs={{32,0},{64,32},{96,64},{128,96},{160,128},{192,160},{224,192},{256... | collective-permute-start | bytes 393224 | tf_op jit(solution)/shard_map/ppermute | solution.py:12
  32.1 8.5 %collective-permute-start.3 = (bf16[1,4,128,128]{3,2,1,0:T(8,128)(2,1)S(1)}, bf16[1,4,128,128]{3,2,1,0:T(8,128)(2,1)S(1)}, u32[]{:S(2)}, u32[]{:S(2)}) collective-permute-start(bf16[1,4,128,128]{3,2,1,0:T(8,128)(2,1)S(1)} %copy-done.2), channel_id=1, source_target_pairs={{64,0},{96,32},{128,64},{160,96},{192,128},{224,160},{256,192},{28... | collective-permute-start | bytes 393224 | tf_op jit(solution)/shard_map/ppermute | solution.py:12
  123.8 129.5 %all-to-all-start = ((bf16[1,32,512,128]{3,1,0,2:T(8,128)(2,1)}), bf16[1,32,512,128]{3,1,0,2:T(8,128)(2,1)}, u32[]{:S(2)}, u32[]{:S(2)}) async-start(bf16[1,32,512,128]{3,1,0,2:T(8,128)(2,1)} %copy.27), calls=%async_computation | async-start | bytes 8388608 | tf_op jit(solution)/shard_map/all_to_all | solution.py:40
  128.9 113.7 %all-gather.2.cloned.1.call-start = ((), (), s32[]{:S(2)}) async-start(), calls=%async_computation.2 | async-start | bytes 2162688 | tf_op jit(solution)/shard_map/all_gather | solution.py:45
  129.7 283.3 %all-reduce.2.cloned.1.call-start = ((), (), s32[]{:S(2)}) async-start(), calls=%async_computation.3 | async-start | bytes 131072 | tf_op jit(solution)/shard_map/psum | solution.py:53
  257.2 2.2 copy-start.1
Sparse Core Ops, SparseCore 0:
  132.9 109.6 all-gather.1
  261.4 151.5 all-reduce.1
where the time goes:
time: 422 us; the launch traced here: 421 us
  waiting for transfers between devices  337 us (80%)
  local copies, waits for them, and re-layouts  30 us (7%)
  starting transfers between devices  26.4 us (6%)
  matrix products  14.4 us (3%)
  between operations  13.6 us (3%)
    psum x1, waiting for transfers between devices, body(): summed = lax.psum(partial_value, 'aux')  152 us
    all_gather x1, waiting for transfers between devices, body(): lax.all_gather(metric, 'aux', axis=1, tiled=True)[0]  107 us
    all_to_all x1, waiting for transfers between devices, body(): lax.all_to_all(integrals, 'aux', split_axis=2, concat_axis=1, tiled=True)  72.6 us
    all_to_all x1, starting transfers between devices, body(): lax.all_to_all(integrals, 'aux', split_axis=2, concat_axis=1, tiled=True)  13.4 us
    unnamed x16, local copies, waits for them, and re-layouts  12.9 us
  transfers between devices with their start and end apart: 8, of which 4 were waited for; matrix products, arithmetic and copies ran while one was open for 7% of the time, Pallas kernels for 0%

commit v1 on v0

v1 whole, which is shorter than its diff:
```python
import jax
import jax.numpy as jnp
from jax import lax
from jax.experimental import pallas as pl
from jax.experimental.pallas import tpu as pltpu
from jax.sharding import PartitionSpec as P

RAD = 2
X_LEN = 4


def passed_along(block, axis, distance):
    devices = range(lax.axis_size(axis))
    route = [((i - distance) % len(devices), i) for i in devices]
    return lax.ppermute(block, axis, route)


def from_grid(block, dx, dz):
    z_len = lax.axis_size("aux") // X_LEN
    route = []
    for x in range(X_LEN):
        for z in range(z_len):
            source = ((x - dx) % X_LEN) * z_len + (z - dz) % z_len
            route.append((source, x * z_len + z))
    return lax.ppermute(block, "aux", route)


def in_order(pieces, here):
    count = len(pieces)
    stack = jnp.stack([pieces[(-k) % count] for k in range(count)])
    twice = jnp.concatenate([stack, stack])
    return lax.dynamic_slice_in_dim(twice, (count - here) % count, count, 0)


def gathered_metric(rows):
    z_len = lax.axis_size("aux") // X_LEN
    me = lax.axis_index("aux")
    my_x, my_z = me // z_len, me % z_len
    up, down = {0: rows}, {0: rows}
    for k in range(1, z_len // 2 + 1):
        up[k] = from_grid(up[k - 1], 0, 1)
        if k < z_len // 2:
            down[k] = from_grid(down[k - 1], 0, -1)
    pieces = [up[k] if k <= z_len // 2 else down[z_len - k] for k in range(z_len)]
    line = in_order(pieces, my_z).reshape(z_len * rows.shape[0], rows.shape[1])
    sides = [line, from_grid(line, 1, 0), from_grid(line, 2, 0), from_grid(line, 3, 0)]
    return in_order(sides, my_x).reshape(-1, rows.shape[1])


def fit_kernel(metric_ref, ints_ref, out_ref):
    parts, width, depth, cols = ints_ref.shape
    for w in range(width):
        right = ints_ref[:, w].reshape(parts * depth, cols)
        out_ref[w] = lax.dot_general(
            right, metric_ref[...], (((0,), (1,)), ((), ())),
            preferred_element_type=jnp.float32,
        ).astype(out_ref.dtype)


def fit(metric, ints):
    parts, slots, depth, cols = ints.shape
    width = 2
    rows = parts * depth
    return pl.pallas_call(
        fit_kernel,
        out_shape=jax.ShapeDtypeStruct((slots, cols, rows), ints.dtype),
        grid=(slots // width,),
        in_specs=[
            pl.BlockSpec((rows, rows), lambda i: (0, 0)),
            pl.BlockSpec((parts, width, depth, cols), lambda i: (0, i, 0, 0)),
        ],
        out_specs=pl.BlockSpec((width, cols, rows), lambda i: (i, 0, 0)),
        compiler_params=pltpu.CompilerParams(vmem_limit_bytes=24 << 20),
        cost_estimate=pl.CostEstimate(
            flops=2 * rows * rows * slots * cols,
            bytes_accessed=2 * rows * rows + 4 * rows * slots * cols,
            transcendentals=0,
        ),
    )(metric, ints)


def close_kernel(fitted_ref, half_ref, out_ref, total_ref):
    step = pl.program_id(0)
    parts, width, depth, cols = half_ref.shape

    @pl.when(step == 0)
    def _():
        total_ref[...] = jnp.zeros_like(total_ref)

    total = total_ref[...]
    for w in range(width):
        right = half_ref[:, w].reshape(parts * depth, cols)
        total += jnp.dot(fitted_ref[w], right, preferred_element_type=jnp.float32)
    total_ref[...] = total

    @pl.when(step == pl.num_programs(0) - 1)
    def _():
        out_ref[...] = total_ref[...].T


def close(fitted, half):
    parts, slots, depth, cols = half.shape
    width = 4
    rows = parts * depth
    return pl.pallas_call(
        close_kernel,
        out_shape=jax.ShapeDtypeStruct((cols, cols), jnp.float32),
        grid=(slots // width,),
        in_specs=[
            pl.BlockSpec((width, cols, rows), lambda i: (i, 0, 0)),
            pl.BlockSpec((parts, width, depth, cols), lambda i: (0, i, 0, 0)),
        ],
        out_specs=pl.BlockSpec((cols, cols), lambda i: (0, 0)),
        scratch_shapes=[pltpu.VMEM((cols, cols), jnp.float32)],
        compiler_params=pltpu.CompilerParams(vmem_limit_bytes=24 << 20),
        cost_estimate=pl.CostEstimate(
            flops=2 * rows * slots * cols * cols,
            bytes_accessed=4 * rows * slots * cols,
            transcendentals=0,
        ),
    )(fitted, half)


def local_density(density, dens_cols, neighbours):
    domain_count = lax.axis_size("dom")
    my_domain = lax.axis_index("dom")
    block_size = density.shape[2]
    neigh_count = neighbours.shape[1]
    my_blocks = lax.dynamic_index_in_dim(neighbours, my_domain, 0, keepdims=False)
    slabs = []
    for offset in range(-RAD, RAD + 1):
        slabs.append(density[0] if offset == 0 else passed_along(density, "dom", -offset)[0])
    row_slabs = jnp.stack(slabs)
    slot_index = (my_blocks - my_domain + RAD) % domain_count
    picked = jnp.take(row_slabs, slot_index, axis=0)
    tile_cols = jnp.take(dens_cols, my_blocks, axis=0)
    matches = (tile_cols[:, None, :] == my_blocks[None, :, None]).astype(jnp.bfloat16)
    tiles = jnp.einsum("jsk,jkab->jasb", matches, picked, preferred_element_type=jnp.float32)
    order = neigh_count * block_size
    return tiles.astype(jnp.bfloat16).reshape(order, order)


def exchanged(array):
    group = lax.axis_size("aux")
    count, slots, cols = array.shape
    by_slot = array.transpose(1, 0, 2).reshape(group, slots // group, count, cols)
    return lax.all_to_all(by_slot, "aux", split_axis=0, concat_axis=0, tiled=True)


def summed(partial):
    group = lax.axis_size("aux")
    rows, cols = partial.shape
    slices = partial.reshape(group, rows // group, cols)
    parts = lax.all_to_all(slices, "aux", split_axis=0, concat_axis=0, tiled=True)
    mine = jnp.sum(parts, axis=0)
    copies = jnp.broadcast_to(mine[None], slices.shape)
    whole = lax.all_to_all(copies, "aux", split_axis=0, concat_axis=0, tiled=True)
    return whole.reshape(rows, cols)


def body(integrals, density, dens_cols, neighbours, metric):
    ints = integrals[0]
    ints_moved = exchanged(ints)
    dense = local_density(density, dens_cols, neighbours)
    half = jnp.einsum("ls,plm->psm", dense, ints, preferred_element_type=jnp.float32)
    half_moved = exchanged(half.astype(jnp.bfloat16))
    fitted = fit(gathered_metric(metric[0]), ints_moved)
    partial = close(fitted, half_moved)
    return summed(partial)[None]


def solution(mesh):
    return jax.shard_map(
        body,
        mesh=mesh,
        in_specs=(
            P("dom", "aux", None, None),
            P("dom", None, None, None),
            P(),
            P(),
            P("dom", "aux", None),
        ),
        out_specs=P("dom", None, None),
        check_vma=False,
    )
```

time: 422 us -> 325 us (0.77)
  the two profiles are of different devices: /device:TPU:16 before, /device:TPU:32 now
where the time goes in v1:
time: 325 us; the launch traced here: 324 us
  waiting for transfers between devices  192 us (59%)
  starting transfers between devices  59.8 us (18%)
  blocking collectives  30.8 us (9%)
  local copies, waits for them, and re-layouts  18.5 us (6%)
  Pallas kernels  17.4 us (5%)
  matrix products  5.12 us (2%)
    ppermute x10, waiting for transfers between devices, from_grid(): return lax.ppermute(block, 'aux', route)  115 us
    all_to_all x2, waiting for transfers between devices, exchanged(): lax.all_to_all(by_slot, 'aux', split_axis=0, concat_axis=0, tiled=True)  74 us
    ppermute x10, starting transfers between devices, from_grid(): return lax.ppermute(block, 'aux', route)  32.3 us
    all_to_all x2, starting transfers between devices, exchanged(): lax.all_to_all(by_slot, 'aux', split_axis=0, concat_axis=0, tiled=True)  18.7 us
    all_to_all x1, blocking collectives, summed(): lax.all_to_all(slices, 'aux', split_axis=0, concat_axis=0, tiled=True)  17.7 us
    pallas_call x1, Pallas kernels, fit(): pl.pallas_call(fit_kernel, out_shape=jax.ShapeDtypeStruct((slots, cols, r...  13.4 us
    all_to_all x1, blocking collectives, summed(): lax.all_to_all(copies, 'aux', split_axis=0, concat_axis=0, tiled=True)  13.1 us
    ppermute x4, starting transfers between devices, passed_along(): return lax.ppermute(block, axis, route)  8.79 us
  transfers between devices with their start and end apart: 16, of which 8 were waited for; matrix products, arithmetic and copies ran while one was open for 4% of the time, Pallas kernels for 4%

profile of v1, /device:TPU:32, one launch (start us, length us, event | category | flops | bytes accessed | tf_op | source)
XLA Modules:
  0.0 324.0 jit_solution(6419810338821040209)
XLA Ops:
  0.0 6.8 %copy.6 = bf16[512,32,128]{2,1,0:T(8,128)(2,1)} copy(bf16[512,32,128]{2,0,1:T(8,128)(2,1)} %bitcast.83) | data formatting | bytes 8388608 | tf_op jit(solution)/shard_map/transpose | solution.py:146
  6.9 13.4 %all-to-all-start = ((bf16[32,16,32,128]{3,2,1,0:T(8,128)(2,1)}), bf16[32,16,32,128]{3,2,1,0:T(8,128)(2,1)}, u32[]{:S(2)}, u32[]{:S(2)}) async-start(bf16[32,16,32,128]{3,2,1,0:T(8,128)(2,1)} %bitcast.77), calls=%async_computation | async-start | bytes 8388608 | tf_op jit(solution)/shard_map/all_to_all | solution.py:147
  20.3 2.6 collective-permute-start.10
  22.9 0.0 collective-permute-start.11
  22.9 2.9 collective-permute-start.12
  25.9 3.2 %collective-permute-start.13 = (bf16[1,4,128,128]{3,2,1,0:T(8,128)(2,1)S(1)}, bf16[1,4,128,128]{3,2,1,0:T(8,128)(2,1)S(1)}, u32[]{:S(2)}, u32[]{:S(2)}) collective-permute-start(bf16[1,4,128,128]{3,2,1,0:T(8,128)(2,1)S(1)} %copy-done.4), channel_id=1, source_target_pairs={{64,0},{96,32},{128,64},{160,96},{192,128},{224,160},{256,192},{28... | collective-permute-start | bytes 393224 | tf_op jit(solution)/shard_map/ppermute | solution.py:15
  29.1 0.1 copy.7
  29.2 0.2 dynamic-slice_reduce_fusion
  29.4 0.6 gather_fusion.1
  30.0 0.1 broadcast_select_fusion.1
  30.1 0.0 collective-permute-done.10
  30.1 0.0 collective-permute-done.11
  30.2 2.5 collective-permute-done.13
  32.7 0.6 gather_fusion
  33.4 0.1 broadcast_select_fusion
  33.5 0.6 convolution_convert_fusion
  34.1 4.6 %fusion.2 = bf16[512,32,128]{2,0,1:T(8,128)(2,1)S(1)} fusion(bf16[1,32,512,128]{3,2,1,0:T(8,128)(2,1)} %param.5, bf16[64,8,4,128]{3,2,1,0:T(4,128)(2,1)S(1)} %bitcast.87), kind=kOutput, calls=%fused_computation.4 | convolution fusion | flops 2149580800 | bytes 8912896 | tf_op jit(solution)/shard_map/ls,plm->psm/dot_general | solution.py:165
  38.6 4.7 %copy.10 = bf16[512,32,128]{2,1,0:T(8,128)(2,1)} copy(bf16[512,32,128]{2,0,1:T(8,128)(2,1)S(1)} %fusion.2) | data formatting | bytes 8388608 | tf_op jit(solution)/shard_map/convert_element_type | solution.py:166
  43.3 74.0 %all-to-all-done.ints_ref = bf16[32,16,32,128]{3,2,1,0:T(8,128)(2,1)} async-done(((bf16[32,16,32,128]{3,2,1,0:T(8,128)(2,1)}), bf16[32,16,32,128]{3,2,1,0:T(8,128)(2,1)}, u32[]{:S(2)}, u32[]{:S(2)}) %all-to-all-start) | async-done | bytes 4194336 | tf_op jit(solution)/shard_map/all_to_all | solution.py:147
  117.3 5.2 %all-to-all-start.1 = ((bf16[32,16,32,128]{3,2,1,0:T(8,128)(2,1)}), bf16[32,16,32,128]{3,2,1,0:T(8,128)(2,1)}, u32[]{:S(2)}, u32[]{:S(2)}) async-start(bf16[32,16,32,128]{3,2,1,0:T(8,128)(2,1)} %bitcast.76), calls=%async_computation.1 | async-start | bytes 8388608 | tf_op jit(solution)/shard_map/all_to_all | solution.py:147
  122.5 4.8 %collective-permute-start = (bf16[32,1024]{1,0:T(8,128)(2,1)S(1)}, bf16[32,1024]{1,0:T(8,128)(2,1)S(1)}, u32[]{:S(2)}, u32[]{:S(2)}) collective-permute-start(bf16[32,1024]{1,0:T(8,128)(2,1)S(1)} %bitcast.84), channel_id=1, source_target_pairs={{1,0},{2,1},{3,2},{4,3},{5,4},{6,5},{7,6},{0,7},{9,8},{10,9},{11,1... | collective-permute-start | bytes 196616 | tf_op jit(solution)/shard_map/ppermute | solution.py:25
  127.4 1.9 collective-permute-start.3
  129.3 85.5 %collective-permute-done = bf16[32,1024]{1,0:T(8,128)(2,1)S(1)} collective-permute-done((bf16[32,1024]{1,0:T(8,128)(2,1)S(1)}, bf16[32,1024]{1,0:T(8,128)(2,1)S(1)}, u32[]{:S(2)}, u32[]{:S(2)}) %collective-permute-start) | collective-permute-done | bytes 65568 | tf_op jit(solution)/shard_map/ppermute | solution.py:25
  214.9 4.2 %collective-permute-start.1 = (bf16[32,1024]{1,0:T(8,128)(2,1)S(1)}, bf16[32,1024]{1,0:T(8,128)(2,1)S(1)}, u32[]{:S(2)}, u32[]{:S(2)}) collective-permute-start(bf16[32,1024]{1,0:T(8,128)(2,1)S(1)} %collective-permute-done), channel_id=1, source_target_pairs={{1,0},{2,1},{3,2},{4,3},{5,4},{6,5},{7,6},{0,7},{9,8},{10,9},{11,1... | collective-permute-start | bytes 196616 | tf_op jit(solution)/shard_map/ppermute | solution.py:25
  219.1 0.0 collective-permute-done.3
  219.1 1.9 collective-permute-start.4
  221.0 0.2 collective-permute-done.1
  221.3 5.2 %collective-permute-start.2 = (bf16[32,1024]{1,0:T(8,128)(2,1)S(1)}, bf16[32,1024]{1,0:T(8,128)(2,1)S(1)}, u32[]{:S(2)}, u32[]{:S(2)}) collective-permute-start(bf16[32,1024]{1,0:T(8,128)(2,1)S(1)} %collective-permute-done.1), channel_id=1, source_target_pairs={{1,0},{2,1},{3,2},{4,3},{5,4},{6,5},{7,6},{0,7},{9,8},{10,9},{11,1... | collective-permute-start | bytes 196616 | tf_op jit(solution)/shard_map/ppermute | solution.py:25
  226.4 0.0 collective-permute-done.4
  226.5 1.9 collective-permute-start.5
  228.4 5.4 %collective-permute-done.5 = bf16[32,1024]{1,0:T(8,128)(2,1)S(1)} collective-permute-done((bf16[32,1024]{1,0:T(8,128)(2,1)S(1)}, bf16[32,1024]{1,0:T(8,128)(2,1)S(1)}, u32[]{:S(2)}, u32[]{:S(2)}) %collective-permute-start.5) | collective-permute-done | bytes 65568 | tf_op jit(solution)/shard_map/ppermute | solution.py:25
  233.8 1.9 collective-permute-start.6
  235.7 0.0 collective-permute-done.2
  235.8 5.4 %collective-permute-done.6 = bf16[32,1024]{1,0:T(8,128)(2,1)S(1)} collective-permute-done((bf16[32,1024]{1,0:T(8,128)(2,1)S(1)}, bf16[32,1024]{1,0:T(8,128)(2,1)S(1)}, u32[]{:S(2)}, u32[]{:S(2)}) %collective-permute-start.6) | collective-permute-done | bytes 65568 | tf_op jit(solution)/shard_map/ppermute | solution.py:25
  241.4 4.8 %collective-permute-start.7 = (bf16[256,1024]{1,0:T(8,128)(2,1)S(1)}, bf16[256,1024]{1,0:T(8,128)(2,1)S(1)}, u32[]{:S(2)}, u32[]{:S(2)}) collective-permute-start(bf16[256,1024]{1,0:T(8,128)(2,1)S(1)} %bitcast.78), channel_id=1, source_target_pairs={{8,0},{9,1},{10,2},{11,3},{12,4},{13,5},{14,6},{15,7},{16,8},{17,9... | collective-permute-start | bytes 1572872 | tf_op jit(solution)/shard_map/ppermute | solution.py:25
  246.2 2.7 collective-permute-start.8
  249.0 3.0 collective-permute-start.9
  252.0 13.0 %collective-permute-done.7 = bf16[256,1024]{1,0:T(8,128)(2,1)S(1)} collective-permute-done((bf16[256,1024]{1,0:T(8,128)(2,1)S(1)}, bf16[256,1024]{1,0:T(8,128)(2,1)S(1)}, u32[]{:S(2)}, u32[]{:S(2)}) %collective-permute-start.7) | collective-permute-done | bytes 524320 | tf_op jit(solution)/shard_map/ppermute | solution.py:25
  265.0 0.0 collective-permute-done.8
  265.0 5.5 %collective-permute-done.9 = bf16[256,1024]{1,0:T(8,128)(2,1)S(1)} collective-permute-done((bf16[256,1024]{1,0:T(8,128)(2,1)S(1)}, bf16[256,1024]{1,0:T(8,128)(2,1)S(1)}, u32[]{:S(2)}, u32[]{:S(2)}) %collective-permute-start.9) | collective-permute-done | bytes 524320 | tf_op jit(solution)/shard_map/ppermute | solution.py:25
  270.8 0.2 constant_dynamic-slice_fusion
  271.0 13.4 %shard_map.55.fitted_ref = bf16[16,128,1024]{2,1,0:T(8,128)(2,1)S(1)} custom-call(bf16[1024,1024]{1,0:T(8,128)(2,1)S(1)} %bitcast.74, bf16[32,16,32,128]{3,2,1,0:T(8,128)(2,1)} %all-to-all-done.ints_ref), custom_call_target="tpu_custom_call" | custom-call | flops 4294967296 | bytes 10485760 | tf_op jit(solution)/shard_map/pallas_call | solution.py:64
  284.4 2.0 copy-done.1
  286.3 2.2 copy-done.2
  288.5 4.0 %shard_map.56 = f32[128,128]{1,0:T(8,128)S(1)} custom-call(bf16[16,128,1024]{2,1,0:T(8,128)(2,1)S(1)} %copy-done.2, bf16[32,16,32,128]{3,2,1,0:T(8,128)(2,1)} %all-to-all-done.1.half_ref), custom_call_target="tpu_custom_call" | custom-call | flops 536870912 | bytes 8388608 | tf_op jit(solution)/shard_map/pallas_call | solution.py:105
  292.5 17.7 %all_to_all.20 = f32[32,4,128]{2,1,0:T(4,128)S(1)} all-to-all(f32[32,4,128]{2,1,0:T(4,128)S(1)} %bitcast.75), channel_id=1, replica_groups=mesh['dom'=16,'aux'=32] {'aux'}, dimensions={0} | all-to-all | bytes 131072 | tf_op jit(solution)/shard_map/all_to_all | solution.py:154
  310.3 13.1 %all_to_all.21 = f32[32,4,128]{2,1,0:T(4,128)S(1)} all-to-all(f32[32,4,128]{2,1,0:T(4,128)S(1)} %broadcast_in_dim.27), channel_id=1, replica_groups=mesh['dom'=16,'aux'=32] {'aux'}, dimensions={0} | all-to-all | bytes 131072 | tf_op jit(solution)/shard_map/all_to_all | solution.py:157
  323.4 0.6 copy.48
  (48 shorter events, 0.6 us)
Async XLA Ops:
  0.0 29.2 %copy-start = (s32[16,4]{0,1:T(4,128)S(1)}, s32[16,4]{0,1:T(4,128)}, u32[]{:S(2)}) copy-start(s32[16,4]{0,1:T(4,128)} %param.8) | copy-start | bytes 772
  6.9 13.4 %copy-start.4 = (bf16[1,4,128,128]{3,2,1,0:T(8,128)(2,1)S(1)}, bf16[1,4,128,128]{3,2,1,0:T(8,128)(2,1)}, u32[]{:S(2)}) copy-start(bf16[1,4,128,128]{3,2,1,0:T(8,128)(2,1)} %param.6) | copy-start | bytes 393220
  6.9 22.3 %copy-start.5 = (s32[16,4]{0,1:T(4,128)S(1)}, s32[16,4]{0,1:T(4,128)}, u32[]{:S(2)}) copy-start(s32[16,4]{0,1:T(4,128)} %param.7) | copy-start | bytes 772
  6.9 110.4 %all-to-all-start = ((bf16[32,16,32,128]{3,2,1,0:T(8,128)(2,1)}), bf16[32,16,32,128]{3,2,1,0:T(8,128)(2,1)}, u32[]{:S(2)}, u32[]{:S(2)}) async-start(bf16[32,16,32,128]{3,2,1,0:T(8,128)(2,1)} %bitcast.77), calls=%async_computation | async-start | bytes 8388608 | tf_op jit(solution)/shard_map/all_to_all | solution.py:147
  20.3 9.8 %collective-permute-start.10 = (bf16[1,4,128,128]{3,2,1,0:T(8,128)(2,1)S(1)}, bf16[1,4,128,128]{3,2,1,0:T(8,128)(2,1)S(1)}, u32[]{:S(2)}, u32[]{:S(2)}) collective-permute-start(bf16[1,4,128,128]{3,2,1,0:T(8,128)(2,1)S(1)} %copy-done.4), channel_id=1, source_target_pairs={{448,0},{480,32},{0,64},{32,96},{64,128},{96,160},{128,192},{160,2... | collective-permute-start | bytes 393224 | tf_op jit(solution)/shard_map/ppermute | solution.py:15
  22.9 7.2 %collective-permute-start.11 = (bf16[1,4,128,128]{3,2,1,0:T(8,128)(2,1)S(1)}, bf16[1,4,128,128]{3,2,1,0:T(8,128)(2,1)S(1)}, u32[]{:S(2)}, u32[]{:S(2)}) collective-permute-start(bf16[1,4,128,128]{3,2,1,0:T(8,128)(2,1)S(1)} %copy-done.4), channel_id=1, source_target_pairs={{480,0},{0,32},{32,64},{64,96},{96,128},{128,160},{160,192},{192,2... | collective-permute-start | bytes 393224 | tf_op jit(solution)/shard_map/ppermute | solution.py:15
  22.9 7.3 %collective-permute-start.12 = (bf16[1,4,128,128]{3,2,1,0:T(8,128)(2,1)S(1)}, bf16[1,4,128,128]{3,2,1,0:T(8,128)(2,1)S(1)}, u32[]{:S(2)}, u32[]{:S(2)}) collective-permute-start(bf16[1,4,128,128]{3,2,1,0:T(8,128)(2,1)S(1)} %copy-done.4), channel_id=1, source_target_pairs={{32,0},{64,32},{96,64},{128,96},{160,128},{192,160},{224,192},{256... | collective-permute-start | bytes 393224 | tf_op jit(solution)/shard_map/ppermute | solution.py:15
  25.9 6.8 %collective-permute-start.13 = (bf16[1,4,128,128]{3,2,1,0:T(8,128)(2,1)S(1)}, bf16[1,4,128,128]{3,2,1,0:T(8,128)(2,1)S(1)}, u32[]{:S(2)}, u32[]{:S(2)}) collective-permute-start(bf16[1,4,128,128]{3,2,1,0:T(8,128)(2,1)S(1)} %copy-done.4), channel_id=1, source_target_pairs={{64,0},{96,32},{128,64},{160,96},{192,128},{224,160},{256,192},{28... | collective-permute-start | bytes 393224 | tf_op jit(solution)/shard_map/ppermute | solution.py:15
  117.3 5.2 %copy-start.3 = (bf16[1,32,1024]{2,1,0:T(8,128)(2,1)S(1)}, bf16[1,32,1024]{2,1,0:T(8,128)(2,1)}, u32[]{:S(2)}) copy-start(bf16[1,32,1024]{2,1,0:T(8,128)(2,1)} %param.9) | copy-start | bytes 196612
  117.3 169.0 %all-to-all-start.1 = ((bf16[32,16,32,128]{3,2,1,0:T(8,128)(2,1)}), bf16[32,16,32,128]{3,2,1,0:T(8,128)(2,1)}, u32[]{:S(2)}, u32[]{:S(2)}) async-start(bf16[32,16,32,128]{3,2,1,0:T(8,128)(2,1)} %bitcast.76), calls=%async_computation.1 | async-start | bytes 8388608 | tf_op jit(solution)/shard_map/all_to_all | solution.py:147
  122.5 92.4 %collective-permute-start = (bf16[32,1024]{1,0:T(8,128)(2,1)S(1)}, bf16[32,1024]{1,0:T(8,128)(2,1)S(1)}, u32[]{:S(2)}, u32[]{:S(2)}) collective-permute-start(bf16[32,1024]{1,0:T(8,128)(2,1)S(1)} %bitcast.84), channel_id=1, source_target_pairs={{1,0},{2,1},{3,2},{4,3},{5,4},{6,5},{7,6},{0,7},{9,8},{10,9},{11,1... | collective-permute-start | bytes 196616 | tf_op jit(solution)/shard_map/ppermute | solution.py:25
  127.4 91.7 %collective-permute-start.3 = (bf16[32,1024]{1,0:T(8,128)(2,1)S(1)}, bf16[32,1024]{1,0:T(8,128)(2,1)S(1)}, u32[]{:S(2)}, u32[]{:S(2)}) collective-permute-start(bf16[32,1024]{1,0:T(8,128)(2,1)S(1)} %bitcast.85), channel_id=1, source_target_pairs={{7,0},{0,1},{1,2},{2,3},{3,4},{4,5},{5,6},{6,7},{15,8},{8,9},{9,10... | collective-permute-start | bytes 196616 | tf_op jit(solution)/shard_map/ppermute | solution.py:25
  214.9 6.4 %collective-permute-start.1 = (bf16[32,1024]{1,0:T(8,128)(2,1)S(1)}, bf16[32,1024]{1,0:T(8,128)(2,1)S(1)}, u32[]{:S(2)}, u32[]{:S(2)}) collective-permute-start(bf16[32,1024]{1,0:T(8,128)(2,1)S(1)} %collective-permute-done), channel_id=1, source_target_pairs={{1,0},{2,1},{3,2},{4,3},{5,4},{6,5},{7,6},{0,7},{9,8},{10,9},{11,1... | collective-permute-start | bytes 196616 | tf_op jit(solution)/shard_map/ppermute | solution.py:25
  219.1 7.4 %collective-permute-start.4 = (bf16[32,1024]{1,0:T(8,128)(2,1)S(1)}, bf16[32,1024]{1,0:T(8,128)(2,1)S(1)}, u32[]{:S(2)}, u32[]{:S(2)}) collective-permute-start(bf16[32,1024]{1,0:T(8,128)(2,1)S(1)} %collective-permute-done.3), channel_id=1, source_target_pairs={{7,0},{0,1},{1,2},{2,3},{3,4},{4,5},{5,6},{6,7},{15,8},{8,9},{9,10... | collective-permute-start | bytes 196616 | tf_op jit(solution)/shard_map/ppermute | solution.py:25
  221.3 14.5 %collective-permute-start.2 = (bf16[32,1024]{1,0:T(8,128)(2,1)S(1)}, bf16[32,1024]{1,0:T(8,128)(2,1)S(1)}, u32[]{:S(2)}, u32[]{:S(2)}) collective-permute-start(bf16[32,1024]{1,0:T(8,128)(2,1)S(1)} %collective-permute-done.1), channel_id=1, source_target_pairs={{1,0},{2,1},{3,2},{4,3},{5,4},{6,5},{7,6},{0,7},{9,8},{10,9},{11,1... | collective-permute-start | bytes 196616 | tf_op jit(solution)/shard_map/ppermute | solution.py:25
  226.5 7.4 %collective-permute-start.5 = (bf16[32,1024]{1,0:T(8,128)(2,1)S(1)}, bf16[32,1024]{1,0:T(8,128)(2,1)S(1)}, u32[]{:S(2)}, u32[]{:S(2)}) collective-permute-start(bf16[32,1024]{1,0:T(8,128)(2,1)S(1)} %collective-permute-done.4), channel_id=1, source_target_pairs={{7,0},{0,1},{1,2},{2,3},{3,4},{4,5},{5,6},{6,7},{15,8},{8,9},{9,10... | collective-permute-start | bytes 196616 | tf_op jit(solution)/shard_map/ppermute | solution.py:25
  233.8 7.4 %collective-permute-start.6 = (bf16[32,1024]{1,0:T(8,128)(2,1)S(1)}, bf16[32,1024]{1,0:T(8,128)(2,1)S(1)}, u32[]{:S(2)}, u32[]{:S(2)}) collective-permute-start(bf16[32,1024]{1,0:T(8,128)(2,1)S(1)} %collective-permute-done.5), channel_id=1, source_target_pairs={{7,0},{0,1},{1,2},{2,3},{3,4},{4,5},{5,6},{6,7},{15,8},{8,9},{9,10... | collective-permute-start | bytes 196616 | tf_op jit(solution)/shard_map/ppermute | solution.py:25
  241.4 23.5 %collective-permute-start.7 = (bf16[256,1024]{1,0:T(8,128)(2,1)S(1)}, bf16[256,1024]{1,0:T(8,128)(2,1)S(1)}, u32[]{:S(2)}, u32[]{:S(2)}) collective-permute-start(bf16[256,1024]{1,0:T(8,128)(2,1)S(1)} %bitcast.78), channel_id=1, source_target_pairs={{8,0},{9,1},{10,2},{11,3},{12,4},{13,5},{14,6},{15,7},{16,8},{17,9... | collective-permute-start | bytes 1572872 | tf_op jit(solution)/shard_map/ppermute | solution.py:25
  246.2 18.8 %collective-permute-start.8 = (bf16[256,1024]{1,0:T(8,128)(2,1)S(1)}, bf16[256,1024]{1,0:T(8,128)(2,1)S(1)}, u32[]{:S(2)}, u32[]{:S(2)}) collective-permute-start(bf16[256,1024]{1,0:T(8,128)(2,1)S(1)} %bitcast.79), channel_id=1, source_target_pairs={{16,0},{17,1},{18,2},{19,3},{20,4},{21,5},{22,6},{23,7},{24,8},{25... | collective-permute-start | bytes 1572872 | tf_op jit(solution)/shard_map/ppermute | solution.py:25
  249.0 21.6 %collective-permute-start.9 = (bf16[256,1024]{1,0:T(8,128)(2,1)S(1)}, bf16[256,1024]{1,0:T(8,128)(2,1)S(1)}, u32[]{:S(2)}, u32[]{:S(2)}) collective-permute-start(bf16[256,1024]{1,0:T(8,128)(2,1)S(1)} %bitcast.80), channel_id=1, source_target_pairs={{24,0},{25,1},{26,2},{27,3},{28,4},{29,5},{30,6},{31,7},{0,8},{1,9... | collective-permute-start | bytes 1572872 | tf_op jit(solution)/shard_map/ppermute | solution.py:25
  284.3 2.0 copy-start.1
  286.3 2.2 copy-start.2

commit v2 on v1

v2 whole, which is shorter than its diff:
```python
import jax
import jax.numpy as jnp
from jax import lax
from jax.experimental import pallas as pl
from jax.experimental.pallas import tpu as pltpu
from jax.sharding import PartitionSpec as P


RAD = 2
X_LEN = 4


def passed_along(block, axis, distance):
    devices = range(lax.axis_size(axis))
    route = [((i - distance) % len(devices), i) for i in devices]
    return lax.ppermute(block, axis, route)


def from_x(block, distance):
    count = lax.axis_size("aux")
    z_len = count // X_LEN
    route = [((i - distance * z_len) % count, i) for i in range(count)]
    return lax.ppermute(block, "aux", route)


def groups_along(which):
    z_len = lax.axis_size("aux") // X_LEN
    lines = [[x * z_len + z for z in range(z_len)] for x in range(X_LEN)]
    return lines if which == "z" else [list(line) for line in zip(*lines)]


def to_all(copies, which):
    return lax.all_to_all(
        copies, "aux", split_axis=0, concat_axis=0, tiled=True,
        axis_index_groups=groups_along(which),
    )


def fit_kernel(x_ref, *refs):
    *metric_refs, ints_ref, out_ref = refs
    parts, width, depth, cols = ints_ref.shape
    count = len(metric_refs)
    for w in range(width):
        right = ints_ref[:, w].reshape(parts * depth, cols)
        for k, metric_ref in enumerate(metric_refs):
            rows = metric_ref.shape[0]
            place = lax.rem(x_ref[0] + (count - k), count)
            start = pl.multiple_of(place * rows, rows)
            out_ref[w, :, pl.ds(start, rows)] = lax.dot_general(
                right, metric_ref[...], (((0,), (1,)), ((), ())),
                preferred_element_type=jnp.float32,
            ).astype(out_ref.dtype)


def fit(metric_parts, my_x, ints):
    parts, slots, depth, cols = ints.shape
    width = 2
    rows = parts * depth
    metric_spec = pl.BlockSpec(metric_parts[0].shape, lambda i, x: (0, 0))
    return pl.pallas_call(
        fit_kernel,
        out_shape=jax.ShapeDtypeStruct((slots, cols, rows), ints.dtype),
        grid_spec=pltpu.PrefetchScalarGridSpec(
            num_scalar_prefetch=1,
            grid=(slots // width,),
            in_specs=[metric_spec] * len(metric_parts) + [
                pl.BlockSpec((parts, width, depth, cols), lambda i, x: (0, i, 0, 0)),
            ],
            out_specs=pl.BlockSpec((width, cols, rows), lambda i, x: (i, 0, 0)),
        ),
        compiler_params=pltpu.CompilerParams(vmem_limit_bytes=24 << 20),
        cost_estimate=pl.CostEstimate(
            flops=2 * rows * rows * slots * cols,
            bytes_accessed=2 * rows * rows + 4 * rows * slots * cols,
            transcendentals=0,
        ),
    )(my_x, *metric_parts, ints)


def close_kernel(fitted_ref, half_ref, out_ref, total_ref):
    step = pl.program_id(0)
    parts, width, depth, cols = half_ref.shape

    @pl.when(step == 0)
    def _():
        total_ref[...] = jnp.zeros_like(total_ref)

    total = total_ref[...]
    for w in range(width):
        right = half_ref[:, w].reshape(parts * depth, cols)
        total += jnp.dot(fitted_ref[w], right, preferred_element_type=jnp.float32)
    total_ref[...] = total

    @pl.when(step == pl.num_programs(0) - 1)
    def _():
        done = total_ref[...].T
        for k in range(out_ref.shape[0]):
            out_ref[k] = done


def close(fitted, half):
    parts, slots, depth, cols = half.shape
    width = 4
    rows = parts * depth
    return pl.pallas_call(
        close_kernel,
        out_shape=jax.ShapeDtypeStruct((X_LEN, cols, cols), jnp.float32),
        grid=(slots // width,),
        in_specs=[
            pl.BlockSpec((width, cols, rows), lambda i: (i, 0, 0)),
            pl.BlockSpec((parts, width, depth, cols), lambda i: (0, i, 0, 0)),
        ],
        out_specs=pl.BlockSpec((X_LEN, cols, cols), lambda i: (0, 0, 0)),
        scratch_shapes=[pltpu.VMEM((cols, cols), jnp.float32)],
        compiler_params=pltpu.CompilerParams(vmem_limit_bytes=24 << 20),
        cost_estimate=pl.CostEstimate(
            flops=2 * rows * slots * cols * cols,
            bytes_accessed=4 * rows * slots * cols,
            transcendentals=0,
        ),
    )(fitted, half)


def local_density(density, dens_cols, neighbours):
    domain_count = lax.axis_size("dom")
    my_domain = lax.axis_index("dom")
    block_size = density.shape[2]
    neigh_count = neighbours.shape[1]
    my_blocks = lax.dynamic_index_in_dim(neighbours, my_domain, 0, keepdims=False)
    slabs = []
    for offset in range(-RAD, RAD + 1):
        slabs.append(density[0] if offset == 0 else passed_along(density, "dom", -offset)[0])
    row_slabs = jnp.stack(slabs)
    slot_index = (my_blocks - my_domain + RAD) % domain_count
    picked = jnp.take(row_slabs, slot_index, axis=0)
    tile_cols = jnp.take(dens_cols, my_blocks, axis=0)
    matches = (tile_cols[:, None, :] == my_blocks[None, :, None]).astype(jnp.bfloat16)
    tiles = jnp.einsum("jsk,jkab->jasb", matches, picked, preferred_element_type=jnp.float32)
    order = neigh_count * block_size
    return tiles.astype(jnp.bfloat16).reshape(order, order)


def by_slot(array):
    group = lax.axis_size("aux")
    count, slots, cols = array.shape
    return array.transpose(1, 0, 2).reshape(group, slots // group, count, cols)


def exchanged(array):
    return lax.all_to_all(array, "aux", split_axis=0, concat_axis=0, tiled=True)


def body(integrals, density, dens_cols, neighbours, metric):
    ints, rows = integrals[0], metric[0]
    group = lax.axis_size("aux")
    z_len = group // X_LEN
    cols = ints.shape[2]
    line = to_all(jnp.broadcast_to(rows[None], (z_len, *rows.shape)), "z")
    line = line.reshape(z_len * rows.shape[0], rows.shape[1])
    line, ints_out = lax.optimization_barrier((line, by_slot(ints)))
    ints_moved = exchanged(ints_out)
    sides = [line] + [from_x(line, k) for k in range(1, X_LEN)]
    dense = local_density(density, dens_cols, neighbours)
    half = jnp.einsum("ls,plm->psm", dense, ints, preferred_element_type=jnp.float32)
    half_moved = exchanged(by_slot(half.astype(jnp.bfloat16)))
    starts = jnp.arange(1, X_LEN, dtype=jnp.int32) * z_len
    my_x = jnp.sum(starts <= lax.axis_index("aux"), dtype=jnp.int32)[None]
    fitted = fit(sides, my_x, ints_moved)
    shares = close(fitted, half_moved)
    shares = jnp.sum(to_all(shares, "x"), axis=0)
    shares = jnp.broadcast_to(shares[None], (z_len, cols, cols))
    return jnp.sum(to_all(shares, "z"), axis=0)[None]


def solution(mesh):
    return jax.shard_map(
        body,
        mesh=mesh,
        in_specs=(
            P("dom", "aux", None, None),
            P("dom", None, None, None),
            P(),
            P(),
            P("dom", "aux", None),
        ),
        out_specs=P("dom", None, None),
        check_vma=False,
    )
```

time: 325 us -> 271 us (0.83)
  the two profiles are of different devices: /device:TPU:32 before, /device:TPU:48 now
where the time goes in v2:
time: 271 us; the launch traced here: 270 us
  waiting for transfers between devices  155 us (57%)
  starting transfers between devices  41.8 us (15%)
  blocking collectives  29.5 us (11%)
  local copies, waits for them, and re-layouts  19 us (7%)
  Pallas kernels  18 us (7%)
  matrix products  5.11 us (2%)
    all_to_all x2, waiting for transfers between devices, exchanged(): return lax.all_to_all(array, 'aux', split_axis=0, concat_axis=0, tiled=True)  99.1 us
    ppermute x3, waiting for transfers between devices, from_x(): return lax.ppermute(block, 'aux', route)  42.9 us
    all_to_all x2, blocking collectives, to_all(): lax.all_to_all(copies, 'aux', split_axis=0, concat_axis=0, tiled=True, ax...  29.5 us
    pallas_call x1, Pallas kernels, fit(): pl.pallas_call(fit_kernel, out_shape=jax.ShapeDtypeStruct((slots, cols, r...  14 us
    all_to_all x2, starting transfers between devices, exchanged(): return lax.all_to_all(array, 'aux', split_axis=0, concat_axis=0, tiled=True)  12.3 us
    ppermute x3, starting transfers between devices, from_x(): return lax.ppermute(block, 'aux', route)  11.6 us
    all_to_all x1, waiting for transfers between devices, to_all(): lax.all_to_all(copies, 'aux', split_axis=0, concat_axis=0, tiled=True, ax...  10.7 us
    all_to_all x1, starting transfers between devices, to_all(): lax.all_to_all(copies, 'aux', split_axis=0, concat_axis=0, tiled=True, ax...  10.3 us
  transfers between devices with their start and end apart: 10, of which 7 were waited for; matrix products, arithmetic and copies ran while one was open for 7% of the time, Pallas kernels for 5%

profile of v2, /device:TPU:48, one launch (start us, length us, event | category | flops | bytes accessed | tf_op | source)
XLA Modules:
  0.0 270.4 jit_solution(11425058771093101531)
XLA Ops:
  0.0 0.0 copy-start
  0.0 1.7 broadcast_in_dim.39
  1.7 10.3 %all-to-all-start = ((bf16[8,32,1024]{2,1,0:T(8,128)(2,1)}), bf16[8,32,1024]{2,1,0:T(8,128)(2,1)S(1)}, u32[]{:S(2)}, u32[]{:S(2)}) async-start(bf16[8,32,1024]{2,1,0:T(8,128)(2,1)} %broadcast_in_dim.39), calls=%async_computation | async-start | bytes 1048576 | tf_op jit(solution)/shard_map/all_to_all | solution.py:33
  12.0 6.8 %copy.11 = bf16[512,32,128]{2,1,0:T(8,128)(2,1)} copy(bf16[512,32,128]{2,0,1:T(8,128)(2,1)} %bitcast.44) | data formatting | bytes 8388608 | tf_op jit(solution)/shard_map/transpose | solution.py:146
  18.9 10.7 %all-to-all-done = bf16[8,32,1024]{2,1,0:T(8,128)(2,1)S(1)} async-done(((bf16[8,32,1024]{2,1,0:T(8,128)(2,1)}), bf16[8,32,1024]{2,1,0:T(8,128)(2,1)S(1)}, u32[]{:S(2)}, u32[]{:S(2)}) %all-to-all-start) | async-done | bytes 524320 | tf_op jit(solution)/shard_map/all_to_all | solution.py:33
  29.5 0.0 copy-start.3
  29.5 0.0 copy-start.4
  29.5 5.0 %all-to-all-start.1 = ((bf16[32,16,32,128]{3,2,1,0:T(8,128)(2,1)}), bf16[32,16,32,128]{3,2,1,0:T(8,128)(2,1)}, u32[]{:S(2)}, u32[]{:S(2)}) async-start(bf16[32,16,32,128]{3,2,1,0:T(8,128)(2,1)} %bitcast.42), calls=%async_computation.1 | async-start | bytes 8388608 | tf_op jit(solution)/shard_map/all_to_all | solution.py:150
  34.6 0.0 copy-done.3
  34.6 2.6 collective-permute-start.3
  37.2 0.0 collective-permute-start.4
  37.2 1.7 collective-permute-start.5
  38.9 3.2 %collective-permute-start.6 = (bf16[1,4,128,128]{3,2,1,0:T(8,128)(2,1)S(1)}, bf16[1,4,128,128]{3,2,1,0:T(8,128)(2,1)S(1)}, u32[]{:S(2)}, u32[]{:S(2)}) collective-permute-start(bf16[1,4,128,128]{3,2,1,0:T(8,128)(2,1)S(1)} %copy-done.3), channel_id=1, source_target_pairs={{64,0},{96,32},{128,64},{160,96},{192,128},{224,160},{256,192},{28... | collective-permute-start | bytes 393224 | tf_op jit(solution)/shard_map/ppermute | solution.py:16
  42.2 0.0 copy-done.4
  42.2 0.1 copy.12
  42.3 0.0 copy-done
  42.3 0.2 dynamic-slice_reduce_fusion
  42.5 0.6 gather_fusion.1
  43.1 0.1 broadcast_select_fusion.1
  43.2 0.0 collective-permute-done.3
  43.2 0.1 collective-permute-done.4
  43.3 0.0 collective-permute-done.5
  43.4 2.4 collective-permute-done.6
  45.8 0.6 gather_fusion
  46.5 0.1 broadcast_select_fusion
  46.6 0.5 convolution_convert_fusion
  47.1 4.6 %fusion.2 = bf16[512,32,128]{2,0,1:T(8,128)(2,1)S(1)} fusion(bf16[1,32,512,128]{3,2,1,0:T(8,128)(2,1)} %param.5, bf16[64,8,4,128]{3,2,1,0:T(4,128)(2,1)S(1)} %bitcast.46), kind=kOutput, calls=%fused_computation.4 | convolution fusion | flops 2149580800 | bytes 8912896 | tf_op jit(solution)/shard_map/ls,plm->psm/dot_general | solution.py:164
  51.7 4.7 %copy.15 = bf16[512,32,128]{2,1,0:T(8,128)(2,1)} copy(bf16[512,32,128]{2,0,1:T(8,128)(2,1)S(1)} %fusion.2) | data formatting | bytes 8388608 | tf_op jit(solution)/shard_map/convert_element_type | solution.py:165
  56.4 73.2 %all-to-all-done.1.refs_4_ = bf16[32,16,32,128]{3,2,1,0:T(8,128)(2,1)} async-done(((bf16[32,16,32,128]{3,2,1,0:T(8,128)(2,1)}), bf16[32,16,32,128]{3,2,1,0:T(8,128)(2,1)}, u32[]{:S(2)}, u32[]{:S(2)}) %all-to-all-start.1) | async-done | bytes 4194336 | tf_op jit(solution)/shard_map/all_to_all | solution.py:150
  129.6 7.3 %all-to-all-start.2 = ((bf16[32,16,32,128]{3,2,1,0:T(8,128)(2,1)}), bf16[32,16,32,128]{3,2,1,0:T(8,128)(2,1)}, u32[]{:S(2)}, u32[]{:S(2)}) async-start(bf16[32,16,32,128]{3,2,1,0:T(8,128)(2,1)} %bitcast.43), calls=%async_computation.2 | async-start | bytes 8388608 | tf_op jit(solution)/shard_map/all_to_all | solution.py:150
  136.9 3.6 %collective-permute-start = (bf16[256,1024]{1,0:T(8,128)(2,1)S(1)}, bf16[256,1024]{1,0:T(8,128)(2,1)S(1)}, u32[]{:S(2)}, u32[]{:S(2)}) collective-permute-start(bf16[256,1024]{1,0:T(8,128)(2,1)S(1)} %bitcast.38), channel_id=1, source_target_pairs={{24,0},{25,1},{26,2},{27,3},{28,4},{29,5},{30,6},{31,7},{0,8},{1,9... | collective-permute-start | bytes 1572872 | tf_op jit(solution)/shard_map/ppermute | solution.py:23
  140.5 4.6 %collective-permute-start.1 = (bf16[256,1024]{1,0:T(8,128)(2,1)S(1)}, bf16[256,1024]{1,0:T(8,128)(2,1)S(1)}, u32[]{:S(2)}, u32[]{:S(2)}) collective-permute-start(bf16[256,1024]{1,0:T(8,128)(2,1)S(1)} %bitcast.39), channel_id=1, source_target_pairs={{16,0},{17,1},{18,2},{19,3},{20,4},{21,5},{22,6},{23,7},{24,8},{25... | collective-permute-start | bytes 1572872 | tf_op jit(solution)/shard_map/ppermute | solution.py:23
  145.2 3.3 %collective-permute-start.2 = (bf16[256,1024]{1,0:T(8,128)(2,1)S(1)}, bf16[256,1024]{1,0:T(8,128)(2,1)S(1)}, u32[]{:S(2)}, u32[]{:S(2)}) collective-permute-start(bf16[256,1024]{1,0:T(8,128)(2,1)S(1)} %bitcast.40), channel_id=1, source_target_pairs={{8,0},{9,1},{10,2},{11,3},{12,4},{13,5},{14,6},{15,7},{16,8},{17,9... | collective-permute-start | bytes 1572872 | tf_op jit(solution)/shard_map/ppermute | solution.py:23
  148.5 0.6 fusion.11
  149.1 21.3 %collective-permute-done.refs_1_ = bf16[256,1024]{1,0:T(8,128)(2,1)S(1)} collective-permute-done((bf16[256,1024]{1,0:T(8,128)(2,1)S(1)}, bf16[256,1024]{1,0:T(8,128)(2,1)S(1)}, u32[]{:S(2)}, u32[]{:S(2)}) %collective-permute-start) | collective-permute-done | bytes 524320 | tf_op jit(solution)/shard_map/ppermute | solution.py:23
  170.4 21.7 %collective-permute-done.1.refs_2_ = bf16[256,1024]{1,0:T(8,128)(2,1)S(1)} collective-permute-done((bf16[256,1024]{1,0:T(8,128)(2,1)S(1)}, bf16[256,1024]{1,0:T(8,128)(2,1)S(1)}, u32[]{:S(2)}, u32[]{:S(2)}) %collective-permute-start.1) | collective-permute-done | bytes 524320 | tf_op jit(solution)/shard_map/ppermute | solution.py:23
  192.1 0.0 collective-permute-done.2.refs_3_
  192.1 14.0 %shard_map.55.fitted_ref = bf16[16,128,1024]{2,1,0:T(8,128)(2,1)S(1)} custom-call(s32[1]{0:T(128)} %bitcast.x_ref, bf16[256,1024]{1,0:T(8,128)(2,1)S(1)} %bitcast.41, bf16[256,1024]{1,0:T(8,128)(2,1)S(1)} %collective-permute-done.refs_1_, bf16[256,1024]{1,0:T(8,128)(2,1)S(1)} %collective-permute-done.1.refs_2_, ...), custom_call_target="tpu_custom_call" | custom-call | flops 4294967296 | bytes 10485760 | tf_op jit(solution)/shard_map/pallas_call | solution.py:60
  206.1 0.0 copy-start.1
  206.1 1.9 copy-done.1
  208.0 25.9 %all-to-all-done.2.half_ref = bf16[32,16,32,128]{3,2,1,0:T(8,128)(2,1)} async-done(((bf16[32,16,32,128]{3,2,1,0:T(8,128)(2,1)}), bf16[32,16,32,128]{3,2,1,0:T(8,128)(2,1)}, u32[]{:S(2)}, u32[]{:S(2)}) %all-to-all-start.2) | async-done | bytes 4194336 | tf_op jit(solution)/shard_map/all_to_all | solution.py:150
  233.9 0.0 copy-start.2
  233.9 2.2 copy-done.2
  236.1 4.0 %shard_map.56 = f32[4,128,128]{2,1,0:T(8,128)S(1)} custom-call(bf16[16,128,1024]{2,1,0:T(8,128)(2,1)S(1)} %copy-done.2, bf16[32,16,32,128]{3,2,1,0:T(8,128)(2,1)} %all-to-all-done.2.half_ref), custom_call_target="tpu_custom_call" | custom-call | flops 536870912 | bytes 8388608 | tf_op jit(solution)/shard_map/pallas_call | solution.py:105
  240.1 9.1 %all_to_all.25 = f32[4,128,128]{2,1,0:T(8,128)S(1)} all-to-all(f32[4,128,128]{2,1,0:T(8,128)S(1)} %shard_map.56), channel_id=1, replica_groups={{0,8,16,24},{1,9,17,25},{2,10,18,26},{3,11,19,27},{4,12,20,28},{5,13,21..., dimensions={0} | all-to-all | bytes 524288 | tf_op jit(solution)/shard_map/all_to_all | solution.py:33
  249.2 20.5 %all_to_all.26 = f32[8,128,128]{2,1,0:T(8,128)S(1)} all-to-all(f32[8,128,128]{2,1,0:T(8,128)S(1)} %broadcast_in_dim.43), channel_id=1, replica_groups={{0,1,2,3,4,5,6,7},{8,9,10,11,12,13,14,15},{16,17,18,19,20,21,22,23},{24..., dimensions={0} | all-to-all | bytes 1048576 | tf_op jit(solution)/shard_map/all_to_all | solution.py:33
  269.7 0.7 reduce_sum.29
  (11 shorter events, 0.2 us)
Async XLA Ops:
  0.0 42.3 %copy-start = (s32[16,4]{0,1:T(4,128)S(1)}, s32[16,4]{0,1:T(4,128)}, u32[]{:S(2)}) copy-start(s32[16,4]{0,1:T(4,128)} %param.8) | copy-start | bytes 772
  1.7 27.8 %all-to-all-start = ((bf16[8,32,1024]{2,1,0:T(8,128)(2,1)}), bf16[8,32,1024]{2,1,0:T(8,128)(2,1)S(1)}, u32[]{:S(2)}, u32[]{:S(2)}) async-start(bf16[8,32,1024]{2,1,0:T(8,128)(2,1)} %broadcast_in_dim.39), calls=%async_computation | async-start | bytes 1048576 | tf_op jit(solution)/shard_map/all_to_all | solution.py:33
  29.5 5.0 %copy-start.3 = (bf16[1,4,128,128]{3,2,1,0:T(8,128)(2,1)S(1)}, bf16[1,4,128,128]{3,2,1,0:T(8,128)(2,1)}, u32[]{:S(2)}) copy-start(bf16[1,4,128,128]{3,2,1,0:T(8,128)(2,1)} %param.6) | copy-start | bytes 393220
  29.5 12.6 %copy-start.4 = (s32[16,4]{0,1:T(4,128)S(1)}, s32[16,4]{0,1:T(4,128)}, u32[]{:S(2)}) copy-start(s32[16,4]{0,1:T(4,128)} %param.7) | copy-start | bytes 772
  29.5 100.1 %all-to-all-start.1 = ((bf16[32,16,32,128]{3,2,1,0:T(8,128)(2,1)}), bf16[32,16,32,128]{3,2,1,0:T(8,128)(2,1)}, u32[]{:S(2)}, u32[]{:S(2)}) async-start(bf16[32,16,32,128]{3,2,1,0:T(8,128)(2,1)} %bitcast.42), calls=%async_computation.1 | async-start | bytes 8388608 | tf_op jit(solution)/shard_map/all_to_all | solution.py:150
  34.6 8.6 %collective-permute-start.3 = (bf16[1,4,128,128]{3,2,1,0:T(8,128)(2,1)S(1)}, bf16[1,4,128,128]{3,2,1,0:T(8,128)(2,1)S(1)}, u32[]{:S(2)}, u32[]{:S(2)}) collective-permute-start(bf16[1,4,128,128]{3,2,1,0:T(8,128)(2,1)S(1)} %copy-done.3), channel_id=1, source_target_pairs={{448,0},{480,32},{0,64},{32,96},{64,128},{96,160},{128,192},{160,2... | collective-permute-start | bytes 393224 | tf_op jit(solution)/shard_map/ppermute | solution.py:16
  37.2 6.1 %collective-permute-start.4 = (bf16[1,4,128,128]{3,2,1,0:T(8,128)(2,1)S(1)}, bf16[1,4,128,128]{3,2,1,0:T(8,128)(2,1)S(1)}, u32[]{:S(2)}, u32[]{:S(2)}) collective-permute-start(bf16[1,4,128,128]{3,2,1,0:T(8,128)(2,1)S(1)} %copy-done.3), channel_id=1, source_target_pairs={{480,0},{0,32},{32,64},{64,96},{96,128},{128,160},{160,192},{192,2... | collective-permute-start | bytes 393224 | tf_op jit(solution)/shard_map/ppermute | solution.py:16
  37.2 6.1 %collective-permute-start.5 = (bf16[1,4,128,128]{3,2,1,0:T(8,128)(2,1)S(1)}, bf16[1,4,128,128]{3,2,1,0:T(8,128)(2,1)S(1)}, u32[]{:S(2)}, u32[]{:S(2)}) collective-permute-start(bf16[1,4,128,128]{3,2,1,0:T(8,128)(2,1)S(1)} %copy-done.3), channel_id=1, source_target_pairs={{32,0},{64,32},{96,64},{128,96},{160,128},{192,160},{224,192},{256... | collective-permute-start | bytes 393224 | tf_op jit(solution)/shard_map/ppermute | solution.py:16
  38.9 6.8 %collective-permute-start.6 = (bf16[1,4,128,128]{3,2,1,0:T(8,128)(2,1)S(1)}, bf16[1,4,128,128]{3,2,1,0:T(8,128)(2,1)S(1)}, u32[]{:S(2)}, u32[]{:S(2)}) collective-permute-start(bf16[1,4,128,128]{3,2,1,0:T(8,128)(2,1)S(1)} %copy-done.3), channel_id=1, source_target_pairs={{64,0},{96,32},{128,64},{160,96},{192,128},{224,160},{256,192},{28... | collective-permute-start | bytes 393224 | tf_op jit(solution)/shard_map/ppermute | solution.py:16
  129.6 104.3 %all-to-all-start.2 = ((bf16[32,16,32,128]{3,2,1,0:T(8,128)(2,1)}), bf16[32,16,32,128]{3,2,1,0:T(8,128)(2,1)}, u32[]{:S(2)}, u32[]{:S(2)}) async-start(bf16[32,16,32,128]{3,2,1,0:T(8,128)(2,1)} %bitcast.43), calls=%async_computation.2 | async-start | bytes 8388608 | tf_op jit(solution)/shard_map/all_to_all | solution.py:150
  136.9 33.5 %collective-permute-start = (bf16[256,1024]{1,0:T(8,128)(2,1)S(1)}, bf16[256,1024]{1,0:T(8,128)(2,1)S(1)}, u32[]{:S(2)}, u32[]{:S(2)}) collective-permute-start(bf16[256,1024]{1,0:T(8,128)(2,1)S(1)} %bitcast.38), channel_id=1, source_target_pairs={{24,0},{25,1},{26,2},{27,3},{28,4},{29,5},{30,6},{31,7},{0,8},{1,9... | collective-permute-start | bytes 1572872 | tf_op jit(solution)/shard_map/ppermute | solution.py:23
  140.5 51.5 %collective-permute-start.1 = (bf16[256,1024]{1,0:T(8,128)(2,1)S(1)}, bf16[256,1024]{1,0:T(8,128)(2,1)S(1)}, u32[]{:S(2)}, u32[]{:S(2)}) collective-permute-start(bf16[256,1024]{1,0:T(8,128)(2,1)S(1)} %bitcast.39), channel_id=1, source_target_pairs={{16,0},{17,1},{18,2},{19,3},{20,4},{21,5},{22,6},{23,7},{24,8},{25... | collective-permute-start | bytes 1572872 | tf_op jit(solution)/shard_map/ppermute | solution.py:23
  145.2 46.9 %collective-permute-start.2 = (bf16[256,1024]{1,0:T(8,128)(2,1)S(1)}, bf16[256,1024]{1,0:T(8,128)(2,1)S(1)}, u32[]{:S(2)}, u32[]{:S(2)}) collective-permute-start(bf16[256,1024]{1,0:T(8,128)(2,1)S(1)} %bitcast.40), channel_id=1, source_target_pairs={{8,0},{9,1},{10,2},{11,3},{12,4},{13,5},{14,6},{15,7},{16,8},{17,9... | collective-permute-start | bytes 1572872 | tf_op jit(solution)/shard_map/ppermute | solution.py:23
  206.1 2.0 copy-start.1
  233.9 2.2 copy-start.2

commit v3 on v2

--- a/solution.py
+++ b/solution.py
@@ -36,34 +36,58 @@
     )
 
 
+BLOCKS = {
+    (0, 0): (0, 0), (0, 1): (0, 1), (0, 2): (0, 2),
+    (1, 1): (1, 0), (1, 2): (1, 1), (1, 3): (1, 2),
+    (2, 2): (2, 0), (2, 3): (2, 1),
+    (3, 3): (3, 0), (3, 0): (3, 1),
+}
+
+
 def fit_kernel(x_ref, *refs):
     *metric_refs, ints_ref, out_ref = refs
     parts, width, depth, cols = ints_ref.shape
     count = len(metric_refs)
-    for w in range(width):
-        right = ints_ref[:, w].reshape(parts * depth, cols)
-        for k, metric_ref in enumerate(metric_refs):
-            rows = metric_ref.shape[0]
-            place = lax.rem(x_ref[0] + (count - k), count)
-            start = pl.multiple_of(place * rows, rows)
-            out_ref[w, :, pl.ds(start, rows)] = lax.dot_general(
-                right, metric_ref[...], (((0,), (1,)), ((), ())),
+    share = parts // count
+    block = share * depth
+    columns = []
+    for k in range(count):
+        place = lax.rem(x_ref[0] + k, count)
+        tile = ints_ref[pl.ds(pl.multiple_of(place * share, share), share)]
+        columns.append(jnp.concatenate(
+            [tile[:, w].reshape(block, cols).T for w in range(width)], axis=0
+        ))
+    for q in range(count):
+        total = jnp.zeros((width * cols, block), jnp.float32)
+        for p in range(count):
+            stored = (q, p) in BLOCKS
+            piece, place = BLOCKS[(q, p) if stored else (p, q)]
+            right = metric_refs[piece][:, place * block:(place + 1) * block]
+            total += lax.dot_general(
+                columns[p], right, (((1,), (1 if stored else 0,)), ((), ())),
                 preferred_element_type=jnp.float32,
-            ).astype(out_ref.dtype)
+            )
+        total = total.astype(out_ref.dtype)
+        place = lax.rem(x_ref[0] + q, count)
+        for w in range(width):
+            out_ref[w, :, pl.ds(pl.multiple_of(place * block, block), block)] = (
+                total[w * cols:(w + 1) * cols]
+            )
 
 
 def fit(metric_parts, my_x, ints):
     parts, slots, depth, cols = ints.shape
     width = 2
     rows = parts * depth
-    metric_spec = pl.BlockSpec(metric_parts[0].shape, lambda i, x: (0, 0))
     return pl.pallas_call(
         fit_kernel,
         out_shape=jax.ShapeDtypeStruct((slots, cols, rows), ints.dtype),
         grid_spec=pltpu.PrefetchScalarGridSpec(
             num_scalar_prefetch=1,
             grid=(slots // width,),
-            in_specs=[metric_spec] * len(metric_parts) + [
+            in_specs=[
+                pl.BlockSpec(part.shape, lambda i, x: (0, 0)) for part in metric_parts
+            ] + [
                 pl.BlockSpec((parts, width, depth, cols), lambda i, x: (0, i, 0, 0)),
             ],
             out_specs=pl.BlockSpec((width, cols, rows), lambda i, x: (i, 0, 0)),
@@ -155,17 +179,21 @@
     group = lax.axis_size("aux")
     z_len = group // X_LEN
     cols = ints.shape[2]
-    line = to_all(jnp.broadcast_to(rows[None], (z_len, *rows.shape)), "z")
-    line = line.reshape(z_len * rows.shape[0], rows.shape[1])
+    starts = jnp.arange(1, X_LEN, dtype=jnp.int32) * z_len
+    my_x = jnp.sum(starts <= lax.axis_index("aux"), dtype=jnp.int32)
+    side = rows.shape[1] // X_LEN
+    around = jnp.concatenate([rows, rows[:, :2 * side]], axis=1)
+    kept = lax.dynamic_slice_in_dim(around, my_x * side, 3 * side, 1)
+    line = to_all(jnp.broadcast_to(kept[None], (z_len, *kept.shape)), "z")
+    line = line.reshape(z_len * kept.shape[0], kept.shape[1])
     line, ints_out = lax.optimization_barrier((line, by_slot(ints)))
     ints_moved = exchanged(ints_out)
-    sides = [line] + [from_x(line, k) for k in range(1, X_LEN)]
+    short = line[:, :2 * side]
+    parts = [line, from_x(line, -1), from_x(short, 2), from_x(short, 1)]
     dense = local_density(density, dens_cols, neighbours)
     half = jnp.einsum("ls,plm->psm", dense, ints, preferred_element_type=jnp.float32)
     half_moved = exchanged(by_slot(half.astype(jnp.bfloat16)))
-    starts = jnp.arange(1, X_LEN, dtype=jnp.int32) * z_len
-    my_x = jnp.sum(starts <= lax.axis_index("aux"), dtype=jnp.int32)[None]
-    fitted = fit(sides, my_x, ints_moved)
+    fitted = fit(parts, my_x[None], ints_moved)
     shares = close(fitted, half_moved)
     shares = jnp.sum(to_all(shares, "x"), axis=0)
     shares = jnp.broadcast_to(shares[None], (z_len, cols, cols))

time: 271 us -> 269 us (level)
  the two profiles are of different devices: /device:TPU:48 before, /device:TPU:40 now
where the time goes in v3:
time: 269 us; the launch traced here: 268 us
  waiting for transfers between devices  159 us (59%)
  starting transfers between devices  39.8 us (15%)
  blocking collectives  29.1 us (11%)
  local copies, waits for them, and re-layouts  18.8 us (7%)
  Pallas kernels  12.9 us (5%)
  matrix products  5.11 us (2%)
    all_to_all x2, waiting for transfers between devices, exchanged(): return lax.all_to_all(array, 'aux', split_axis=0, concat_axis=0, tiled=True)  129 us
    all_to_all x2, blocking collectives, to_all(): lax.all_to_all(copies, 'aux', split_axis=0, concat_axis=0, tiled=True, ax...  29.1 us
    ppermute x3, waiting for transfers between devices, from_x(): return lax.ppermute(block, 'aux', route)  21.5 us
    ppermute x3, starting transfers between devices, from_x(): return lax.ppermute(block, 'aux', route)  10.4 us
    all_to_all x2, starting transfers between devices, exchanged(): return lax.all_to_all(array, 'aux', split_axis=0, concat_axis=0, tiled=True)  10.3 us
    all_to_all x1, starting transfers between devices, to_all(): lax.all_to_all(copies, 'aux', split_axis=0, concat_axis=0, tiled=True, ax...  10.3 us
    pallas_call x1, Pallas kernels, fit(): pl.pallas_call(fit_kernel, out_shape=jax.ShapeDtypeStruct((slots, cols, r...  8.89 us
    ppermute x4, starting transfers between devices, passed_along(): return lax.ppermute(block, axis, route)  8.79 us
  transfers between devices with their start and end apart: 10, of which 6 were waited for; matrix products, arithmetic and copies ran while one was open for 7% of the time, Pallas kernels for 3%

profile of v3, /device:TPU:40, one launch (start us, length us, event | category | flops | bytes accessed | tf_op | source)
XLA Modules:
  0.0 268.5 jit_solution(9539486225159653791)
XLA Ops:
  0.0 0.0 copy-start
  0.0 0.6 fusion.12
  1.3 0.8 slice.12
  2.1 0.8 fusion.7
  2.9 0.8 broadcast_in_dim.37
  3.7 10.3 %all-to-all-start = ((bf16[8,32,768]{2,1,0:T(8,128)(2,1)}), bf16[8,32,768]{2,1,0:T(8,128)(2,1)S(1)}, u32[]{:S(2)}, u32[]{:S(2)}) async-start(bf16[8,32,768]{2,1,0:T(8,128)(2,1)} %broadcast_in_dim.37), calls=%async_computation | async-start | bytes 786432 | tf_op jit(solution)/shard_map/all_to_all | solution.py:33
  14.0 6.8 %copy.11 = bf16[512,32,128]{2,1,0:T(8,128)(2,1)} copy(bf16[512,32,128]{2,0,1:T(8,128)(2,1)} %bitcast.43) | data formatting | bytes 8388608 | tf_op jit(solution)/shard_map/transpose | solution.py:170
  20.8 7.9 %all-to-all-done = bf16[8,32,768]{2,1,0:T(8,128)(2,1)S(1)} async-done(((bf16[8,32,768]{2,1,0:T(8,128)(2,1)}), bf16[8,32,768]{2,1,0:T(8,128)(2,1)S(1)}, u32[]{:S(2)}, u32[]{:S(2)}) %all-to-all-start) | async-done | bytes 393248 | tf_op jit(solution)/shard_map/all_to_all | solution.py:33
  28.7 0.0 copy-start.3
  28.7 0.0 copy-start.4
  28.7 5.0 %all-to-all-start.1 = ((bf16[32,16,32,128]{3,2,1,0:T(8,128)(2,1)}), bf16[32,16,32,128]{3,2,1,0:T(8,128)(2,1)}, u32[]{:S(2)}, u32[]{:S(2)}) async-start(bf16[32,16,32,128]{3,2,1,0:T(8,128)(2,1)} %bitcast.41), calls=%async_computation.1 | async-start | bytes 8388608 | tf_op jit(solution)/shard_map/all_to_all | solution.py:174
  33.7 0.0 copy-done.3
  33.7 2.6 collective-permute-start.3
  36.3 0.0 collective-permute-start.4
  36.3 1.7 collective-permute-start.5
  38.1 4.5 %collective-permute-start.6 = (bf16[1,4,128,128]{3,2,1,0:T(8,128)(2,1)S(1)}, bf16[1,4,128,128]{3,2,1,0:T(8,128)(2,1)S(1)}, u32[]{:S(2)}, u32[]{:S(2)}) collective-permute-start(bf16[1,4,128,128]{3,2,1,0:T(8,128)(2,1)S(1)} %copy-done.3), channel_id=1, source_target_pairs={{64,0},{96,32},{128,64},{160,96},{192,128},{224,160},{256,192},{28... | collective-permute-start | bytes 393224 | tf_op jit(solution)/shard_map/ppermute | solution.py:16
  42.5 0.0 copy-done.4
  42.5 0.1 copy.12
  42.6 0.0 copy-done
  42.6 0.2 dynamic-slice_reduce_fusion
  42.8 0.6 gather_fusion.1
  43.4 0.1 broadcast_select_fusion.1
  43.5 0.0 collective-permute-done.3
  43.5 0.0 collective-permute-done.4
  43.6 0.0 collective-permute-done.5
  43.6 1.4 collective-permute-done.6
  45.0 0.6 gather_fusion
  45.7 0.1 broadcast_select_fusion
  45.8 0.5 convolution_convert_fusion
  46.4 4.6 %fusion.2 = bf16[512,32,128]{2,0,1:T(8,128)(2,1)S(1)} fusion(bf16[1,32,512,128]{3,2,1,0:T(8,128)(2,1)} %param.5, bf16[64,8,4,128]{3,2,1,0:T(4,128)(2,1)S(1)} %bitcast.46), kind=kOutput, calls=%fused_computation.4 | convolution fusion | flops 2149580800 | bytes 8912896 | tf_op jit(solution)/shard_map/ls,plm->psm/dot_general | solution.py:194
  50.9 4.7 %copy.15 = bf16[512,32,128]{2,1,0:T(8,128)(2,1)} copy(bf16[512,32,128]{2,0,1:T(8,128)(2,1)S(1)} %fusion.2) | data formatting | bytes 8388608 | tf_op jit(solution)/shard_map/convert_element_type | solution.py:195
  55.6 74.7 %all-to-all-done.1.refs_4_ = bf16[32,16,32,128]{3,2,1,0:T(8,128)(2,1)} async-done(((bf16[32,16,32,128]{3,2,1,0:T(8,128)(2,1)}), bf16[32,16,32,128]{3,2,1,0:T(8,128)(2,1)}, u32[]{:S(2)}, u32[]{:S(2)}) %all-to-all-start.1) | async-done | bytes 4194336 | tf_op jit(solution)/shard_map/all_to_all | solution.py:174
  130.3 5.3 %all-to-all-start.2 = ((bf16[32,16,32,128]{3,2,1,0:T(8,128)(2,1)}), bf16[32,16,32,128]{3,2,1,0:T(8,128)(2,1)}, u32[]{:S(2)}, u32[]{:S(2)}) async-start(bf16[32,16,32,128]{3,2,1,0:T(8,128)(2,1)} %bitcast.42), calls=%async_computation.2 | async-start | bytes 8388608 | tf_op jit(solution)/shard_map/all_to_all | solution.py:174
  135.6 4.9 %collective-permute-start = (bf16[256,768]{1,0:T(8,128)(2,1)S(1)}, bf16[256,768]{1,0:T(8,128)(2,1)S(1)}, u32[]{:S(2)}, u32[]{:S(2)}) collective-permute-start(bf16[256,768]{1,0:T(8,128)(2,1)S(1)} %bitcast.38), channel_id=1, source_target_pairs={{8,0},{9,1},{10,2},{11,3},{12,4},{13,5},{14,6},{15,7},{16,8},{17,9... | collective-permute-start | bytes 1179656 | tf_op jit(solution)/shard_map/ppermute | solution.py:23
  140.5 2.7 %collective-permute-start.1 = (bf16[256,512]{1,0:T(8,128)(2,1)S(1)}, bf16[256,512]{1,0:T(8,128)(2,1)S(1)}, u32[]{:S(2)}, u32[]{:S(2)}) collective-permute-start(bf16[256,512]{1,0:T(8,128)(2,1)S(1)} %slice.7), channel_id=1, source_target_pairs={{16,0},{17,1},{18,2},{19,3},{20,4},{21,5},{22,6},{23,7},{24,8},{25... | collective-permute-start | bytes 786440 | tf_op jit(solution)/shard_map/ppermute | solution.py:23
  143.3 2.8 %collective-permute-start.2 = (bf16[256,512]{1,0:T(8,128)(2,1)S(1)}, bf16[256,512]{1,0:T(8,128)(2,1)S(1)}, u32[]{:S(2)}, u32[]{:S(2)}) collective-permute-start(bf16[256,512]{1,0:T(8,128)(2,1)S(1)} %slice.7), channel_id=1, source_target_pairs={{24,0},{25,1},{26,2},{27,3},{28,4},{29,5},{30,6},{31,7},{0,8},{1,9... | collective-permute-start | bytes 786440 | tf_op jit(solution)/shard_map/ppermute | solution.py:23
  146.1 14.9 %collective-permute-done.1.refs_2_ = bf16[256,512]{1,0:T(8,128)(2,1)S(1)} collective-permute-done((bf16[256,512]{1,0:T(8,128)(2,1)S(1)}, bf16[256,512]{1,0:T(8,128)(2,1)S(1)}, u32[]{:S(2)}, u32[]{:S(2)}) %collective-permute-start.1) | collective-permute-done | bytes 262176 | tf_op jit(solution)/shard_map/ppermute | solution.py:23
  161.0 6.6 %collective-permute-done.2.refs_3_ = bf16[256,512]{1,0:T(8,128)(2,1)S(1)} collective-permute-done((bf16[256,512]{1,0:T(8,128)(2,1)S(1)}, bf16[256,512]{1,0:T(8,128)(2,1)S(1)}, u32[]{:S(2)}, u32[]{:S(2)}) %collective-permute-start.2) | collective-permute-done | bytes 262176 | tf_op jit(solution)/shard_map/ppermute | solution.py:23
  167.6 0.0 collective-permute-done.refs_1_
  167.6 8.9 %shard_map.55.fitted_ref = bf16[16,128,1024]{2,1,0:T(8,128)(2,1)S(1)} custom-call(s32[1]{0:T(128)} %bitcast.x_ref, bf16[256,768]{1,0:T(8,128)(2,1)S(1)} %bitcast.40, bf16[256,768]{1,0:T(8,128)(2,1)S(1)} %collective-permute-done.refs_1_, bf16[256,512]{1,0:T(8,128)(2,1)S(1)} %collective-permute-done.1.refs_2_, ...), custom_call_target="tpu_custom_call" | custom-call | flops 4294967296 | bytes 10485760 | tf_op jit(solution)/shard_map/pallas_call | solution.py:82
  176.5 0.0 copy-start.1
  176.5 1.9 copy-done.1
  178.4 54.0 %all-to-all-done.2.half_ref = bf16[32,16,32,128]{3,2,1,0:T(8,128)(2,1)} async-done(((bf16[32,16,32,128]{3,2,1,0:T(8,128)(2,1)}), bf16[32,16,32,128]{3,2,1,0:T(8,128)(2,1)}, u32[]{:S(2)}, u32[]{:S(2)}) %all-to-all-start.2) | async-done | bytes 4194336 | tf_op jit(solution)/shard_map/all_to_all | solution.py:174
  232.4 2.2 copy-done.2
  234.6 4.0 %shard_map.56 = f32[4,128,128]{2,1,0:T(8,128)S(1)} custom-call(bf16[16,128,1024]{2,1,0:T(8,128)(2,1)S(1)} %copy-done.2, bf16[32,16,32,128]{3,2,1,0:T(8,128)(2,1)} %all-to-all-done.2.half_ref), custom_call_target="tpu_custom_call" | custom-call | flops 536870912 | bytes 8388608 | tf_op jit(solution)/shard_map/pallas_call | solution.py:129
  238.6 9.1 %all_to_all.25 = f32[4,128,128]{2,1,0:T(8,128)S(1)} all-to-all(f32[4,128,128]{2,1,0:T(8,128)S(1)} %shard_map.56), channel_id=1, replica_groups={{0,8,16,24},{1,9,17,25},{2,10,18,26},{3,11,19,27},{4,12,20,28},{5,13,21..., dimensions={0} | all-to-all | bytes 524288 | tf_op jit(solution)/shard_map/all_to_all | solution.py:33
  247.8 20.1 %all_to_all.26 = f32[8,128,128]{2,1,0:T(8,128)S(1)} all-to-all(f32[8,128,128]{2,1,0:T(8,128)S(1)} %broadcast_in_dim.41), channel_id=1, replica_groups={{0,1,2,3,4,5,6,7},{8,9,10,11,12,13,14,15},{16,17,18,19,20,21,22,23},{24..., dimensions={0} | all-to-all | bytes 1048576 | tf_op jit(solution)/shard_map/all_to_all | solution.py:33
  267.8 0.7 reduce_sum.29
  (13 shorter events, 0.2 us)
Async XLA Ops:
  0.0 42.6 %copy-start = (s32[16,4]{0,1:T(4,128)S(1)}, s32[16,4]{0,1:T(4,128)}, u32[]{:S(2)}) copy-start(s32[16,4]{0,1:T(4,128)} %param.8) | copy-start | bytes 772
  3.7 25.0 %all-to-all-start = ((bf16[8,32,768]{2,1,0:T(8,128)(2,1)}), bf16[8,32,768]{2,1,0:T(8,128)(2,1)S(1)}, u32[]{:S(2)}, u32[]{:S(2)}) async-start(bf16[8,32,768]{2,1,0:T(8,128)(2,1)} %broadcast_in_dim.37), calls=%async_computation | async-start | bytes 786432 | tf_op jit(solution)/shard_map/all_to_all | solution.py:33
  28.7 5.0 %copy-start.3 = (bf16[1,4,128,128]{3,2,1,0:T(8,128)(2,1)S(1)}, bf16[1,4,128,128]{3,2,1,0:T(8,128)(2,1)}, u32[]{:S(2)}) copy-start(bf16[1,4,128,128]{3,2,1,0:T(8,128)(2,1)} %param.6) | copy-start | bytes 393220
  28.7 13.9 %copy-start.4 = (s32[16,4]{0,1:T(4,128)S(1)}, s32[16,4]{0,1:T(4,128)}, u32[]{:S(2)}) copy-start(s32[16,4]{0,1:T(4,128)} %param.7) | copy-start | bytes 772
  28.7 101.6 %all-to-all-start.1 = ((bf16[32,16,32,128]{3,2,1,0:T(8,128)(2,1)}), bf16[32,16,32,128]{3,2,1,0:T(8,128)(2,1)}, u32[]{:S(2)}, u32[]{:S(2)}) async-start(bf16[32,16,32,128]{3,2,1,0:T(8,128)(2,1)} %bitcast.41), calls=%async_computation.1 | async-start | bytes 8388608 | tf_op jit(solution)/shard_map/all_to_all | solution.py:174
  33.7 9.8 %collective-permute-start.3 = (bf16[1,4,128,128]{3,2,1,0:T(8,128)(2,1)S(1)}, bf16[1,4,128,128]{3,2,1,0:T(8,128)(2,1)S(1)}, u32[]{:S(2)}, u32[]{:S(2)}) collective-permute-start(bf16[1,4,128,128]{3,2,1,0:T(8,128)(2,1)S(1)} %copy-done.3), channel_id=1, source_target_pairs={{448,0},{480,32},{0,64},{32,96},{64,128},{96,160},{128,192},{160,2... | collective-permute-start | bytes 393224 | tf_op jit(solution)/shard_map/ppermute | solution.py:16
  36.3 7.2 %collective-permute-start.4 = (bf16[1,4,128,128]{3,2,1,0:T(8,128)(2,1)S(1)}, bf16[1,4,128,128]{3,2,1,0:T(8,128)(2,1)S(1)}, u32[]{:S(2)}, u32[]{:S(2)}) collective-permute-start(bf16[1,4,128,128]{3,2,1,0:T(8,128)(2,1)S(1)} %copy-done.3), channel_id=1, source_target_pairs={{480,0},{0,32},{32,64},{64,96},{96,128},{128,160},{160,192},{192,2... | collective-permute-start | bytes 393224 | tf_op jit(solution)/shard_map/ppermute | solution.py:16
  36.3 7.3 %collective-permute-start.5 = (bf16[1,4,128,128]{3,2,1,0:T(8,128)(2,1)S(1)}, bf16[1,4,128,128]{3,2,1,0:T(8,128)(2,1)S(1)}, u32[]{:S(2)}, u32[]{:S(2)}) collective-permute-start(bf16[1,4,128,128]{3,2,1,0:T(8,128)(2,1)S(1)} %copy-done.3), channel_id=1, source_target_pairs={{32,0},{64,32},{96,64},{128,96},{160,128},{192,160},{224,192},{256... | collective-permute-start | bytes 393224 | tf_op jit(solution)/shard_map/ppermute | solution.py:16
  38.1 7.0 %collective-permute-start.6 = (bf16[1,4,128,128]{3,2,1,0:T(8,128)(2,1)S(1)}, bf16[1,4,128,128]{3,2,1,0:T(8,128)(2,1)S(1)}, u32[]{:S(2)}, u32[]{:S(2)}) collective-permute-start(bf16[1,4,128,128]{3,2,1,0:T(8,128)(2,1)S(1)} %copy-done.3), channel_id=1, source_target_pairs={{64,0},{96,32},{128,64},{160,96},{192,128},{224,160},{256,192},{28... | collective-permute-start | bytes 393224 | tf_op jit(solution)/shard_map/ppermute | solution.py:16
  130.3 102.1 %all-to-all-start.2 = ((bf16[32,16,32,128]{3,2,1,0:T(8,128)(2,1)}), bf16[32,16,32,128]{3,2,1,0:T(8,128)(2,1)}, u32[]{:S(2)}, u32[]{:S(2)}) async-start(bf16[32,16,32,128]{3,2,1,0:T(8,128)(2,1)} %bitcast.42), calls=%async_computation.2 | async-start | bytes 8388608 | tf_op jit(solution)/shard_map/all_to_all | solution.py:174
  135.6 31.9 %collective-permute-start = (bf16[256,768]{1,0:T(8,128)(2,1)S(1)}, bf16[256,768]{1,0:T(8,128)(2,1)S(1)}, u32[]{:S(2)}, u32[]{:S(2)}) collective-permute-start(bf16[256,768]{1,0:T(8,128)(2,1)S(1)} %bitcast.38), channel_id=1, source_target_pairs={{8,0},{9,1},{10,2},{11,3},{12,4},{13,5},{14,6},{15,7},{16,8},{17,9... | collective-permute-start | bytes 1179656 | tf_op jit(solution)/shard_map/ppermute | solution.py:23
  140.5 20.4 %collective-permute-start.1 = (bf16[256,512]{1,0:T(8,128)(2,1)S(1)}, bf16[256,512]{1,0:T(8,128)(2,1)S(1)}, u32[]{:S(2)}, u32[]{:S(2)}) collective-permute-start(bf16[256,512]{1,0:T(8,128)(2,1)S(1)} %slice.7), channel_id=1, source_target_pairs={{16,0},{17,1},{18,2},{19,3},{20,4},{21,5},{22,6},{23,7},{24,8},{25... | collective-permute-start | bytes 786440 | tf_op jit(solution)/shard_map/ppermute | solution.py:23
  143.3 24.3 %collective-permute-start.2 = (bf16[256,512]{1,0:T(8,128)(2,1)S(1)}, bf16[256,512]{1,0:T(8,128)(2,1)S(1)}, u32[]{:S(2)}, u32[]{:S(2)}) collective-permute-start(bf16[256,512]{1,0:T(8,128)(2,1)S(1)} %slice.7), channel_id=1, source_target_pairs={{24,0},{25,1},{26,2},{27,3},{28,4},{29,5},{30,6},{31,7},{0,8},{1,9... | collective-permute-start | bytes 786440 | tf_op jit(solution)/shard_map/ppermute | solution.py:23
  176.5 2.0 copy-start.1
  232.4 2.2 copy-start.2

commit v4 on v3

--- a/solution.py
+++ b/solution.py
@@ -36,6 +36,31 @@
     )
 
 
+def metric_kernel(me_ref, rows_ref, out_ref):
+    copies, _, kept = out_ref.shape
+    side = rows_ref.shape[1] // X_LEN
+    my_x = me_ref[0] // copies
+    for k in range(kept // side):
+        place = lax.rem(my_x + k, X_LEN)
+        block = rows_ref[:, pl.ds(pl.multiple_of(place * side, side), side)]
+        for copy in range(copies):
+            out_ref[copy, :, k * side:(k + 1) * side] = block
+
+
+def metric_copies(rows, me, copies):
+    count, cols = rows.shape
+    return pl.pallas_call(
+        metric_kernel,
+        out_shape=jax.ShapeDtypeStruct((copies, count, 3 * cols // X_LEN), rows.dtype),
+        in_specs=[
+            pl.BlockSpec(memory_space=pltpu.SMEM),
+            pl.BlockSpec(memory_space=pltpu.VMEM),
+        ],
+        out_specs=pl.BlockSpec(memory_space=pltpu.VMEM),
+        compiler_params=pltpu.CompilerParams(vmem_limit_bytes=4 << 20),
+    )(me, rows)
+
+
 BLOCKS = {
     (0, 0): (0, 0), (0, 1): (0, 1), (0, 2): (0, 2),
     (1, 1): (1, 0), (1, 2): (1, 1), (1, 3): (1, 2),
@@ -44,15 +69,16 @@
 }
 
 
-def fit_kernel(x_ref, *refs):
+def fit_kernel(me_ref, *refs):
     *metric_refs, ints_ref, out_ref = refs
     parts, width, depth, cols = ints_ref.shape
     count = len(metric_refs)
     share = parts // count
     block = share * depth
+    my_x = me_ref[0] // share
     columns = []
     for k in range(count):
-        place = lax.rem(x_ref[0] + k, count)
+        place = lax.rem(my_x + k, count)
         tile = ints_ref[pl.ds(pl.multiple_of(place * share, share), share)]
         columns.append(jnp.concatenate(
             [tile[:, w].reshape(block, cols).T for w in range(width)], axis=0
@@ -68,14 +94,14 @@
                 preferred_element_type=jnp.float32,
             )
         total = total.astype(out_ref.dtype)
-        place = lax.rem(x_ref[0] + q, count)
+        place = lax.rem(my_x + q, count)
         for w in range(width):
             out_ref[w, :, pl.ds(pl.multiple_of(place * block, block), block)] = (
                 total[w * cols:(w + 1) * cols]
             )
 
 
-def fit(metric_parts, my_x, ints):
+def fit(metric_parts, me, ints):
     parts, slots, depth, cols = ints.shape
     width = 2
     rows = parts * depth
@@ -86,11 +112,11 @@
             num_scalar_prefetch=1,
             grid=(slots // width,),
             in_specs=[
-                pl.BlockSpec(part.shape, lambda i, x: (0, 0)) for part in metric_parts
+                pl.BlockSpec(part.shape, lambda i, me: (0, 0)) for part in metric_parts
             ] + [
-                pl.BlockSpec((parts, width, depth, cols), lambda i, x: (0, i, 0, 0)),
+                pl.BlockSpec((parts, width, depth, cols), lambda i, me: (0, i, 0, 0)),
             ],
-            out_specs=pl.BlockSpec((width, cols, rows), lambda i, x: (i, 0, 0)),
+            out_specs=pl.BlockSpec((width, cols, rows), lambda i, me: (i, 0, 0)),
         ),
         compiler_params=pltpu.CompilerParams(vmem_limit_bytes=24 << 20),
         cost_estimate=pl.CostEstimate(
@@ -98,7 +124,7 @@
             bytes_accessed=2 * rows * rows + 4 * rows * slots * cols,
             transcendentals=0,
         ),
-    )(my_x, *metric_parts, ints)
+    )(me, *metric_parts, ints)
 
 
 def close_kernel(fitted_ref, half_ref, out_ref, total_ref):
@@ -124,7 +150,7 @@
 
 def close(fitted, half):
     parts, slots, depth, cols = half.shape
-    width = 4
+    width = 2
     rows = parts * depth
     return pl.pallas_call(
         close_kernel,
@@ -142,7 +168,7 @@
             bytes_accessed=4 * rows * slots * cols,
             transcendentals=0,
         ),
-    )(fitted, half)
+    )(*(pltpu.with_memory_space_constraint(x, pltpu.HBM) for x in (fitted, half)))
 
 
 def local_density(density, dens_cols, neighbours):
@@ -179,21 +205,17 @@
     group = lax.axis_size("aux")
     z_len = group // X_LEN
     cols = ints.shape[2]
-    starts = jnp.arange(1, X_LEN, dtype=jnp.int32) * z_len
-    my_x = jnp.sum(starts <= lax.axis_index("aux"), dtype=jnp.int32)
-    side = rows.shape[1] // X_LEN
-    around = jnp.concatenate([rows, rows[:, :2 * side]], axis=1)
-    kept = lax.dynamic_slice_in_dim(around, my_x * side, 3 * side, 1)
-    line = to_all(jnp.broadcast_to(kept[None], (z_len, *kept.shape)), "z")
-    line = line.reshape(z_len * kept.shape[0], kept.shape[1])
+    me = lax.axis_index("aux")[None]
+    line = to_all(metric_copies(rows, me, z_len), "z")
+    line = line.reshape(-1, line.shape[2])
     line, ints_out = lax.optimization_barrier((line, by_slot(ints)))
     ints_moved = exchanged(ints_out)
-    short = line[:, :2 * side]
+    short = line[:, :2 * rows.shape[1] // X_LEN]
     parts = [line, from_x(line, -1), from_x(short, 2), from_x(short, 1)]
     dense = local_density(density, dens_cols, neighbours)
     half = jnp.einsum("ls,plm->psm", dense, ints, preferred_element_type=jnp.float32)
     half_moved = exchanged(by_slot(half.astype(jnp.bfloat16)))
-    fitted = fit(parts, my_x[None], ints_moved)
+    fitted = fit(parts, me, ints_moved)
     shares = close(fitted, half_moved)
     shares = jnp.sum(to_all(shares, "x"), axis=0)
     shares = jnp.broadcast_to(shares[None], (z_len, cols, cols))

time: 269 us -> 268 us (level)
  the two profiles are of different devices: /device:TPU:40 before, /device:TPU:32 now
where the time goes in v4:
time: 268 us; the launch traced here: 267 us
  waiting for transfers between devices  160 us (60%)
  starting transfers between devices  39.8 us (15%)
  blocking collectives  29.1 us (11%)
  local copies, waits for them, and re-layouts  15.9 us (6%)
  Pallas kernels  15.7 us (6%)
  matrix products  5.12 us (2%)
    all_to_all x2, waiting for transfers between devices, exchanged(): return lax.all_to_all(array, 'aux', split_axis=0, concat_axis=0, tiled=True)  128 us
    all_to_all x2, blocking collectives, to_all(): lax.all_to_all(copies, 'aux', split_axis=0, concat_axis=0, tiled=True, ax...  29.1 us
    ppermute x3, waiting for transfers between devices, from_x(): return lax.ppermute(block, 'aux', route)  21.5 us
    ppermute x3, starting transfers between devices, from_x(): return lax.ppermute(block, 'aux', route)  10.4 us
    all_to_all x2, starting transfers between devices, exchanged(): return lax.all_to_all(array, 'aux', split_axis=0, concat_axis=0, tiled=True)  10.3 us
    all_to_all x1, starting transfers between devices, to_all(): lax.all_to_all(copies, 'aux', split_axis=0, concat_axis=0, tiled=True, ax...  10.3 us
    ppermute x4, starting transfers between devices, passed_along(): return lax.ppermute(block, axis, route)  8.79 us
    pallas_call x1, Pallas kernels, fit(): pl.pallas_call(fit_kernel, out_shape=jax.ShapeDtypeStruct((slots, cols, r...  8.24 us
  transfers between devices with their start and end apart: 10, of which 6 were waited for; matrix products, arithmetic and copies ran while one was open for 7% of the time, Pallas kernels for 3%

profile of v4, /device:TPU:32, one launch (start us, length us, event | category | flops | bytes accessed | tf_op | source)
XLA Modules:
  0.0 266.9 jit_solution(6376004823540620768)
XLA Ops:
  0.0 0.0 copy-start
  0.0 0.0 copy-start.2
  0.0 0.9 copy-done.2
  0.9 0.8 shard_map.55
  1.6 10.3 %all-to-all-start = ((bf16[8,32,768]{2,1,0:T(8,128)(2,1)}), bf16[8,32,768]{2,1,0:T(8,128)(2,1)S(1)}, u32[]{:S(2)}, u32[]{:S(2)}) async-start(bf16[8,32,768]{2,1,0:T(8,128)(2,1)} %shard_map.55), calls=%async_computation | async-start | bytes 786432 | tf_op jit(solution)/shard_map/all_to_all | solution.py:33
  11.9 6.8 %copy.11 = bf16[512,32,128]{2,1,0:T(8,128)(2,1)} copy(bf16[512,32,128]{2,0,1:T(8,128)(2,1)} %bitcast.44) | data formatting | bytes 8388608 | tf_op jit(solution)/shard_map/transpose | solution.py:196
  18.8 7.8 %all-to-all-done = bf16[8,32,768]{2,1,0:T(8,128)(2,1)S(1)} async-done(((bf16[8,32,768]{2,1,0:T(8,128)(2,1)}), bf16[8,32,768]{2,1,0:T(8,128)(2,1)S(1)}, u32[]{:S(2)}, u32[]{:S(2)}) %all-to-all-start) | async-done | bytes 393248 | tf_op jit(solution)/shard_map/all_to_all | solution.py:33
  26.6 0.0 copy-start.3
  26.6 0.0 copy-start.4
  26.6 5.0 %all-to-all-start.1 = ((bf16[32,16,32,128]{3,2,1,0:T(8,128)(2,1)}), bf16[32,16,32,128]{3,2,1,0:T(8,128)(2,1)}, u32[]{:S(2)}, u32[]{:S(2)}) async-start(bf16[32,16,32,128]{3,2,1,0:T(8,128)(2,1)} %bitcast.42), calls=%async_computation.1 | async-start | bytes 8388608 | tf_op jit(solution)/shard_map/all_to_all | solution.py:200
  31.6 0.0 copy-done.3
  31.7 2.6 collective-permute-start.3
  34.2 0.0 collective-permute-start.4
  34.3 2.9 %collective-permute-start.5 = (bf16[1,4,128,128]{3,2,1,0:T(8,128)(2,1)S(1)}, bf16[1,4,128,128]{3,2,1,0:T(8,128)(2,1)S(1)}, u32[]{:S(2)}, u32[]{:S(2)}) collective-permute-start(bf16[1,4,128,128]{3,2,1,0:T(8,128)(2,1)S(1)} %copy-done.3), channel_id=1, source_target_pairs={{32,0},{64,32},{96,64},{128,96},{160,128},{192,160},{224,192},{256... | collective-permute-start | bytes 393224 | tf_op jit(solution)/shard_map/ppermute | solution.py:16
  37.2 3.2 %collective-permute-start.6 = (bf16[1,4,128,128]{3,2,1,0:T(8,128)(2,1)S(1)}, bf16[1,4,128,128]{3,2,1,0:T(8,128)(2,1)S(1)}, u32[]{:S(2)}, u32[]{:S(2)}) collective-permute-start(bf16[1,4,128,128]{3,2,1,0:T(8,128)(2,1)S(1)} %copy-done.3), channel_id=1, source_target_pairs={{64,0},{96,32},{128,64},{160,96},{192,128},{224,160},{256,192},{28... | collective-permute-start | bytes 393224 | tf_op jit(solution)/shard_map/ppermute | solution.py:16
  40.5 0.0 copy-done.4
  40.5 0.1 copy.12
  40.6 0.0 copy-done
  40.6 0.2 dynamic-slice_reduce_fusion
  40.8 0.6 gather_fusion.1
  41.4 0.1 broadcast_select_fusion.1
  41.4 0.0 collective-permute-done.3
  41.5 0.0 collective-permute-done.4
  41.5 0.0 collective-permute-done.5
  41.6 2.5 collective-permute-done.6
  44.1 0.6 gather_fusion
  44.7 0.1 broadcast_select_fusion
  44.9 0.5 convolution_convert_fusion
  45.4 4.6 %fusion.2 = bf16[512,32,128]{2,0,1:T(8,128)(2,1)S(1)} fusion(bf16[1,32,512,128]{3,2,1,0:T(8,128)(2,1)} %param.5, bf16[64,8,4,128]{3,2,1,0:T(4,128)(2,1)S(1)} %bitcast.45), kind=kOutput, calls=%fused_computation.4 | convolution fusion | flops 2149580800 | bytes 8912896 | tf_op jit(solution)/shard_map/ls,plm->psm/dot_general | solution.py:216
  50.0 4.7 %copy.15 = bf16[512,32,128]{2,1,0:T(8,128)(2,1)} copy(bf16[512,32,128]{2,0,1:T(8,128)(2,1)S(1)} %fusion.2) | data formatting | bytes 8388608 | tf_op jit(solution)/shard_map/convert_element_type | solution.py:217
  54.7 73.6 %all-to-all-done.1.refs_4_ = bf16[32,16,32,128]{3,2,1,0:T(8,128)(2,1)} async-done(((bf16[32,16,32,128]{3,2,1,0:T(8,128)(2,1)}), bf16[32,16,32,128]{3,2,1,0:T(8,128)(2,1)}, u32[]{:S(2)}, u32[]{:S(2)}) %all-to-all-start.1) | async-done | bytes 4194336 | tf_op jit(solution)/shard_map/all_to_all | solution.py:200
  128.2 5.3 %all-to-all-start.2 = ((bf16[32,16,32,128]{3,2,1,0:T(8,128)(2,1)}), bf16[32,16,32,128]{3,2,1,0:T(8,128)(2,1)}, u32[]{:S(2)}, u32[]{:S(2)}) async-start(bf16[32,16,32,128]{3,2,1,0:T(8,128)(2,1)} %bitcast.43), calls=%async_computation.2 | async-start | bytes 8388608 | tf_op jit(solution)/shard_map/all_to_all | solution.py:200
  133.6 4.9 %collective-permute-start = (bf16[256,768]{1,0:T(8,128)(2,1)S(1)}, bf16[256,768]{1,0:T(8,128)(2,1)S(1)}, u32[]{:S(2)}, u32[]{:S(2)}) collective-permute-start(bf16[256,768]{1,0:T(8,128)(2,1)S(1)} %bitcast.38), channel_id=1, source_target_pairs={{8,0},{9,1},{10,2},{11,3},{12,4},{13,5},{14,6},{15,7},{16,8},{17,9... | collective-permute-start | bytes 1179656 | tf_op jit(solution)/shard_map/ppermute | solution.py:23
  138.5 2.7 %collective-permute-start.1 = (bf16[256,512]{1,0:T(8,128)(2,1)S(1)}, bf16[256,512]{1,0:T(8,128)(2,1)S(1)}, u32[]{:S(2)}, u32[]{:S(2)}) collective-permute-start(bf16[256,512]{1,0:T(8,128)(2,1)S(1)} %slice.3), channel_id=1, source_target_pairs={{16,0},{17,1},{18,2},{19,3},{20,4},{21,5},{22,6},{23,7},{24,8},{25... | collective-permute-start | bytes 786440 | tf_op jit(solution)/shard_map/ppermute | solution.py:23
  141.2 2.8 %collective-permute-start.2 = (bf16[256,512]{1,0:T(8,128)(2,1)S(1)}, bf16[256,512]{1,0:T(8,128)(2,1)S(1)}, u32[]{:S(2)}, u32[]{:S(2)}) collective-permute-start(bf16[256,512]{1,0:T(8,128)(2,1)S(1)} %slice.3), channel_id=1, source_target_pairs={{24,0},{25,1},{26,2},{27,3},{28,4},{29,5},{30,6},{31,7},{0,8},{1,9... | collective-permute-start | bytes 786440 | tf_op jit(solution)/shard_map/ppermute | solution.py:23
  144.0 14.9 %collective-permute-done.1.refs_2_ = bf16[256,512]{1,0:T(8,128)(2,1)S(1)} collective-permute-done((bf16[256,512]{1,0:T(8,128)(2,1)S(1)}, bf16[256,512]{1,0:T(8,128)(2,1)S(1)}, u32[]{:S(2)}, u32[]{:S(2)}) %collective-permute-start.1) | collective-permute-done | bytes 262176 | tf_op jit(solution)/shard_map/ppermute | solution.py:23
  158.9 6.6 %collective-permute-done.2.refs_3_ = bf16[256,512]{1,0:T(8,128)(2,1)S(1)} collective-permute-done((bf16[256,512]{1,0:T(8,128)(2,1)S(1)}, bf16[256,512]{1,0:T(8,128)(2,1)S(1)}, u32[]{:S(2)}, u32[]{:S(2)}) %collective-permute-start.2) | collective-permute-done | bytes 262176 | tf_op jit(solution)/shard_map/ppermute | solution.py:23
  165.5 0.0 collective-permute-done.refs_1_
  165.5 8.2 %shard_map.56.fitted_ref = bf16[16,128,1024]{2,1,0:T(8,128)(2,1)S(1)} custom-call(s32[1]{0:T(128)} %bitcast.me_ref, bf16[256,768]{1,0:T(8,128)(2,1)S(1)} %bitcast.40, bf16[256,768]{1,0:T(8,128)(2,1)S(1)} %collective-permute-done.refs_1_, bf16[256,512]{1,0:T(8,128)(2,1)S(1)} %collective-permute-done.1.refs_2_, ...), custom_call_target="tpu_custom_call" | custom-call | flops 4294967296 | bytes 10485760 | tf_op jit(solution)/shard_map/pallas_call | solution.py:108
  173.8 0.0 copy-start.1
  173.8 2.0 copy-done.1
  175.7 54.6 %all-to-all-done.2.half_ref = bf16[32,16,32,128]{3,2,1,0:T(8,128)(2,1)} async-done(((bf16[32,16,32,128]{3,2,1,0:T(8,128)(2,1)}), bf16[32,16,32,128]{3,2,1,0:T(8,128)(2,1)}, u32[]{:S(2)}, u32[]{:S(2)}) %all-to-all-start.2) | async-done | bytes 4194336 | tf_op jit(solution)/shard_map/all_to_all | solution.py:200
  230.3 6.7 %shard_map.57 = f32[4,128,128]{2,1,0:T(8,128)S(1)} custom-call(bf16[16,128,1024]{2,1,0:T(8,128)(2,1)} %copy-done.1, bf16[32,16,32,128]{3,2,1,0:T(8,128)(2,1)} %all-to-all-done.2.half_ref), custom_call_target="tpu_custom_call" | custom-call | flops 536870912 | bytes 8388608 | tf_op jit(solution)/shard_map/pallas_call | solution.py:155
  237.0 9.1 %all_to_all.25 = f32[4,128,128]{2,1,0:T(8,128)S(1)} all-to-all(f32[4,128,128]{2,1,0:T(8,128)S(1)} %shard_map.57), channel_id=1, replica_groups={{0,8,16,24},{1,9,17,25},{2,10,18,26},{3,11,19,27},{4,12,20,28},{5,13,21..., dimensions={0} | all-to-all | bytes 524288 | tf_op jit(solution)/shard_map/all_to_all | solution.py:33
  246.2 20.0 %all_to_all.26 = f32[8,128,128]{2,1,0:T(8,128)S(1)} all-to-all(f32[8,128,128]{2,1,0:T(8,128)S(1)} %broadcast_in_dim.34), channel_id=1, replica_groups={{0,1,2,3,4,5,6,7},{8,9,10,11,12,13,14,15},{16,17,18,19,20,21,22,23},{24..., dimensions={0} | all-to-all | bytes 1048576 | tf_op jit(solution)/shard_map/all_to_all | solution.py:33
  266.2 0.7 reduce_sum.19
  (12 shorter events, 0.2 us)
Async XLA Ops:
  0.0 40.6 %copy-start = (s32[16,4]{0,1:T(4,128)S(1)}, s32[16,4]{0,1:T(4,128)}, u32[]{:S(2)}) copy-start(s32[16,4]{0,1:T(4,128)} %param.8) | copy-start | bytes 772
  0.0 0.9 copy-start.2
  1.6 25.0 %all-to-all-start = ((bf16[8,32,768]{2,1,0:T(8,128)(2,1)}), bf16[8,32,768]{2,1,0:T(8,128)(2,1)S(1)}, u32[]{:S(2)}, u32[]{:S(2)}) async-start(bf16[8,32,768]{2,1,0:T(8,128)(2,1)} %shard_map.55), calls=%async_computation | async-start | bytes 786432 | tf_op jit(solution)/shard_map/all_to_all | solution.py:33
  26.6 5.0 %copy-start.3 = (bf16[1,4,128,128]{3,2,1,0:T(8,128)(2,1)S(1)}, bf16[1,4,128,128]{3,2,1,0:T(8,128)(2,1)}, u32[]{:S(2)}) copy-start(bf16[1,4,128,128]{3,2,1,0:T(8,128)(2,1)} %param.6) | copy-start | bytes 393220
  26.6 13.8 %copy-start.4 = (s32[16,4]{0,1:T(4,128)S(1)}, s32[16,4]{0,1:T(4,128)}, u32[]{:S(2)}) copy-start(s32[16,4]{0,1:T(4,128)} %param.7) | copy-start | bytes 772
  26.6 101.6 %all-to-all-start.1 = ((bf16[32,16,32,128]{3,2,1,0:T(8,128)(2,1)}), bf16[32,16,32,128]{3,2,1,0:T(8,128)(2,1)}, u32[]{:S(2)}, u32[]{:S(2)}) async-start(bf16[32,16,32,128]{3,2,1,0:T(8,128)(2,1)} %bitcast.42), calls=%async_computation.1 | async-start | bytes 8388608 | tf_op jit(solution)/shard_map/all_to_all | solution.py:200
  31.7 9.8 %collective-permute-start.3 = (bf16[1,4,128,128]{3,2,1,0:T(8,128)(2,1)S(1)}, bf16[1,4,128,128]{3,2,1,0:T(8,128)(2,1)S(1)}, u32[]{:S(2)}, u32[]{:S(2)}) collective-permute-start(bf16[1,4,128,128]{3,2,1,0:T(8,128)(2,1)S(1)} %copy-done.3), channel_id=1, source_target_pairs={{448,0},{480,32},{0,64},{32,96},{64,128},{96,160},{128,192},{160,2... | collective-permute-start | bytes 393224 | tf_op jit(solution)/shard_map/ppermute | solution.py:16
  34.2 7.2 %collective-permute-start.4 = (bf16[1,4,128,128]{3,2,1,0:T(8,128)(2,1)S(1)}, bf16[1,4,128,128]{3,2,1,0:T(8,128)(2,1)S(1)}, u32[]{:S(2)}, u32[]{:S(2)}) collective-permute-start(bf16[1,4,128,128]{3,2,1,0:T(8,128)(2,1)S(1)} %copy-done.3), channel_id=1, source_target_pairs={{480,0},{0,32},{32,64},{64,96},{96,128},{128,160},{160,192},{192,2... | collective-permute-start | bytes 393224 | tf_op jit(solution)/shard_map/ppermute | solution.py:16
  34.3 7.3 %collective-permute-start.5 = (bf16[1,4,128,128]{3,2,1,0:T(8,128)(2,1)S(1)}, bf16[1,4,128,128]{3,2,1,0:T(8,128)(2,1)S(1)}, u32[]{:S(2)}, u32[]{:S(2)}) collective-permute-start(bf16[1,4,128,128]{3,2,1,0:T(8,128)(2,1)S(1)} %copy-done.3), channel_id=1, source_target_pairs={{32,0},{64,32},{96,64},{128,96},{160,128},{192,160},{224,192},{256... | collective-permute-start | bytes 393224 | tf_op jit(solution)/shard_map/ppermute | solution.py:16
  37.2 6.8 %collective-permute-start.6 = (bf16[1,4,128,128]{3,2,1,0:T(8,128)(2,1)S(1)}, bf16[1,4,128,128]{3,2,1,0:T(8,128)(2,1)S(1)}, u32[]{:S(2)}, u32[]{:S(2)}) collective-permute-start(bf16[1,4,128,128]{3,2,1,0:T(8,128)(2,1)S(1)} %copy-done.3), channel_id=1, source_target_pairs={{64,0},{96,32},{128,64},{160,96},{192,128},{224,160},{256,192},{28... | collective-permute-start | bytes 393224 | tf_op jit(solution)/shard_map/ppermute | solution.py:16
  128.2 102.1 %all-to-all-start.2 = ((bf16[32,16,32,128]{3,2,1,0:T(8,128)(2,1)}), bf16[32,16,32,128]{3,2,1,0:T(8,128)(2,1)}, u32[]{:S(2)}, u32[]{:S(2)}) async-start(bf16[32,16,32,128]{3,2,1,0:T(8,128)(2,1)} %bitcast.43), calls=%async_computation.2 | async-start | bytes 8388608 | tf_op jit(solution)/shard_map/all_to_all | solution.py:200
  133.6 31.9 %collective-permute-start = (bf16[256,768]{1,0:T(8,128)(2,1)S(1)}, bf16[256,768]{1,0:T(8,128)(2,1)S(1)}, u32[]{:S(2)}, u32[]{:S(2)}) collective-permute-start(bf16[256,768]{1,0:T(8,128)(2,1)S(1)} %bitcast.38), channel_id=1, source_target_pairs={{8,0},{9,1},{10,2},{11,3},{12,4},{13,5},{14,6},{15,7},{16,8},{17,9... | collective-permute-start | bytes 1179656 | tf_op jit(solution)/shard_map/ppermute | solution.py:23
  138.5 20.4 %collective-permute-start.1 = (bf16[256,512]{1,0:T(8,128)(2,1)S(1)}, bf16[256,512]{1,0:T(8,128)(2,1)S(1)}, u32[]{:S(2)}, u32[]{:S(2)}) collective-permute-start(bf16[256,512]{1,0:T(8,128)(2,1)S(1)} %slice.3), channel_id=1, source_target_pairs={{16,0},{17,1},{18,2},{19,3},{20,4},{21,5},{22,6},{23,7},{24,8},{25... | collective-permute-start | bytes 786440 | tf_op jit(solution)/shard_map/ppermute | solution.py:23
  141.2 24.3 %collective-permute-start.2 = (bf16[256,512]{1,0:T(8,128)(2,1)S(1)}, bf16[256,512]{1,0:T(8,128)(2,1)S(1)}, u32[]{:S(2)}, u32[]{:S(2)}) collective-permute-start(bf16[256,512]{1,0:T(8,128)(2,1)S(1)} %slice.3), channel_id=1, source_target_pairs={{24,0},{25,1},{26,2},{27,3},{28,4},{29,5},{30,6},{31,7},{0,8},{1,9... | collective-permute-start | bytes 786440 | tf_op jit(solution)/shard_map/ppermute | solution.py:23
  173.8 2.0 copy-start.1

commit v5 on v4

--- a/solution.py
+++ b/solution.py
@@ -101,8 +101,8 @@
             )
 
 
-def fit(metric_parts, me, ints):
-    parts, slots, depth, cols = ints.shape
+def fit(metric_parts, me, ints, first, slots):
+    parts, _, depth, cols = ints.shape
     width = 2
     rows = parts * depth
     return pl.pallas_call(
@@ -114,11 +114,14 @@
             in_specs=[
                 pl.BlockSpec(part.shape, lambda i, me: (0, 0)) for part in metric_parts
             ] + [
-                pl.BlockSpec((parts, width, depth, cols), lambda i, me: (0, i, 0, 0)),
+                pl.BlockSpec(
+                    (parts, width, depth, cols),
+                    lambda i, me: (0, i + first // width, 0, 0),
+                ),
             ],
             out_specs=pl.BlockSpec((width, cols, rows), lambda i, me: (i, 0, 0)),
         ),
-        compiler_params=pltpu.CompilerParams(vmem_limit_bytes=24 << 20),
+        compiler_params=pltpu.CompilerParams(vmem_limit_bytes=12 << 20),
         cost_estimate=pl.CostEstimate(
             flops=2 * rows * rows * slots * cols,
             bytes_accessed=2 * rows * rows + 4 * rows * slots * cols,
@@ -127,18 +130,20 @@
     )(me, *metric_parts, ints)
 
 
-def close_kernel(fitted_ref, half_ref, out_ref, total_ref):
+def close_kernel(*refs):
+    *pairs, out_ref, total_ref = refs
     step = pl.program_id(0)
-    parts, width, depth, cols = half_ref.shape
 
     @pl.when(step == 0)
     def _():
         total_ref[...] = jnp.zeros_like(total_ref)
 
     total = total_ref[...]
-    for w in range(width):
-        right = half_ref[:, w].reshape(parts * depth, cols)
-        total += jnp.dot(fitted_ref[w], right, preferred_element_type=jnp.float32)
+    for fitted_ref, half_ref in zip(pairs[::2], pairs[1::2]):
+        parts, width, depth, cols = half_ref.shape
+        for w in range(width):
+            right = half_ref[:, w].reshape(parts * depth, cols)
+            total += jnp.dot(fitted_ref[w], right, preferred_element_type=jnp.float32)
     total_ref[...] = total
 
     @pl.when(step == pl.num_programs(0) - 1)
@@ -148,27 +153,33 @@
             out_ref[k] = done
 
 
-def close(fitted, half):
+def close(fitted_parts, half, steps):
     parts, slots, depth, cols = half.shape
-    width = 2
     rows = parts * depth
+    specs, operands, first = [], [], 0
+    for fitted in fitted_parts:
+        width = fitted.shape[0] // steps
+        specs.append(pl.BlockSpec((width, cols, rows), lambda i: (i, 0, 0)))
+        specs.append(pl.BlockSpec(
+            (parts, width, depth, cols),
+            lambda i, start=first // width: (0, i + start, 0, 0),
+        ))
+        operands += [fitted, half]
+        first += fitted.shape[0]
     return pl.pallas_call(
         close_kernel,
         out_shape=jax.ShapeDtypeStruct((X_LEN, cols, cols), jnp.float32),
-        grid=(slots // width,),
-        in_specs=[
-            pl.BlockSpec((width, cols, rows), lambda i: (i, 0, 0)),
-            pl.BlockSpec((parts, width, depth, cols), lambda i: (0, i, 0, 0)),
-        ],
+        grid=(steps,),
+        in_specs=specs,
         out_specs=pl.BlockSpec((X_LEN, cols, cols), lambda i: (0, 0, 0)),
         scratch_shapes=[pltpu.VMEM((cols, cols), jnp.float32)],
-        compiler_params=pltpu.CompilerParams(vmem_limit_bytes=24 << 20),
+        compiler_params=pltpu.CompilerParams(vmem_limit_bytes=12 << 20),
         cost_estimate=pl.CostEstimate(
             flops=2 * rows * slots * cols * cols,
             bytes_accessed=4 * rows * slots * cols,
             transcendentals=0,
         ),
-    )(*(pltpu.with_memory_space_constraint(x, pltpu.HBM) for x in (fitted, half)))
+    )(*operands)
 
 
 def local_density(density, dens_cols, neighbours):
@@ -215,11 +226,17 @@
     dense = local_density(density, dens_cols, neighbours)
     half = jnp.einsum("ls,plm->psm", dense, ints, preferred_element_type=jnp.float32)
     half_moved = exchanged(by_slot(half.astype(jnp.bfloat16)))
-    fitted = fit(parts, me, ints_moved)
-    shares = close(fitted, half_moved)
-    shares = jnp.sum(to_all(shares, "x"), axis=0)
+    most = 3 * ints_moved.shape[1] // 4
+    rest = fit(parts, me, ints_moved, most, ints_moved.shape[1] - most)
+    fitted = [
+        fit(parts, me, ints_moved, 0, most),
+        pltpu.with_memory_space_constraint(rest, pltpu.HBM),
+    ]
+    shares = close(fitted, half_moved, 4)
+    shares = jnp.sum(to_all(shares, "x"), axis=0).astype(jnp.bfloat16)
     shares = jnp.broadcast_to(shares[None], (z_len, cols, cols))
-    return jnp.sum(to_all(shares, "z"), axis=0)[None]
+    shares = to_all(shares, "z").astype(jnp.float32)
+    return jnp.sum(shares, axis=0)[None]
 
 
 def solution(mesh):

time: 268 us -> 260 us (0.970)
  the two profiles are of different devices: /device:TPU:32 before, /device:TPU:48 now
where the time goes in v5:
time: 260 us; the launch traced here: 259 us
  waiting for transfers between devices  162 us (62%)
  starting transfers between devices  38 us (15%)
  blocking collectives  23.8 us (9%)
  local copies, waits for them, and re-layouts  15 us (6%)
  Pallas kernels  13.9 us (5%)
  matrix products  5.11 us (2%)
    all_to_all x2, waiting for transfers between devices, exchanged(): return lax.all_to_all(array, 'aux', split_axis=0, concat_axis=0, tiled=True)  129 us
    all_to_all x2, blocking collectives, to_all(): lax.all_to_all(copies, 'aux', split_axis=0, concat_axis=0, tiled=True, ax...  23.8 us
    ppermute x3, waiting for transfers between devices, from_x(): return lax.ppermute(block, 'aux', route)  21.6 us
    ppermute x3, starting transfers between devices, from_x(): return lax.ppermute(block, 'aux', route)  11 us
    all_to_all x1, starting transfers between devices, to_all(): lax.all_to_all(copies, 'aux', split_axis=0, concat_axis=0, tiled=True, ax...  10.3 us
    all_to_all x2, starting transfers between devices, exchanged(): return lax.all_to_all(array, 'aux', split_axis=0, concat_axis=0, tiled=True)  10.3 us
    pallas_call x2, Pallas kernels, fit(): pl.pallas_call(fit_kernel, out_shape=jax.ShapeDtypeStruct((slots, cols, r...  8.99 us
    all_to_all x1, waiting for transfers between devices, to_all(): lax.all_to_all(copies, 'aux', split_axis=0, concat_axis=0, tiled=True, ax...  7.84 us
  transfers between devices with their start and end apart: 10, of which 6 were waited for; matrix products, arithmetic and copies ran while one was open for 7% of the time, Pallas kernels for 3%

profile of v5, /device:TPU:48, one launch (start us, length us, event | category | flops | bytes accessed | tf_op | source)
XLA Modules:
  0.0 258.9 jit_solution(8722084549154269499)
XLA Ops:
  0.0 0.0 copy-start
  0.0 0.0 copy-start.2
  0.0 0.9 copy-done.2
  0.9 0.8 shard_map.55
  1.6 10.3 %all-to-all-start = ((bf16[8,32,768]{2,1,0:T(8,128)(2,1)}), bf16[8,32,768]{2,1,0:T(8,128)(2,1)S(1)}, u32[]{:S(2)}, u32[]{:S(2)}) async-start(bf16[8,32,768]{2,1,0:T(8,128)(2,1)} %shard_map.55), calls=%async_computation | async-start | bytes 786432 | tf_op jit(solution)/shard_map/all_to_all | solution.py:33
  11.9 6.8 %copy.11 = bf16[512,32,128]{2,1,0:T(8,128)(2,1)} copy(bf16[512,32,128]{2,0,1:T(8,128)(2,1)} %bitcast.45) | data formatting | bytes 8388608 | tf_op jit(solution)/shard_map/transpose | solution.py:207
  18.8 7.8 %all-to-all-done = bf16[8,32,768]{2,1,0:T(8,128)(2,1)S(1)} async-done(((bf16[8,32,768]{2,1,0:T(8,128)(2,1)}), bf16[8,32,768]{2,1,0:T(8,128)(2,1)S(1)}, u32[]{:S(2)}, u32[]{:S(2)}) %all-to-all-start) | async-done | bytes 393248 | tf_op jit(solution)/shard_map/all_to_all | solution.py:33
  26.6 0.0 copy-start.3
  26.6 0.0 copy-start.4
  26.6 5.0 %all-to-all-start.1 = ((bf16[32,16,32,128]{3,2,1,0:T(8,128)(2,1)}), bf16[32,16,32,128]{3,2,1,0:T(8,128)(2,1)}, u32[]{:S(2)}, u32[]{:S(2)}) async-start(bf16[32,16,32,128]{3,2,1,0:T(8,128)(2,1)} %bitcast.43), calls=%async_computation.1 | async-start | bytes 8388608 | tf_op jit(solution)/shard_map/all_to_all | solution.py:211
  31.6 0.0 copy-done.3
  31.6 0.1 collective-permute-start.5
  31.7 0.4 collective-permute-start.4
  32.2 2.6 collective-permute-start.3
  34.7 3.3 %collective-permute-start.6 = (bf16[1,4,128,128]{3,2,1,0:T(8,128)(2,1)S(1)}, bf16[1,4,128,128]{3,2,1,0:T(8,128)(2,1)S(1)}, u32[]{:S(2)}, u32[]{:S(2)}) collective-permute-start(bf16[1,4,128,128]{3,2,1,0:T(8,128)(2,1)S(1)} %copy-done.3), channel_id=1, source_target_pairs={{64,0},{96,32},{128,64},{160,96},{192,128},{224,160},{256,192},{28... | collective-permute-start | bytes 393224 | tf_op jit(solution)/shard_map/ppermute | solution.py:16
  38.0 0.0 copy-done.4
  38.0 0.1 copy.12
  38.1 0.0 copy-done
  38.1 0.2 dynamic-slice_reduce_fusion
  38.3 0.6 gather_fusion.1
  38.9 0.1 broadcast_select_fusion.1
  39.0 0.8 collective-permute-done.3
  39.8 0.0 collective-permute-done.4
  39.9 0.0 collective-permute-done.5
  39.9 2.7 %collective-permute-done.6 = bf16[1,4,128,128]{3,2,1,0:T(8,128)(2,1)S(1)} collective-permute-done((bf16[1,4,128,128]{3,2,1,0:T(8,128)(2,1)S(1)}, bf16[1,4,128,128]{3,2,1,0:T(8,128)(2,1)S(1)}, u32[]{:S(2)}, u32[]{:S(2)}) %collective-permute-start.6) | collective-permute-done | bytes 131104 | tf_op jit(solution)/shard_map/ppermute | solution.py:16
  42.7 0.6 gather_fusion
  43.3 0.1 broadcast_select_fusion
  43.5 0.5 convolution_convert_fusion
  44.0 4.6 %fusion.2 = bf16[512,32,128]{2,0,1:T(8,128)(2,1)S(1)} fusion(bf16[1,32,512,128]{3,2,1,0:T(8,128)(2,1)} %param.5, bf16[64,8,4,128]{3,2,1,0:T(4,128)(2,1)S(1)} %bitcast.46), kind=kOutput, calls=%fused_computation.4 | convolution fusion | flops 2149580800 | bytes 8912896 | tf_op jit(solution)/shard_map/ls,plm->psm/dot_general | solution.py:227
  48.6 4.7 %copy.15 = bf16[512,32,128]{2,1,0:T(8,128)(2,1)} copy(bf16[512,32,128]{2,0,1:T(8,128)(2,1)S(1)} %fusion.2) | data formatting | bytes 8388608 | tf_op jit(solution)/shard_map/convert_element_type | solution.py:228
  53.3 75.0 %all-to-all-done.1.refs_4_ = bf16[32,16,32,128]{3,2,1,0:T(8,128)(2,1)} async-done(((bf16[32,16,32,128]{3,2,1,0:T(8,128)(2,1)}), bf16[32,16,32,128]{3,2,1,0:T(8,128)(2,1)}, u32[]{:S(2)}, u32[]{:S(2)}) %all-to-all-start.1) | async-done | bytes 4194336 | tf_op jit(solution)/shard_map/all_to_all | solution.py:211
  128.2 5.3 %all-to-all-start.2 = ((bf16[32,16,32,128]{3,2,1,0:T(8,128)(2,1)}), bf16[32,16,32,128]{3,2,1,0:T(8,128)(2,1)}, u32[]{:S(2)}, u32[]{:S(2)}) async-start(bf16[32,16,32,128]{3,2,1,0:T(8,128)(2,1)} %bitcast.44), calls=%async_computation.2 | async-start | bytes 8388608 | tf_op jit(solution)/shard_map/all_to_all | solution.py:211
  133.6 4.9 %collective-permute-start = (bf16[256,768]{1,0:T(8,128)(2,1)S(1)}, bf16[256,768]{1,0:T(8,128)(2,1)S(1)}, u32[]{:S(2)}, u32[]{:S(2)}) collective-permute-start(bf16[256,768]{1,0:T(8,128)(2,1)S(1)} %bitcast.38), channel_id=1, source_target_pairs={{8,0},{9,1},{10,2},{11,3},{12,4},{13,5},{14,6},{15,7},{16,8},{17,9... | collective-permute-start | bytes 1179656 | tf_op jit(solution)/shard_map/ppermute | solution.py:23
  138.5 1.9 collective-permute-start.2
  140.4 4.2 %collective-permute-start.1 = (bf16[256,512]{1,0:T(8,128)(2,1)S(1)}, bf16[256,512]{1,0:T(8,128)(2,1)S(1)}, u32[]{:S(2)}, u32[]{:S(2)}) collective-permute-start(bf16[256,512]{1,0:T(8,128)(2,1)S(1)} %slice.3), channel_id=1, source_target_pairs={{16,0},{17,1},{18,2},{19,3},{20,4},{21,5},{22,6},{23,7},{24,8},{25... | collective-permute-start | bytes 786440 | tf_op jit(solution)/shard_map/ppermute | solution.py:23
  144.6 21.6 %collective-permute-done.2.refs_3_ = bf16[256,512]{1,0:T(8,128)(2,1)S(1)} collective-permute-done((bf16[256,512]{1,0:T(8,128)(2,1)S(1)}, bf16[256,512]{1,0:T(8,128)(2,1)S(1)}, u32[]{:S(2)}, u32[]{:S(2)}) %collective-permute-start.2) | collective-permute-done | bytes 262176 | tf_op jit(solution)/shard_map/ppermute | solution.py:23
  166.2 0.0 collective-permute-done.1.refs_2_
  166.2 0.0 collective-permute-done.refs_1_
  166.2 2.6 %shard_map.57.refs_2_ = bf16[4,128,1024]{2,1,0:T(8,128)(2,1)S(1)} custom-call(s32[1]{0:T(128)} %bitcast.me_ref, bf16[256,768]{1,0:T(8,128)(2,1)S(1)} %bitcast.40, bf16[256,768]{1,0:T(8,128)(2,1)S(1)} %collective-permute-done.refs_1_, bf16[256,512]{1,0:T(8,128)(2,1)S(1)} %collective-permute-done.1.refs_2_, ...), custom_call_target="tpu_custom_call" | custom-call | flops 1073741824 | bytes 4194304 | tf_op jit(solution)/shard_map/pallas_call | solution.py:108
  168.9 0.0 copy-start.1
  168.9 1.0 copy-done.1
  169.9 6.4 %shard_map.56.refs_0_ = bf16[12,128,1024]{2,1,0:T(8,128)(2,1)S(1)} custom-call(s32[1]{0:T(128)} %bitcast.me_ref, bf16[256,768]{1,0:T(8,128)(2,1)S(1)} %bitcast.41, bf16[256,768]{1,0:T(8,128)(2,1)S(1)} %collective-permute-done.refs_1_, bf16[256,512]{1,0:T(8,128)(2,1)S(1)} %collective-permute-done.1.refs_2_, ...), custom_call_target="tpu_custom_call" | custom-call | flops 3221225472 | bytes 8388608 | tf_op jit(solution)/shard_map/pallas_call | solution.py:108
  176.3 54.0 %all-to-all-done.2.refs_1_.refs_3_ = bf16[32,16,32,128]{3,2,1,0:T(8,128)(2,1)} async-done(((bf16[32,16,32,128]{3,2,1,0:T(8,128)(2,1)}), bf16[32,16,32,128]{3,2,1,0:T(8,128)(2,1)}, u32[]{:S(2)}, u32[]{:S(2)}) %all-to-all-start.2) | async-done | bytes 4194336 | tf_op jit(solution)/shard_map/all_to_all | solution.py:211
  230.3 4.2 %shard_map.58 = f32[4,128,128]{2,1,0:T(8,128)S(1)} custom-call(bf16[12,128,1024]{2,1,0:T(8,128)(2,1)S(1)} %shard_map.56.refs_0_, bf16[32,16,32,128]{3,2,1,0:T(8,128)(2,1)} %all-to-all-done.2.refs_1_.refs_3_, bf16[4,128,1024]{2,1,0:T(8,128)(2,1)} %copy-done.1, bf16[32,16,32,128]{3,2,1,0:T(8,128)(2,1)} %all-to-all-done.2.refs_1_.refs_3_), custom_call_target="tpu_custom_call" | custom-call | flops 536870912 | bytes 8388608 | tf_op jit(solution)/shard_map/pallas_call | solution.py:169
  234.4 9.1 %all_to_all.25 = f32[4,128,128]{2,1,0:T(8,128)S(1)} all-to-all(f32[4,128,128]{2,1,0:T(8,128)S(1)} %shard_map.58), channel_id=1, replica_groups={{0,8,16,24},{1,9,17,25},{2,10,18,26},{3,11,19,27},{4,12,20,28},{5,13,21..., dimensions={0} | all-to-all | bytes 524288 | tf_op jit(solution)/shard_map/all_to_all | solution.py:33
  243.6 14.7 %all_to_all.26 = bf16[8,128,128]{2,1,0:T(8,128)(2,1)S(1)} all-to-all(bf16[8,128,128]{2,1,0:T(8,128)(2,1)S(1)} %broadcast_in_dim.34), channel_id=1, replica_groups={{0,1,2,3,4,5,6,7},{8,9,10,11,12,13,14,15},{16,17,18,19,20,21,22,23},{24..., dimensions={0} | all-to-all | bytes 524288 | tf_op jit(solution)/shard_map/all_to_all | solution.py:33
  258.3 0.7 convert_reduce_fusion
  (12 shorter events, 0.2 us)
Async XLA Ops:
  0.0 38.1 %copy-start = (s32[16,4]{0,1:T(4,128)S(1)}, s32[16,4]{0,1:T(4,128)}, u32[]{:S(2)}) copy-start(s32[16,4]{0,1:T(4,128)} %param.8) | copy-start | bytes 772
  0.0 0.9 copy-start.2
  1.6 25.0 %all-to-all-start = ((bf16[8,32,768]{2,1,0:T(8,128)(2,1)}), bf16[8,32,768]{2,1,0:T(8,128)(2,1)S(1)}, u32[]{:S(2)}, u32[]{:S(2)}) async-start(bf16[8,32,768]{2,1,0:T(8,128)(2,1)} %shard_map.55), calls=%async_computation | async-start | bytes 786432 | tf_op jit(solution)/shard_map/all_to_all | solution.py:33
  26.6 5.0 %copy-start.3 = (bf16[1,4,128,128]{3,2,1,0:T(8,128)(2,1)S(1)}, bf16[1,4,128,128]{3,2,1,0:T(8,128)(2,1)}, u32[]{:S(2)}) copy-start(bf16[1,4,128,128]{3,2,1,0:T(8,128)(2,1)} %param.6) | copy-start | bytes 393220
  26.6 11.4 %copy-start.4 = (s32[16,4]{0,1:T(4,128)S(1)}, s32[16,4]{0,1:T(4,128)}, u32[]{:S(2)}) copy-start(s32[16,4]{0,1:T(4,128)} %param.7) | copy-start | bytes 772
  26.6 101.6 %all-to-all-start.1 = ((bf16[32,16,32,128]{3,2,1,0:T(8,128)(2,1)}), bf16[32,16,32,128]{3,2,1,0:T(8,128)(2,1)}, u32[]{:S(2)}, u32[]{:S(2)}) async-start(bf16[32,16,32,128]{3,2,1,0:T(8,128)(2,1)} %bitcast.43), calls=%async_computation.1 | async-start | bytes 8388608 | tf_op jit(solution)/shard_map/all_to_all | solution.py:211
  31.6 8.3 %collective-permute-start.5 = (bf16[1,4,128,128]{3,2,1,0:T(8,128)(2,1)S(1)}, bf16[1,4,128,128]{3,2,1,0:T(8,128)(2,1)S(1)}, u32[]{:S(2)}, u32[]{:S(2)}) collective-permute-start(bf16[1,4,128,128]{3,2,1,0:T(8,128)(2,1)S(1)} %copy-done.3), channel_id=1, source_target_pairs={{32,0},{64,32},{96,64},{128,96},{160,128},{192,160},{224,192},{256... | collective-permute-start | bytes 393224 | tf_op jit(solution)/shard_map/ppermute | solution.py:16
  31.7 8.1 %collective-permute-start.4 = (bf16[1,4,128,128]{3,2,1,0:T(8,128)(2,1)S(1)}, bf16[1,4,128,128]{3,2,1,0:T(8,128)(2,1)S(1)}, u32[]{:S(2)}, u32[]{:S(2)}) collective-permute-start(bf16[1,4,128,128]{3,2,1,0:T(8,128)(2,1)S(1)} %copy-done.3), channel_id=1, source_target_pairs={{480,0},{0,32},{32,64},{64,96},{96,128},{128,160},{160,192},{192,2... | collective-permute-start | bytes 393224 | tf_op jit(solution)/shard_map/ppermute | solution.py:16
  32.2 7.7 %collective-permute-start.3 = (bf16[1,4,128,128]{3,2,1,0:T(8,128)(2,1)S(1)}, bf16[1,4,128,128]{3,2,1,0:T(8,128)(2,1)S(1)}, u32[]{:S(2)}, u32[]{:S(2)}) collective-permute-start(bf16[1,4,128,128]{3,2,1,0:T(8,128)(2,1)S(1)} %copy-done.3), channel_id=1, source_target_pairs={{448,0},{480,32},{0,64},{32,96},{64,128},{96,160},{128,192},{160,2... | collective-permute-start | bytes 393224 | tf_op jit(solution)/shard_map/ppermute | solution.py:16
  34.7 7.9 %collective-permute-start.6 = (bf16[1,4,128,128]{3,2,1,0:T(8,128)(2,1)S(1)}, bf16[1,4,128,128]{3,2,1,0:T(8,128)(2,1)S(1)}, u32[]{:S(2)}, u32[]{:S(2)}) collective-permute-start(bf16[1,4,128,128]{3,2,1,0:T(8,128)(2,1)S(1)} %copy-done.3), channel_id=1, source_target_pairs={{64,0},{96,32},{128,64},{160,96},{192,128},{224,160},{256,192},{28... | collective-permute-start | bytes 393224 | tf_op jit(solution)/shard_map/ppermute | solution.py:16
  128.2 102.1 %all-to-all-start.2 = ((bf16[32,16,32,128]{3,2,1,0:T(8,128)(2,1)}), bf16[32,16,32,128]{3,2,1,0:T(8,128)(2,1)}, u32[]{:S(2)}, u32[]{:S(2)}) async-start(bf16[32,16,32,128]{3,2,1,0:T(8,128)(2,1)} %bitcast.44), calls=%async_computation.2 | async-start | bytes 8388608 | tf_op jit(solution)/shard_map/all_to_all | solution.py:211
  133.6 32.7 %collective-permute-start = (bf16[256,768]{1,0:T(8,128)(2,1)S(1)}, bf16[256,768]{1,0:T(8,128)(2,1)S(1)}, u32[]{:S(2)}, u32[]{:S(2)}) collective-permute-start(bf16[256,768]{1,0:T(8,128)(2,1)S(1)} %bitcast.38), channel_id=1, source_target_pairs={{8,0},{9,1},{10,2},{11,3},{12,4},{13,5},{14,6},{15,7},{16,8},{17,9... | collective-permute-start | bytes 1179656 | tf_op jit(solution)/shard_map/ppermute | solution.py:23
  138.5 27.8 %collective-permute-start.2 = (bf16[256,512]{1,0:T(8,128)(2,1)S(1)}, bf16[256,512]{1,0:T(8,128)(2,1)S(1)}, u32[]{:S(2)}, u32[]{:S(2)}) collective-permute-start(bf16[256,512]{1,0:T(8,128)(2,1)S(1)} %slice.3), channel_id=1, source_target_pairs={{24,0},{25,1},{26,2},{27,3},{28,4},{29,5},{30,6},{31,7},{0,8},{1,9... | collective-permute-start | bytes 786440 | tf_op jit(solution)/shard_map/ppermute | solution.py:23
  140.4 25.8 %collective-permute-start.1 = (bf16[256,512]{1,0:T(8,128)(2,1)S(1)}, bf16[256,512]{1,0:T(8,128)(2,1)S(1)}, u32[]{:S(2)}, u32[]{:S(2)}) collective-permute-start(bf16[256,512]{1,0:T(8,128)(2,1)S(1)} %slice.3), channel_id=1, source_target_pairs={{16,0},{17,1},{18,2},{19,3},{20,4},{21,5},{22,6},{23,7},{24,8},{25... | collective-permute-start | bytes 786440 | tf_op jit(solution)/shard_map/ppermute | solution.py:23
  168.9 1.1 copy-start.1

commit v6 on v4

--- a/solution.py
+++ b/solution.py
@@ -75,7 +75,7 @@
     count = len(metric_refs)
     share = parts // count
     block = share * depth
-    my_x = me_ref[0] // share
+    my_x, my_z = me_ref[0] // share, lax.rem(me_ref[0], share)
     columns = []
     for k in range(count):
         place = lax.rem(my_x + k, count)
@@ -93,12 +93,9 @@
                 columns[p], right, (((1,), (1 if stored else 0,)), ((), ())),
                 preferred_element_type=jnp.float32,
             )
-        total = total.astype(out_ref.dtype)
-        place = lax.rem(my_x + q, count)
+        total = pltpu.roll(total, lax.rem(block - depth * my_z, block), 1).astype(out_ref.dtype)
         for w in range(width):
-            out_ref[w, :, pl.ds(pl.multiple_of(place * block, block), block)] = (
-                total[w * cols:(w + 1) * cols]
-            )
+            out_ref[w, :, q * block:(q + 1) * block] = total[w * cols:(w + 1) * cols]
 
 
 def fit(metric_parts, me, ints):
@@ -118,7 +115,7 @@
             ],
             out_specs=pl.BlockSpec((width, cols, rows), lambda i, me: (i, 0, 0)),
         ),
-        compiler_params=pltpu.CompilerParams(vmem_limit_bytes=24 << 20),
+        compiler_params=pltpu.CompilerParams(vmem_limit_bytes=12 << 20),
         cost_estimate=pl.CostEstimate(
             flops=2 * rows * rows * slots * cols,
             bytes_accessed=2 * rows * rows + 4 * rows * slots * cols,
@@ -127,18 +124,70 @@
     )(me, *metric_parts, ints)
 
 
-def close_kernel(fitted_ref, half_ref, out_ref, total_ref):
+def spread_kernel(me_ref, half_ref, *out_refs):
+    group, slots = len(out_refs), out_refs[0].shape[0]
+    z_len = group // X_LEN
+    my_x, my_z = me_ref[0] // z_len, lax.rem(me_ref[0], z_len)
+    for k, out_ref in enumerate(out_refs):
+        dx, dz = k // z_len, k % z_len
+        owner_x = lax.rem(my_x + X_LEN - dx, X_LEN)
+        owner = owner_x * z_len + lax.rem(my_z + z_len - dz, z_len)
+        tile = half_ref[:, pl.ds(pl.multiple_of(owner * slots, slots), slots), :]
+        out_ref[...] = jnp.swapaxes(tile, 0, 1)
+
+
+def spread(half, me):
+    group = lax.axis_size("aux")
+    count, slots, cols = half.shape
+    piece = jax.ShapeDtypeStruct((slots // group, count, cols), half.dtype)
+    return pl.pallas_call(
+        spread_kernel,
+        out_shape=[piece] * group,
+        in_specs=[
+            pl.BlockSpec(memory_space=pltpu.SMEM),
+            pl.BlockSpec(memory_space=pltpu.VMEM),
+        ],
+        out_specs=[pl.BlockSpec(memory_space=pltpu.VMEM)] * group,
+        compiler_params=pltpu.CompilerParams(vmem_limit_bytes=16 << 20),
+        cost_estimate=pl.CostEstimate(
+            flops=0, bytes_accessed=4 * half.size, transcendentals=0,
+        ),
+    )(me, half)
+
+
+def moved(pieces):
+    z_len = len(pieces) // X_LEN
+    grid = [(x, z) for x in range(X_LEN) for z in range(z_len)]
+    out = list(pieces)
+    for dz in sorted(range(z_len), key=lambda dz: (-min(dz, z_len - dz), dz)):
+        for dx in range(X_LEN):
+            k = dx * z_len + dz
+            if k:
+                route = [
+                    ((x + dx) % X_LEN * z_len + (z + dz) % z_len, x * z_len + z)
+                    for x, z in grid
+                ]
+                out[k] = lax.ppermute(pieces[k], "aux", route)
+    return out
+
+
+def close_kernel(fitted_ref, *refs):
+    *half_refs, out_ref, total_ref = refs
     step = pl.program_id(0)
-    parts, width, depth, cols = half_ref.shape
+    width, cols, _ = fitted_ref.shape
 
     @pl.when(step == 0)
     def _():
         total_ref[...] = jnp.zeros_like(total_ref)
 
     total = total_ref[...]
-    for w in range(width):
-        right = half_ref[:, w].reshape(parts * depth, cols)
-        total += jnp.dot(fitted_ref[w], right, preferred_element_type=jnp.float32)
+    for w in range(0, width, 2):
+        left = jnp.concatenate([fitted_ref[w], fitted_ref[w + 1]], axis=0)
+        right = jnp.concatenate([
+            jnp.concatenate([ref[v] for ref in half_refs], axis=0) for v in (w, w + 1)
+        ], axis=1)
+        pair = jnp.dot(left, right, preferred_element_type=jnp.float32)
+        total += pair[:cols, :cols] + pair[cols:, cols:]
     total_ref[...] = total
 
     @pl.when(step == pl.num_programs(0) - 1)
@@ -148,27 +197,26 @@
             out_ref[k] = done
 
 
-def close(fitted, half):
-    parts, slots, depth, cols = half.shape
-    width = 2
-    rows = parts * depth
+def close(fitted, pieces):
+    slots, depth, cols = pieces[0].shape
+    rows = fitted.shape[2]
+    width = 4
     return pl.pallas_call(
         close_kernel,
         out_shape=jax.ShapeDtypeStruct((X_LEN, cols, cols), jnp.float32),
         grid=(slots // width,),
-        in_specs=[
-            pl.BlockSpec((width, cols, rows), lambda i: (i, 0, 0)),
-            pl.BlockSpec((parts, width, depth, cols), lambda i: (0, i, 0, 0)),
+        in_specs=[pl.BlockSpec((width, cols, rows), lambda i: (i, 0, 0))] + [
+            pl.BlockSpec((width, depth, cols), lambda i: (i, 0, 0)) for _ in pieces
         ],
         out_specs=pl.BlockSpec((X_LEN, cols, cols), lambda i: (0, 0, 0)),
         scratch_shapes=[pltpu.VMEM((cols, cols), jnp.float32)],
-        compiler_params=pltpu.CompilerParams(vmem_limit_bytes=24 << 20),
+        compiler_params=pltpu.CompilerParams(vmem_limit_bytes=12 << 20),
         cost_estimate=pl.CostEstimate(
             flops=2 * rows * slots * cols * cols,
             bytes_accessed=4 * rows * slots * cols,
             transcendentals=0,
         ),
-    )(*(pltpu.with_memory_space_constraint(x, pltpu.HBM) for x in (fitted, half)))
+    )(fitted, *pieces)
 
 
 def local_density(density, dens_cols, neighbours):
@@ -214,12 +262,15 @@
     parts = [line, from_x(line, -1), from_x(short, 2), from_x(short, 1)]
     dense = local_density(density, dens_cols, neighbours)
     half = jnp.einsum("ls,plm->psm", dense, ints, preferred_element_type=jnp.float32)
-    half_moved = exchanged(by_slot(half.astype(jnp.bfloat16)))
-    fitted = fit(parts, me, ints_moved)
-    shares = close(fitted, half_moved)
-    shares = jnp.sum(to_all(shares, "x"), axis=0)
+    pieces = spread(half.astype(jnp.bfloat16), me)
+    pieces = moved(pieces)
+    first = jnp.sum(jnp.arange(1, lax.axis_size("aux")) <= me[0], dtype=jnp.int32)[None]
+    fitted = fit(parts, first, ints_moved)
+    shares = close(fitted, pieces)
+    shares = jnp.sum(to_all(shares, "x"), axis=0).astype(jnp.bfloat16)
     shares = jnp.broadcast_to(shares[None], (z_len, cols, cols))
-    return jnp.sum(to_all(shares, "z"), axis=0)[None]
+    shares = to_all(shares, "z").astype(jnp.float32)
+    return jnp.sum(shares, axis=0)[None]
 
 
 def solution(mesh):

time: 268 us -> 321 us (1.20)
  the two profiles are of different devices: /device:TPU:32 before, /device:TPU:56 now
where the time goes in v6:
time: 321 us; the launch traced here: 319 us
  starting transfers between devices  214 us (67%)
  waiting for transfers between devices  37.4 us (12%)
  blocking collectives  28.5 us (9%)
  local copies, waits for them, and re-layouts  16.4 us (5%)
  Pallas kernels  15.2 us (5%)
  matrix products  5.12 us (2%)
    ppermute x31, starting transfers between devices, moved(): out[k] = lax.ppermute(pieces[k], 'aux', route)  142 us
    ppermute x4, starting transfers between devices, passed_along(): return lax.ppermute(block, axis, route)  47.2 us
    all_to_all x2, blocking collectives, to_all(): lax.all_to_all(copies, 'aux', split_axis=0, concat_axis=0, tiled=True, ax...  28.5 us
    ppermute x31, waiting for transfers between devices, moved(): out[k] = lax.ppermute(pieces[k], 'aux', route)  23.9 us
    all_to_all x1, starting transfers between devices, to_all(): lax.all_to_all(copies, 'aux', split_axis=0, concat_axis=0, tiled=True, ax...  10.3 us
    ppermute x3, starting transfers between devices, from_x(): return lax.ppermute(block, 'aux', route)  9.87 us
    pallas_call x1, Pallas kernels, fit(): pl.pallas_call(fit_kernel, out_shape=jax.ShapeDtypeStruct((slots, cols, r...  9.23 us
    unnamed x37, local copies, waits for them, and re-layouts  8.02 us
  transfers between devices with their start and end apart: 40, of which 5 were waited for; matrix products, arithmetic and copies ran while one was open for 5% of the time, Pallas kernels for 4%

profile of v6, /device:TPU:56, one launch (start us, length us, event | category | flops | bytes accessed | tf_op | source)
XLA Modules:
  0.0 319.0 jit_solution(177947696758835893)
XLA Ops:
  1.6 10.3 %all-to-all-start = ((bf16[8,32,768]{2,1,0:T(8,128)(2,1)}), bf16[8,32,768]{2,1,0:T(8,128)(2,1)S(1)}, u32[]{:S(2)}, u32[]{:S(2)}) async-start(bf16[8,32,768]{2,1,0:T(8,128)(2,1)} %shard_map.55), calls=%async_computation | async-start | bytes 786432 | tf_op jit(solution)/shard_map/all_to_all | solution.py:33
  11.9 6.9 %copy.10 = bf16[512,32,128]{2,1,0:T(8,128)(2,1)} copy(bf16[512,32,128]{2,0,1:T(8,128)(2,1)} %bitcast.45) | data formatting | bytes 8388608 | tf_op jit(solution)/shard_map/transpose | solution.py:244
  18.8 7.8 %all-to-all-done = bf16[8,32,768]{2,1,0:T(8,128)(2,1)S(1)} async-done(((bf16[8,32,768]{2,1,0:T(8,128)(2,1)}), bf16[8,32,768]{2,1,0:T(8,128)(2,1)S(1)}, u32[]{:S(2)}, u32[]{:S(2)}) %all-to-all-start) | async-done | bytes 393248 | tf_op jit(solution)/shard_map/all_to_all | solution.py:33
  26.6 5.0 %all-to-all-start.1 = ((bf16[32,16,32,128]{3,2,1,0:T(8,128)(2,1)}), bf16[32,16,32,128]{3,2,1,0:T(8,128)(2,1)}, u32[]{:S(2)}, u32[]{:S(2)}) async-start(bf16[32,16,32,128]{3,2,1,0:T(8,128)(2,1)} %bitcast.44), calls=%async_computation.1 | async-start | bytes 8388608 | tf_op jit(solution)/shard_map/all_to_all | solution.py:248
  31.6 14.7 %collective-permute-start.3 = (bf16[1,4,128,128]{3,2,1,0:T(8,128)(2,1)S(1)}, bf16[1,4,128,128]{3,2,1,0:T(8,128)(2,1)S(1)}, u32[]{:S(2)}, u32[]{:S(2)}) collective-permute-start(bf16[1,4,128,128]{3,2,1,0:T(8,128)(2,1)S(1)} %copy-done.14), channel_id=1, source_target_pairs={{448,0},{480,32},{0,64},{32,96},{64,128},{96,160},{128,192},{160,2... | collective-permute-start | bytes 393224 | tf_op jit(solution)/shard_map/ppermute | solution.py:16
  46.5 15.7 %collective-permute-start.5 = (bf16[1,4,128,128]{3,2,1,0:T(8,128)(2,1)S(1)}, bf16[1,4,128,128]{3,2,1,0:T(8,128)(2,1)S(1)}, u32[]{:S(2)}, u32[]{:S(2)}) collective-permute-start(bf16[1,4,128,128]{3,2,1,0:T(8,128)(2,1)S(1)} %copy-done.14), channel_id=1, source_target_pairs={{32,0},{64,32},{96,64},{128,96},{160,128},{192,160},{224,192},{256... | collective-permute-start | bytes 393224 | tf_op jit(solution)/shard_map/ppermute | solution.py:16
  62.1 16.7 %collective-permute-start.6 = (bf16[1,4,128,128]{3,2,1,0:T(8,128)(2,1)S(1)}, bf16[1,4,128,128]{3,2,1,0:T(8,128)(2,1)S(1)}, u32[]{:S(2)}, u32[]{:S(2)}) collective-permute-start(bf16[1,4,128,128]{3,2,1,0:T(8,128)(2,1)S(1)} %copy-done.14), channel_id=1, source_target_pairs={{64,0},{96,32},{128,64},{160,96},{192,128},{224,160},{256,192},{28... | collective-permute-start | bytes 393224 | tf_op jit(solution)/shard_map/ppermute | solution.py:16
  80.0 5.7 %collective-permute-done.6 = bf16[1,4,128,128]{3,2,1,0:T(8,128)(2,1)S(1)} collective-permute-done((bf16[1,4,128,128]{3,2,1,0:T(8,128)(2,1)S(1)}, bf16[1,4,128,128]{3,2,1,0:T(8,128)(2,1)S(1)}, u32[]{:S(2)}, u32[]{:S(2)}) %collective-permute-start.6) | collective-permute-done | bytes 131104 | tf_op jit(solution)/shard_map/ppermute | solution.py:16
  87.0 4.6 %convert_bitcast_fusion.half_ref = bf16[32,512,128]{2,1,0:T(8,128)(2,1)S(1)} fusion(bf16[1,32,512,128]{3,2,1,0:T(8,128)(2,1)} %param.5, bf16[64,8,4,128]{3,2,1,0:T(4,128)(2,1)S(1)} %bitcast.46), kind=kOutput, calls=%fused_computation.4 | convolution fusion | flops 2149580800 | bytes 8912896 | tf_op jit(solution)/shard_map/ls,plm->psm/dot_general | solution.py:264
  91.6 2.0 shard_map.57
  93.5 5.4 %collective-permute-start.7 = (bf16[16,32,128]{2,1,0:T(8,128)(2,1)S(1)}, bf16[16,32,128]{2,1,0:T(8,128)(2,1)S(1)}, u32[]{:S(2)}, u32[]{:S(2)}) collective-permute-start(bf16[16,32,128]{2,1,0:T(8,128)(2,1)S(1)} %get-tuple-element.42), channel_id=1, source_target_pairs={{1,0},{2,1},{3,2},{4,3},{5,4},{6,5},{7,6},{0,7},{9,8},{10,9},{11,1... | collective-permute-start | bytes 393224 | tf_op jit(solution)/shard_map/ppermute | solution.py:170
  99.0 3.2 %collective-permute-start.8 = (bf16[16,32,128]{2,1,0:T(8,128)(2,1)S(1)}, bf16[16,32,128]{2,1,0:T(8,128)(2,1)S(1)}, u32[]{:S(2)}, u32[]{:S(2)}) collective-permute-start(bf16[16,32,128]{2,1,0:T(8,128)(2,1)S(1)} %get-tuple-element.43), channel_id=1, source_target_pairs={{2,0},{3,1},{4,2},{5,3},{6,4},{7,5},{0,6},{1,7},{10,8},{11,9},{12,... | collective-permute-start | bytes 393224 | tf_op jit(solution)/shard_map/ppermute | solution.py:170
  102.2 2.3 collective-permute-start.9
  104.5 7.1 %collective-permute-start.10 = (bf16[16,32,128]{2,1,0:T(8,128)(2,1)S(1)}, bf16[16,32,128]{2,1,0:T(8,128)(2,1)S(1)}, u32[]{:S(2)}, u32[]{:S(2)}) collective-permute-start(bf16[16,32,128]{2,1,0:T(8,128)(2,1)S(1)} %get-tuple-element.45), channel_id=1, source_target_pairs={{4,0},{5,1},{6,2},{7,3},{0,4},{1,5},{2,6},{3,7},{12,8},{13,9},{14,... | collective-permute-start | bytes 393224 | tf_op jit(solution)/shard_map/ppermute | solution.py:170
  111.6 1.9 collective-permute-start.11
  113.5 13.6 %collective-permute-done.7.refs_1_ = bf16[16,32,128]{2,1,0:T(8,128)(2,1)S(1)} collective-permute-done((bf16[16,32,128]{2,1,0:T(8,128)(2,1)S(1)}, bf16[16,32,128]{2,1,0:T(8,128)(2,1)S(1)}, u32[]{:S(2)}, u32[]{:S(2)}) %collective-permute-start.7) | collective-permute-done | bytes 131104 | tf_op jit(solution)/shard_map/ppermute | solution.py:170
  127.1 4.7 %collective-permute-start.12 = (bf16[16,32,128]{2,1,0:T(8,128)(2,1)S(1)}, bf16[16,32,128]{2,1,0:T(8,128)(2,1)S(1)}, u32[]{:S(2)}, u32[]{:S(2)}) collective-permute-start(bf16[16,32,128]{2,1,0:T(8,128)(2,1)S(1)} %get-tuple-element.47), channel_id=1, source_target_pairs={{6,0},{7,1},{0,2},{1,3},{2,4},{3,5},{4,6},{5,7},{14,8},{15,9},{8,1... | collective-permute-start | bytes 393224 | tf_op jit(solution)/shard_map/ppermute | solution.py:170
  131.9 3.2 collective-permute-done.8.refs_2_
  135.0 2.4 collective-permute-start.13
  137.5 7.0 %collective-permute-done.9.refs_3_ = bf16[16,32,128]{2,1,0:T(8,128)(2,1)S(1)} collective-permute-done((bf16[16,32,128]{2,1,0:T(8,128)(2,1)S(1)}, bf16[16,32,128]{2,1,0:T(8,128)(2,1)S(1)}, u32[]{:S(2)}, u32[]{:S(2)}) %collective-permute-start.9) | collective-permute-done | bytes 131104 | tf_op jit(solution)/shard_map/ppermute | solution.py:170
  144.5 5.2 %collective-permute-start.14 = (bf16[16,32,128]{2,1,0:T(8,128)(2,1)S(1)}, bf16[16,32,128]{2,1,0:T(8,128)(2,1)S(1)}, u32[]{:S(2)}, u32[]{:S(2)}) collective-permute-start(bf16[16,32,128]{2,1,0:T(8,128)(2,1)S(1)} %get-tuple-element.49), channel_id=1, source_target_pairs={{8,0},{9,1},{10,2},{11,3},{12,4},{13,5},{14,6},{15,7},{16,8},{17,9... | collective-permute-start | bytes 393224 | tf_op jit(solution)/shard_map/ppermute | solution.py:170
  149.7 4.5 %collective-permute-start.15 = (bf16[16,32,128]{2,1,0:T(8,128)(2,1)S(1)}, bf16[16,32,128]{2,1,0:T(8,128)(2,1)S(1)}, u32[]{:S(2)}, u32[]{:S(2)}) collective-permute-start(bf16[16,32,128]{2,1,0:T(8,128)(2,1)S(1)} %get-tuple-element.50), channel_id=1, source_target_pairs={{9,0},{10,1},{11,2},{12,3},{13,4},{14,5},{15,6},{8,7},{17,8},{18,9... | collective-permute-start | bytes 393224 | tf_op jit(solution)/shard_map/ppermute | solution.py:170
  154.2 2.6 collective-permute-start.16
  156.8 6.9 %collective-permute-start.17 = (bf16[16,32,128]{2,1,0:T(8,128)(2,1)S(1)}, bf16[16,32,128]{2,1,0:T(8,128)(2,1)S(1)}, u32[]{:S(2)}, u32[]{:S(2)}) collective-permute-start(bf16[16,32,128]{2,1,0:T(8,128)(2,1)S(1)} %get-tuple-element.52), channel_id=1, source_target_pairs={{11,0},{12,1},{13,2},{14,3},{15,4},{8,5},{9,6},{10,7},{19,8},{20,9... | collective-permute-start | bytes 393224 | tf_op jit(solution)/shard_map/ppermute | solution.py:170
  163.7 5.8 %collective-permute-start.18 = (bf16[16,32,128]{2,1,0:T(8,128)(2,1)S(1)}, bf16[16,32,128]{2,1,0:T(8,128)(2,1)S(1)}, u32[]{:S(2)}, u32[]{:S(2)}) collective-permute-start(bf16[16,32,128]{2,1,0:T(8,128)(2,1)S(1)} %get-tuple-element.53), channel_id=1, source_target_pairs={{12,0},{13,1},{14,2},{15,3},{8,4},{9,5},{10,6},{11,7},{20,8},{21,9... | collective-permute-start | bytes 393224 | tf_op jit(solution)/shard_map/ppermute | solution.py:170
  169.5 4.8 %collective-permute-start.19 = (bf16[16,32,128]{2,1,0:T(8,128)(2,1)S(1)}, bf16[16,32,128]{2,1,0:T(8,128)(2,1)S(1)}, u32[]{:S(2)}, u32[]{:S(2)}) collective-permute-start(bf16[16,32,128]{2,1,0:T(8,128)(2,1)S(1)} %get-tuple-element.54), channel_id=1, source_target_pairs={{13,0},{14,1},{15,2},{8,3},{9,4},{10,5},{11,6},{12,7},{21,8},{22,9... | collective-permute-start | bytes 393224 | tf_op jit(solution)/shard_map/ppermute | solution.py:170
  174.3 5.5 %collective-permute-start.20 = (bf16[16,32,128]{2,1,0:T(8,128)(2,1)S(1)}, bf16[16,32,128]{2,1,0:T(8,128)(2,1)S(1)}, u32[]{:S(2)}, u32[]{:S(2)}) collective-permute-start(bf16[16,32,128]{2,1,0:T(8,128)(2,1)S(1)} %get-tuple-element.55), channel_id=1, source_target_pairs={{14,0},{15,1},{8,2},{9,3},{10,4},{11,5},{12,6},{13,7},{22,8},{23,9... | collective-permute-start | bytes 393224 | tf_op jit(solution)/shard_map/ppermute | solution.py:170
  179.8 1.9 collective-permute-start.21
  181.7 5.4 %collective-permute-start.22 = (bf16[16,32,128]{2,1,0:T(8,128)(2,1)S(1)}, bf16[16,32,128]{2,1,0:T(8,128)(2,1)S(1)}, u32[]{:S(2)}, u32[]{:S(2)}) collective-permute-start(bf16[16,32,128]{2,1,0:T(8,128)(2,1)S(1)} %get-tuple-element.57), channel_id=1, source_target_pairs={{16,0},{17,1},{18,2},{19,3},{20,4},{21,5},{22,6},{23,7},{24,8},{25... | collective-permute-start | bytes 393224 | tf_op jit(solution)/shard_map/ppermute | solution.py:170
  187.2 4.9 %collective-permute-start.23 = (bf16[16,32,128]{2,1,0:T(8,128)(2,1)S(1)}, bf16[16,32,128]{2,1,0:T(8,128)(2,1)S(1)}, u32[]{:S(2)}, u32[]{:S(2)}) collective-permute-start(bf16[16,32,128]{2,1,0:T(8,128)(2,1)S(1)} %get-tuple-element.58), channel_id=1, source_target_pairs={{17,0},{18,1},{19,2},{20,3},{21,4},{22,5},{23,6},{16,7},{25,8},{26... | collective-permute-start | bytes 393224 | tf_op jit(solution)/shard_map/ppermute | solution.py:170
  192.1 3.3 %collective-permute-start.24 = (bf16[16,32,128]{2,1,0:T(8,128)(2,1)S(1)}, bf16[16,32,128]{2,1,0:T(8,128)(2,1)S(1)}, u32[]{:S(2)}, u32[]{:S(2)}) collective-permute-start(bf16[16,32,128]{2,1,0:T(8,128)(2,1)S(1)} %get-tuple-element.59), channel_id=1, source_target_pairs={{18,0},{19,1},{20,2},{21,3},{22,4},{23,5},{16,6},{17,7},{26,8},{27... | collective-permute-start | bytes 393224 | tf_op jit(solution)/shard_map/ppermute | solution.py:170
  195.4 4.1 %collective-permute-start.25 = (bf16[16,32,128]{2,1,0:T(8,128)(2,1)S(1)}, bf16[16,32,128]{2,1,0:T(8,128)(2,1)S(1)}, u32[]{:S(2)}, u32[]{:S(2)}) collective-permute-start(bf16[16,32,128]{2,1,0:T(8,128)(2,1)S(1)} %get-tuple-element.60), channel_id=1, source_target_pairs={{19,0},{20,1},{21,2},{22,3},{23,4},{16,5},{17,6},{18,7},{27,8},{28... | collective-permute-start | bytes 393224 | tf_op jit(solution)/shard_map/ppermute | solution.py:170
  199.5 9.3 %collective-permute-start.26 = (bf16[16,32,128]{2,1,0:T(8,128)(2,1)S(1)}, bf16[16,32,128]{2,1,0:T(8,128)(2,1)S(1)}, u32[]{:S(2)}, u32[]{:S(2)}) collective-permute-start(bf16[16,32,128]{2,1,0:T(8,128)(2,1)S(1)} %get-tuple-element.61), channel_id=1, source_target_pairs={{20,0},{21,1},{22,2},{23,3},{16,4},{17,5},{18,6},{19,7},{28,8},{29... | collective-permute-start | bytes 393224 | tf_op jit(solution)/shard_map/ppermute | solution.py:170
  208.8 1.9 collective-permute-start.27
  210.8 6.3 %collective-permute-start.28 = (bf16[16,32,128]{2,1,0:T(8,128)(2,1)S(1)}, bf16[16,32,128]{2,1,0:T(8,128)(2,1)S(1)}, u32[]{:S(2)}, u32[]{:S(2)}) collective-permute-start(bf16[16,32,128]{2,1,0:T(8,128)(2,1)S(1)} %get-tuple-element.63), channel_id=1, source_target_pairs={{22,0},{23,1},{16,2},{17,3},{18,4},{19,5},{20,6},{21,7},{30,8},{31... | collective-permute-start | bytes 393224 | tf_op jit(solution)/shard_map/ppermute | solution.py:170
  217.1 3.1 collective-permute-start
  220.2 2.2 collective-permute-start.29
  222.5 3.3 %collective-permute-start.30 = (bf16[16,32,128]{2,1,0:T(8,128)(2,1)S(1)}, bf16[16,32,128]{2,1,0:T(8,128)(2,1)S(1)}, u32[]{:S(2)}, u32[]{:S(2)}) collective-permute-start(bf16[16,32,128]{2,1,0:T(8,128)(2,1)S(1)} %get-tuple-element.65), channel_id=1, source_target_pairs={{24,0},{25,1},{26,2},{27,3},{28,4},{29,5},{30,6},{31,7},{0,8},{1,9... | collective-permute-start | bytes 393224 | tf_op jit(solution)/shard_map/ppermute | solution.py:170
  225.8 4.9 %collective-permute-start.1 = (bf16[256,512]{1,0:T(8,128)(2,1)S(1)}, bf16[256,512]{1,0:T(8,128)(2,1)S(1)}, u32[]{:S(2)}, u32[]{:S(2)}) collective-permute-start(bf16[256,512]{1,0:T(8,128)(2,1)S(1)} %slice.3), channel_id=1, source_target_pairs={{16,0},{17,1},{18,2},{19,3},{20,4},{21,5},{22,6},{23,7},{24,8},{25... | collective-permute-start | bytes 786440 | tf_op jit(solution)/shard_map/ppermute | solution.py:23
  232.6 4.3 %collective-permute-start.31 = (bf16[16,32,128]{2,1,0:T(8,128)(2,1)S(1)}, bf16[16,32,128]{2,1,0:T(8,128)(2,1)S(1)}, u32[]{:S(2)}, u32[]{:S(2)}) collective-permute-start(bf16[16,32,128]{2,1,0:T(8,128)(2,1)S(1)} %get-tuple-element.66), channel_id=1, source_target_pairs={{25,0},{26,1},{27,2},{28,3},{29,4},{30,5},{31,6},{24,7},{1,8},{2,9... | collective-permute-start | bytes 393224 | tf_op jit(solution)/shard_map/ppermute | solution.py:170
  237.6 5.7 %collective-permute-start.32 = (bf16[16,32,128]{2,1,0:T(8,128)(2,1)S(1)}, bf16[16,32,128]{2,1,0:T(8,128)(2,1)S(1)}, u32[]{:S(2)}, u32[]{:S(2)}) collective-permute-start(bf16[16,32,128]{2,1,0:T(8,128)(2,1)S(1)} %get-tuple-element.67), channel_id=1, source_target_pairs={{26,0},{27,1},{28,2},{29,3},{30,4},{31,5},{24,6},{25,7},{2,8},{3,9... | collective-permute-start | bytes 393224 | tf_op jit(solution)/shard_map/ppermute | solution.py:170
  244.7 7.6 %collective-permute-start.33 = (bf16[16,32,128]{2,1,0:T(8,128)(2,1)}, bf16[16,32,128]{2,1,0:T(8,128)(2,1)}, u32[]{:S(2)}, u32[]{:S(2)}) collective-permute-start(bf16[16,32,128]{2,1,0:T(8,128)(2,1)} %get-tuple-element.68), channel_id=1, source_target_pairs={{27,0},{28,1},{29,2},{30,3},{31,4},{24,5},{25,6},{26,7},{3,8},{4,9... | collective-permute-start | bytes 393224 | tf_op jit(solution)/shard_map/ppermute | solution.py:170
  252.9 4.7 %collective-permute-start.34 = (bf16[16,32,128]{2,1,0:T(8,128)(2,1)}, bf16[16,32,128]{2,1,0:T(8,128)(2,1)}, u32[]{:S(2)}, u32[]{:S(2)}) collective-permute-start(bf16[16,32,128]{2,1,0:T(8,128)(2,1)} %get-tuple-element.69), channel_id=1, source_target_pairs={{28,0},{29,1},{30,2},{31,3},{24,4},{25,5},{26,6},{27,7},{4,8},{5,9... | collective-permute-start | bytes 393224 | tf_op jit(solution)/shard_map/ppermute | solution.py:170
  258.3 10.7 %collective-permute-start.35 = (bf16[16,32,128]{2,1,0:T(8,128)(2,1)}, bf16[16,32,128]{2,1,0:T(8,128)(2,1)}, u32[]{:S(2)}, u32[]{:S(2)}) collective-permute-start(bf16[16,32,128]{2,1,0:T(8,128)(2,1)} %get-tuple-element.70), channel_id=1, source_target_pairs={{29,0},{30,1},{31,2},{24,3},{25,4},{26,5},{27,6},{28,7},{5,8},{6,9... | collective-permute-start | bytes 393224 | tf_op jit(solution)/shard_map/ppermute | solution.py:170
  277.2 9.2 %shard_map.56.fitted_ref = bf16[16,128,1024]{2,1,0:T(8,128)(2,1)S(1)} custom-call(s32[1]{0:T(128)} %bitcast.me_ref, bf16[256,768]{1,0:T(8,128)(2,1)S(1)} %bitcast.42, bf16[256,768]{1,0:T(8,128)(2,1)S(1)} %copy-done.9, bf16[256,512]{1,0:T(8,128)(2,1)S(1)} %copy-done.11, bf16[256,512]{1,0:T(8,128)(2,1)S(1)} %copy-done.13, ...), custom_call_target="tpu_custom_call" | custom-call | flops 4294967296 | bytes 10485760 | tf_op jit(solution)/shard_map/pallas_call | solution.py:105
  286.6 3.3 %shard_map.58 = f32[4,128,128]{2,1,0:T(8,128)S(1)} custom-call(bf16[16,128,1024]{2,1,0:T(8,128)(2,1)S(1)} %shard_map.56.fitted_ref, bf16[16,32,128]{2,1,0:T(8,128)(2,1)S(1)} %get-tuple-element.41.refs_0_, bf16[16,32,128]{2,1,0:T(8,128)(2,1)S(1)} %collective-permute-done.7.refs_1_, bf16[16,32,128]{2,1,0:T(8,128)(2,1)S(1)} %collective-permute-done.8.refs_2_, ...), custom_call_target="tpu_custom_call" | custom-call | flops 536870912 | bytes 8388608 | tf_op jit(solution)/shard_map/pallas_call | solution.py:204
  289.8 11.0 %all_to_all.20 = f32[4,128,128]{2,1,0:T(8,128)S(1)} all-to-all(f32[4,128,128]{2,1,0:T(8,128)S(1)} %shard_map.58), channel_id=1, replica_groups={{0,8,16,24},{1,9,17,25},{2,10,18,26},{3,11,19,27},{4,12,20,28},{5,13,21..., dimensions={0} | all-to-all | bytes 524288 | tf_op jit(solution)/shard_map/all_to_all | solution.py:33
  300.9 17.5 %all_to_all.21 = bf16[8,128,128]{2,1,0:T(8,128)(2,1)S(1)} all-to-all(bf16[8,128,128]{2,1,0:T(8,128)(2,1)S(1)} %broadcast_in_dim.38), channel_id=1, replica_groups={{0,1,2,3,4,5,6,7},{8,9,10,11,12,13,14,15},{16,17,18,19,20,21,22,23},{24..., dimensions={0} | all-to-all | bytes 524288 | tf_op jit(solution)/shard_map/all_to_all | solution.py:33
  (93 shorter events, 18.3 us)
Async XLA Ops:
  0.0 79.0 %copy-start = (s32[16,4]{0,1:T(4,128)S(1)}, s32[16,4]{0,1:T(4,128)}, u32[]{:S(2)}) copy-start(s32[16,4]{0,1:T(4,128)} %param.8) | copy-start | bytes 772
  1.6 25.0 %all-to-all-start = ((bf16[8,32,768]{2,1,0:T(8,128)(2,1)}), bf16[8,32,768]{2,1,0:T(8,128)(2,1)S(1)}, u32[]{:S(2)}, u32[]{:S(2)}) async-start(bf16[8,32,768]{2,1,0:T(8,128)(2,1)} %shard_map.55), calls=%async_computation | async-start | bytes 786432 | tf_op jit(solution)/shard_map/all_to_all | solution.py:33
  26.6 5.0 %copy-start.14 = (bf16[1,4,128,128]{3,2,1,0:T(8,128)(2,1)S(1)}, bf16[1,4,128,128]{3,2,1,0:T(8,128)(2,1)}, u32[]{:S(2)}) copy-start(bf16[1,4,128,128]{3,2,1,0:T(8,128)(2,1)} %param.6) | copy-start | bytes 393220
  26.6 52.3 %copy-start.15 = (s32[16,4]{0,1:T(4,128)S(1)}, s32[16,4]{0,1:T(4,128)}, u32[]{:S(2)}) copy-start(s32[16,4]{0,1:T(4,128)} %param.7) | copy-start | bytes 772
  26.6 247.7 %all-to-all-start.1 = ((bf16[32,16,32,128]{3,2,1,0:T(8,128)(2,1)}), bf16[32,16,32,128]{3,2,1,0:T(8,128)(2,1)}, u32[]{:S(2)}, u32[]{:S(2)}) async-start(bf16[32,16,32,128]{3,2,1,0:T(8,128)(2,1)} %bitcast.44), calls=%async_computation.1 | async-start | bytes 8388608 | tf_op jit(solution)/shard_map/all_to_all | solution.py:248
  31.6 48.2 %collective-permute-start.3 = (bf16[1,4,128,128]{3,2,1,0:T(8,128)(2,1)S(1)}, bf16[1,4,128,128]{3,2,1,0:T(8,128)(2,1)S(1)}, u32[]{:S(2)}, u32[]{:S(2)}) collective-permute-start(bf16[1,4,128,128]{3,2,1,0:T(8,128)(2,1)S(1)} %copy-done.14), channel_id=1, source_target_pairs={{448,0},{480,32},{0,64},{32,96},{64,128},{96,160},{128,192},{160,2... | collective-permute-start | bytes 393224 | tf_op jit(solution)/shard_map/ppermute | solution.py:16
  46.3 33.5 %collective-permute-start.4 = (bf16[1,4,128,128]{3,2,1,0:T(8,128)(2,1)S(1)}, bf16[1,4,128,128]{3,2,1,0:T(8,128)(2,1)S(1)}, u32[]{:S(2)}, u32[]{:S(2)}) collective-permute-start(bf16[1,4,128,128]{3,2,1,0:T(8,128)(2,1)S(1)} %copy-done.14), channel_id=1, source_target_pairs={{480,0},{0,32},{32,64},{64,96},{96,128},{128,160},{160,192},{192,2... | collective-permute-start | bytes 393224 | tf_op jit(solution)/shard_map/ppermute | solution.py:16
  46.5 33.5 %collective-permute-start.5 = (bf16[1,4,128,128]{3,2,1,0:T(8,128)(2,1)S(1)}, bf16[1,4,128,128]{3,2,1,0:T(8,128)(2,1)S(1)}, u32[]{:S(2)}, u32[]{:S(2)}) collective-permute-start(bf16[1,4,128,128]{3,2,1,0:T(8,128)(2,1)S(1)} %copy-done.14), channel_id=1, source_target_pairs={{32,0},{64,32},{96,64},{128,96},{160,128},{192,160},{224,192},{256... | collective-permute-start | bytes 393224 | tf_op jit(solution)/shard_map/ppermute | solution.py:16
  62.1 23.5 %collective-permute-start.6 = (bf16[1,4,128,128]{3,2,1,0:T(8,128)(2,1)S(1)}, bf16[1,4,128,128]{3,2,1,0:T(8,128)(2,1)S(1)}, u32[]{:S(2)}, u32[]{:S(2)}) collective-permute-start(bf16[1,4,128,128]{3,2,1,0:T(8,128)(2,1)S(1)} %copy-done.14), channel_id=1, source_target_pairs={{64,0},{96,32},{128,64},{160,96},{192,128},{224,160},{256,192},{28... | collective-permute-start | bytes 393224 | tf_op jit(solution)/shard_map/ppermute | solution.py:16
  93.5 33.6 %collective-permute-start.7 = (bf16[16,32,128]{2,1,0:T(8,128)(2,1)S(1)}, bf16[16,32,128]{2,1,0:T(8,128)(2,1)S(1)}, u32[]{:S(2)}, u32[]{:S(2)}) collective-permute-start(bf16[16,32,128]{2,1,0:T(8,128)(2,1)S(1)} %get-tuple-element.42), channel_id=1, source_target_pairs={{1,0},{2,1},{3,2},{4,3},{5,4},{6,5},{7,6},{0,7},{9,8},{10,9},{11,1... | collective-permute-start | bytes 393224 | tf_op jit(solution)/shard_map/ppermute | solution.py:170
  99.0 36.1 %collective-permute-start.8 = (bf16[16,32,128]{2,1,0:T(8,128)(2,1)S(1)}, bf16[16,32,128]{2,1,0:T(8,128)(2,1)S(1)}, u32[]{:S(2)}, u32[]{:S(2)}) collective-permute-start(bf16[16,32,128]{2,1,0:T(8,128)(2,1)S(1)} %get-tuple-element.43), channel_id=1, source_target_pairs={{2,0},{3,1},{4,2},{5,3},{6,4},{7,5},{0,6},{1,7},{10,8},{11,9},{12,... | collective-permute-start | bytes 393224 | tf_op jit(solution)/shard_map/ppermute | solution.py:170
  102.2 42.3 %collective-permute-start.9 = (bf16[16,32,128]{2,1,0:T(8,128)(2,1)S(1)}, bf16[16,32,128]{2,1,0:T(8,128)(2,1)S(1)}, u32[]{:S(2)}, u32[]{:S(2)}) collective-permute-start(bf16[16,32,128]{2,1,0:T(8,128)(2,1)S(1)} %get-tuple-element.44), channel_id=1, source_target_pairs={{3,0},{4,1},{5,2},{6,3},{7,4},{0,5},{1,6},{2,7},{11,8},{12,9},{13,... | collective-permute-start | bytes 393224 | tf_op jit(solution)/shard_map/ppermute | solution.py:170
  104.5 45.3 %collective-permute-start.10 = (bf16[16,32,128]{2,1,0:T(8,128)(2,1)S(1)}, bf16[16,32,128]{2,1,0:T(8,128)(2,1)S(1)}, u32[]{:S(2)}, u32[]{:S(2)}) collective-permute-start(bf16[16,32,128]{2,1,0:T(8,128)(2,1)S(1)} %get-tuple-element.45), channel_id=1, source_target_pairs={{4,0},{5,1},{6,2},{7,3},{0,4},{1,5},{2,6},{3,7},{12,8},{13,9},{14,... | collective-permute-start | bytes 393224 | tf_op jit(solution)/shard_map/ppermute | solution.py:170
  111.6 42.6 %collective-permute-start.11 = (bf16[16,32,128]{2,1,0:T(8,128)(2,1)S(1)}, bf16[16,32,128]{2,1,0:T(8,128)(2,1)S(1)}, u32[]{:S(2)}, u32[]{:S(2)}) collective-permute-start(bf16[16,32,128]{2,1,0:T(8,128)(2,1)S(1)} %get-tuple-element.46), channel_id=1, source_target_pairs={{5,0},{6,1},{7,2},{0,3},{1,4},{2,5},{3,6},{4,7},{13,8},{14,9},{15,... | collective-permute-start | bytes 393224 | tf_op jit(solution)/shard_map/ppermute | solution.py:170
  127.1 29.6 %collective-permute-start.12 = (bf16[16,32,128]{2,1,0:T(8,128)(2,1)S(1)}, bf16[16,32,128]{2,1,0:T(8,128)(2,1)S(1)}, u32[]{:S(2)}, u32[]{:S(2)}) collective-permute-start(bf16[16,32,128]{2,1,0:T(8,128)(2,1)S(1)} %get-tuple-element.47), channel_id=1, source_target_pairs={{6,0},{7,1},{0,2},{1,3},{2,4},{3,5},{4,6},{5,7},{14,8},{15,9},{8,1... | collective-permute-start | bytes 393224 | tf_op jit(solution)/shard_map/ppermute | solution.py:170
  135.0 28.6 %collective-permute-start.13 = (bf16[16,32,128]{2,1,0:T(8,128)(2,1)S(1)}, bf16[16,32,128]{2,1,0:T(8,128)(2,1)S(1)}, u32[]{:S(2)}, u32[]{:S(2)}) collective-permute-start(bf16[16,32,128]{2,1,0:T(8,128)(2,1)S(1)} %get-tuple-element.48), channel_id=1, source_target_pairs={{7,0},{0,1},{1,2},{2,3},{3,4},{4,5},{5,6},{6,7},{15,8},{8,9},{9,10... | collective-permute-start | bytes 393224 | tf_op jit(solution)/shard_map/ppermute | solution.py:170
  144.5 25.0 %collective-permute-start.14 = (bf16[16,32,128]{2,1,0:T(8,128)(2,1)S(1)}, bf16[16,32,128]{2,1,0:T(8,128)(2,1)S(1)}, u32[]{:S(2)}, u32[]{:S(2)}) collective-permute-start(bf16[16,32,128]{2,1,0:T(8,128)(2,1)S(1)} %get-tuple-element.49), channel_id=1, source_target_pairs={{8,0},{9,1},{10,2},{11,3},{12,4},{13,5},{14,6},{15,7},{16,8},{17,9... | collective-permute-start | bytes 393224 | tf_op jit(solution)/shard_map/ppermute | solution.py:170
  149.7 24.6 %collective-permute-start.15 = (bf16[16,32,128]{2,1,0:T(8,128)(2,1)S(1)}, bf16[16,32,128]{2,1,0:T(8,128)(2,1)S(1)}, u32[]{:S(2)}, u32[]{:S(2)}) collective-permute-start(bf16[16,32,128]{2,1,0:T(8,128)(2,1)S(1)} %get-tuple-element.50), channel_id=1, source_target_pairs={{9,0},{10,1},{11,2},{12,3},{13,4},{14,5},{15,6},{8,7},{17,8},{18,9... | collective-permute-start | bytes 393224 | tf_op jit(solution)/shard_map/ppermute | solution.py:170
  154.2 25.6 %collective-permute-start.16 = (bf16[16,32,128]{2,1,0:T(8,128)(2,1)S(1)}, bf16[16,32,128]{2,1,0:T(8,128)(2,1)S(1)}, u32[]{:S(2)}, u32[]{:S(2)}) collective-permute-start(bf16[16,32,128]{2,1,0:T(8,128)(2,1)S(1)} %get-tuple-element.51), channel_id=1, source_target_pairs={{10,0},{11,1},{12,2},{13,3},{14,4},{15,5},{8,6},{9,7},{18,8},{19,9... | collective-permute-start | bytes 393224 | tf_op jit(solution)/shard_map/ppermute | solution.py:170
  156.8 24.9 %collective-permute-start.17 = (bf16[16,32,128]{2,1,0:T(8,128)(2,1)S(1)}, bf16[16,32,128]{2,1,0:T(8,128)(2,1)S(1)}, u32[]{:S(2)}, u32[]{:S(2)}) collective-permute-start(bf16[16,32,128]{2,1,0:T(8,128)(2,1)S(1)} %get-tuple-element.52), channel_id=1, source_target_pairs={{11,0},{12,1},{13,2},{14,3},{15,4},{8,5},{9,6},{10,7},{19,8},{20,9... | collective-permute-start | bytes 393224 | tf_op jit(solution)/shard_map/ppermute | solution.py:170
  163.7 23.5 %collective-permute-start.18 = (bf16[16,32,128]{2,1,0:T(8,128)(2,1)S(1)}, bf16[16,32,128]{2,1,0:T(8,128)(2,1)S(1)}, u32[]{:S(2)}, u32[]{:S(2)}) collective-permute-start(bf16[16,32,128]{2,1,0:T(8,128)(2,1)S(1)} %get-tuple-element.53), channel_id=1, source_target_pairs={{12,0},{13,1},{14,2},{15,3},{8,4},{9,5},{10,6},{11,7},{20,8},{21,9... | collective-permute-start | bytes 393224 | tf_op jit(solution)/shard_map/ppermute | solution.py:170
  169.5 22.6 %collective-permute-start.19 = (bf16[16,32,128]{2,1,0:T(8,128)(2,1)S(1)}, bf16[16,32,128]{2,1,0:T(8,128)(2,1)S(1)}, u32[]{:S(2)}, u32[]{:S(2)}) collective-permute-start(bf16[16,32,128]{2,1,0:T(8,128)(2,1)S(1)} %get-tuple-element.54), channel_id=1, source_target_pairs={{13,0},{14,1},{15,2},{8,3},{9,4},{10,5},{11,6},{12,7},{21,8},{22,9... | collective-permute-start | bytes 393224 | tf_op jit(solution)/shard_map/ppermute | solution.py:170
  174.3 21.2 %collective-permute-start.20 = (bf16[16,32,128]{2,1,0:T(8,128)(2,1)S(1)}, bf16[16,32,128]{2,1,0:T(8,128)(2,1)S(1)}, u32[]{:S(2)}, u32[]{:S(2)}) collective-permute-start(bf16[16,32,128]{2,1,0:T(8,128)(2,1)S(1)} %get-tuple-element.55), channel_id=1, source_target_pairs={{14,0},{15,1},{8,2},{9,3},{10,4},{11,5},{12,6},{13,7},{22,8},{23,9... | collective-permute-start | bytes 393224 | tf_op jit(solution)/shard_map/ppermute | solution.py:170
  179.8 19.7 %collective-permute-start.21 = (bf16[16,32,128]{2,1,0:T(8,128)(2,1)S(1)}, bf16[16,32,128]{2,1,0:T(8,128)(2,1)S(1)}, u32[]{:S(2)}, u32[]{:S(2)}) collective-permute-start(bf16[16,32,128]{2,1,0:T(8,128)(2,1)S(1)} %get-tuple-element.56), channel_id=1, source_target_pairs={{15,0},{8,1},{9,2},{10,3},{11,4},{12,5},{13,6},{14,7},{23,8},{16,9... | collective-permute-start | bytes 393224 | tf_op jit(solution)/shard_map/ppermute | solution.py:170
  181.7 27.1 %collective-permute-start.22 = (bf16[16,32,128]{2,1,0:T(8,128)(2,1)S(1)}, bf16[16,32,128]{2,1,0:T(8,128)(2,1)S(1)}, u32[]{:S(2)}, u32[]{:S(2)}) collective-permute-start(bf16[16,32,128]{2,1,0:T(8,128)(2,1)S(1)} %get-tuple-element.57), channel_id=1, source_target_pairs={{16,0},{17,1},{18,2},{19,3},{20,4},{21,5},{22,6},{23,7},{24,8},{25... | collective-permute-start | bytes 393224 | tf_op jit(solution)/shard_map/ppermute | solution.py:170
  187.2 23.6 %collective-permute-start.23 = (bf16[16,32,128]{2,1,0:T(8,128)(2,1)S(1)}, bf16[16,32,128]{2,1,0:T(8,128)(2,1)S(1)}, u32[]{:S(2)}, u32[]{:S(2)}) collective-permute-start(bf16[16,32,128]{2,1,0:T(8,128)(2,1)S(1)} %get-tuple-element.58), channel_id=1, source_target_pairs={{17,0},{18,1},{19,2},{20,3},{21,4},{22,5},{23,6},{16,7},{25,8},{26... | collective-permute-start | bytes 393224 | tf_op jit(solution)/shard_map/ppermute | solution.py:170
  192.1 25.0 %collective-permute-start.24 = (bf16[16,32,128]{2,1,0:T(8,128)(2,1)S(1)}, bf16[16,32,128]{2,1,0:T(8,128)(2,1)S(1)}, u32[]{:S(2)}, u32[]{:S(2)}) collective-permute-start(bf16[16,32,128]{2,1,0:T(8,128)(2,1)S(1)} %get-tuple-element.59), channel_id=1, source_target_pairs={{18,0},{19,1},{20,2},{21,3},{22,4},{23,5},{16,6},{17,7},{26,8},{27... | collective-permute-start | bytes 393224 | tf_op jit(solution)/shard_map/ppermute | solution.py:170
  195.4 24.8 %collective-permute-start.25 = (bf16[16,32,128]{2,1,0:T(8,128)(2,1)S(1)}, bf16[16,32,128]{2,1,0:T(8,128)(2,1)S(1)}, u32[]{:S(2)}, u32[]{:S(2)}) collective-permute-start(bf16[16,32,128]{2,1,0:T(8,128)(2,1)S(1)} %get-tuple-element.60), channel_id=1, source_target_pairs={{19,0},{20,1},{21,2},{22,3},{23,4},{16,5},{17,6},{18,7},{27,8},{28... | collective-permute-start | bytes 393224 | tf_op jit(solution)/shard_map/ppermute | solution.py:170
  199.5 23.0 %collective-permute-start.26 = (bf16[16,32,128]{2,1,0:T(8,128)(2,1)S(1)}, bf16[16,32,128]{2,1,0:T(8,128)(2,1)S(1)}, u32[]{:S(2)}, u32[]{:S(2)}) collective-permute-start(bf16[16,32,128]{2,1,0:T(8,128)(2,1)S(1)} %get-tuple-element.61), channel_id=1, source_target_pairs={{20,0},{21,1},{22,2},{23,3},{16,4},{17,5},{18,6},{19,7},{28,8},{29... | collective-permute-start | bytes 393224 | tf_op jit(solution)/shard_map/ppermute | solution.py:170
  208.8 17.0 %collective-permute-start.27 = (bf16[16,32,128]{2,1,0:T(8,128)(2,1)S(1)}, bf16[16,32,128]{2,1,0:T(8,128)(2,1)S(1)}, u32[]{:S(2)}, u32[]{:S(2)}) collective-permute-start(bf16[16,32,128]{2,1,0:T(8,128)(2,1)S(1)} %get-tuple-element.62), channel_id=1, source_target_pairs={{21,0},{22,1},{23,2},{16,3},{17,4},{18,5},{19,6},{20,7},{29,8},{30... | collective-permute-start | bytes 393224 | tf_op jit(solution)/shard_map/ppermute | solution.py:170
  210.8 19.9 %collective-permute-start.28 = (bf16[16,32,128]{2,1,0:T(8,128)(2,1)S(1)}, bf16[16,32,128]{2,1,0:T(8,128)(2,1)S(1)}, u32[]{:S(2)}, u32[]{:S(2)}) collective-permute-start(bf16[16,32,128]{2,1,0:T(8,128)(2,1)S(1)} %get-tuple-element.63), channel_id=1, source_target_pairs={{22,0},{23,1},{16,2},{17,3},{18,4},{19,5},{20,6},{21,7},{30,8},{31... | collective-permute-start | bytes 393224 | tf_op jit(solution)/shard_map/ppermute | solution.py:170
  217.1 54.5 %collective-permute-start = (bf16[256,768]{1,0:T(8,128)(2,1)S(1)}, bf16[256,768]{1,0:T(8,128)(2,1)S(1)}, u32[]{:S(2)}, u32[]{:S(2)}) collective-permute-start(bf16[256,768]{1,0:T(8,128)(2,1)S(1)} %bitcast.40), channel_id=1, source_target_pairs={{8,0},{9,1},{10,2},{11,3},{12,4},{13,5},{14,6},{15,7},{16,8},{17,9... | collective-permute-start | bytes 1179656 | tf_op jit(solution)/shard_map/ppermute | solution.py:23
  220.2 12.4 %collective-permute-start.29 = (bf16[16,32,128]{2,1,0:T(8,128)(2,1)S(1)}, bf16[16,32,128]{2,1,0:T(8,128)(2,1)S(1)}, u32[]{:S(2)}, u32[]{:S(2)}) collective-permute-start(bf16[16,32,128]{2,1,0:T(8,128)(2,1)S(1)} %get-tuple-element.64), channel_id=1, source_target_pairs={{23,0},{16,1},{17,2},{18,3},{19,4},{20,5},{21,6},{22,7},{31,8},{24... | collective-permute-start | bytes 393224 | tf_op jit(solution)/shard_map/ppermute | solution.py:170
  222.5 14.5 %collective-permute-start.30 = (bf16[16,32,128]{2,1,0:T(8,128)(2,1)S(1)}, bf16[16,32,128]{2,1,0:T(8,128)(2,1)S(1)}, u32[]{:S(2)}, u32[]{:S(2)}) collective-permute-start(bf16[16,32,128]{2,1,0:T(8,128)(2,1)S(1)} %get-tuple-element.65), channel_id=1, source_target_pairs={{24,0},{25,1},{26,2},{27,3},{28,4},{29,5},{30,6},{31,7},{0,8},{1,9... | collective-permute-start | bytes 393224 | tf_op jit(solution)/shard_map/ppermute | solution.py:170
  225.8 31.7 %collective-permute-start.1 = (bf16[256,512]{1,0:T(8,128)(2,1)S(1)}, bf16[256,512]{1,0:T(8,128)(2,1)S(1)}, u32[]{:S(2)}, u32[]{:S(2)}) collective-permute-start(bf16[256,512]{1,0:T(8,128)(2,1)S(1)} %slice.3), channel_id=1, source_target_pairs={{16,0},{17,1},{18,2},{19,3},{20,4},{21,5},{22,6},{23,7},{24,8},{25... | collective-permute-start | bytes 786440 | tf_op jit(solution)/shard_map/ppermute | solution.py:23
  230.7 38.3 %collective-permute-start.2 = (bf16[256,512]{1,0:T(8,128)(2,1)S(1)}, bf16[256,512]{1,0:T(8,128)(2,1)S(1)}, u32[]{:S(2)}, u32[]{:S(2)}) collective-permute-start(bf16[256,512]{1,0:T(8,128)(2,1)S(1)} %slice.3), channel_id=1, source_target_pairs={{24,0},{25,1},{26,2},{27,3},{28,4},{29,5},{30,6},{31,7},{0,8},{1,9... | collective-permute-start | bytes 786440 | tf_op jit(solution)/shard_map/ppermute | solution.py:23
  232.6 11.3 %collective-permute-start.31 = (bf16[16,32,128]{2,1,0:T(8,128)(2,1)S(1)}, bf16[16,32,128]{2,1,0:T(8,128)(2,1)S(1)}, u32[]{:S(2)}, u32[]{:S(2)}) collective-permute-start(bf16[16,32,128]{2,1,0:T(8,128)(2,1)S(1)} %get-tuple-element.66), channel_id=1, source_target_pairs={{25,0},{26,1},{27,2},{28,3},{29,4},{30,5},{31,6},{24,7},{1,8},{2,9... | collective-permute-start | bytes 393224 | tf_op jit(solution)/shard_map/ppermute | solution.py:170
  237.6 14.6 %collective-permute-start.32 = (bf16[16,32,128]{2,1,0:T(8,128)(2,1)S(1)}, bf16[16,32,128]{2,1,0:T(8,128)(2,1)S(1)}, u32[]{:S(2)}, u32[]{:S(2)}) collective-permute-start(bf16[16,32,128]{2,1,0:T(8,128)(2,1)S(1)} %get-tuple-element.67), channel_id=1, source_target_pairs={{26,0},{27,1},{28,2},{29,3},{30,4},{31,5},{24,6},{25,7},{2,8},{3,9... | collective-permute-start | bytes 393224 | tf_op jit(solution)/shard_map/ppermute | solution.py:170
  244.7 41.8 %collective-permute-start.33 = (bf16[16,32,128]{2,1,0:T(8,128)(2,1)}, bf16[16,32,128]{2,1,0:T(8,128)(2,1)}, u32[]{:S(2)}, u32[]{:S(2)}) collective-permute-start(bf16[16,32,128]{2,1,0:T(8,128)(2,1)} %get-tuple-element.68), channel_id=1, source_target_pairs={{27,0},{28,1},{29,2},{30,3},{31,4},{24,5},{25,6},{26,7},{3,8},{4,9... | collective-permute-start | bytes 393224 | tf_op jit(solution)/shard_map/ppermute | solution.py:170
  252.9 33.6 %collective-permute-start.34 = (bf16[16,32,128]{2,1,0:T(8,128)(2,1)}, bf16[16,32,128]{2,1,0:T(8,128)(2,1)}, u32[]{:S(2)}, u32[]{:S(2)}) collective-permute-start(bf16[16,32,128]{2,1,0:T(8,128)(2,1)} %get-tuple-element.69), channel_id=1, source_target_pairs={{28,0},{29,1},{30,2},{31,3},{24,4},{25,5},{26,6},{27,7},{4,8},{5,9... | collective-permute-start | bytes 393224 | tf_op jit(solution)/shard_map/ppermute | solution.py:170
  258.3 28.2 %collective-permute-start.35 = (bf16[16,32,128]{2,1,0:T(8,128)(2,1)}, bf16[16,32,128]{2,1,0:T(8,128)(2,1)}, u32[]{:S(2)}, u32[]{:S(2)}) collective-permute-start(bf16[16,32,128]{2,1,0:T(8,128)(2,1)} %get-tuple-element.70), channel_id=1, source_target_pairs={{29,0},{30,1},{31,2},{24,3},{25,4},{26,5},{27,6},{28,7},{5,8},{6,9... | collective-permute-start | bytes 393224 | tf_op jit(solution)/shard_map/ppermute | solution.py:170
  269.7 16.8 %collective-permute-start.36 = (bf16[16,32,128]{2,1,0:T(8,128)(2,1)}, bf16[16,32,128]{2,1,0:T(8,128)(2,1)}, u32[]{:S(2)}, u32[]{:S(2)}) collective-permute-start(bf16[16,32,128]{2,1,0:T(8,128)(2,1)} %get-tuple-element.71), channel_id=1, source_target_pairs={{30,0},{31,1},{24,2},{25,3},{26,4},{27,5},{28,6},{29,7},{6,8},{7,9... | collective-permute-start | bytes 393224 | tf_op jit(solution)/shard_map/ppermute | solution.py:170
  272.4 14.1 %collective-permute-start.37 = (bf16[16,32,128]{2,1,0:T(8,128)(2,1)}, bf16[16,32,128]{2,1,0:T(8,128)(2,1)}, u32[]{:S(2)}, u32[]{:S(2)}) collective-permute-start(bf16[16,32,128]{2,1,0:T(8,128)(2,1)} %get-tuple-element.72), channel_id=1, source_target_pairs={{31,0},{24,1},{25,2},{26,3},{27,4},{28,5},{29,6},{30,7},{7,8},{0,9... | collective-permute-start | bytes 393224 | tf_op jit(solution)/shard_map/ppermute | solution.py:170
  274.3 1.0 copy-start.9
  275.3 0.9 copy-start.11
  277.2 9.3 %copy-start.2 = (bf16[16,32,128]{2,1,0:T(8,128)(2,1)S(1)}, bf16[16,32,128]{2,1,0:T(8,128)(2,1)}, u32[]{:S(2)}) copy-start(bf16[16,32,128]{2,1,0:T(8,128)(2,1)} %copy-done.1) | copy-start | bytes 393220
  277.2 9.3 %copy-start.4 = (bf16[16,32,128]{2,1,0:T(8,128)(2,1)S(1)}, bf16[16,32,128]{2,1,0:T(8,128)(2,1)}, u32[]{:S(2)}) copy-start(bf16[16,32,128]{2,1,0:T(8,128)(2,1)} %copy-done.3) | copy-start | bytes 393220
  277.2 9.3 %copy-start.6 = (bf16[16,32,128]{2,1,0:T(8,128)(2,1)S(1)}, bf16[16,32,128]{2,1,0:T(8,128)(2,1)}, u32[]{:S(2)}) copy-start(bf16[16,32,128]{2,1,0:T(8,128)(2,1)} %copy-done.5) | copy-start | bytes 393220
  (8 other events, 5.9 us)

commit v7 on v5

--- a/solution.py
+++ b/solution.py
@@ -7,7 +7,7 @@
 
 
 RAD = 2
-X_LEN = 4
+X_LEN, Z_LEN = 4, 8
 
 
 def passed_along(block, axis, distance):
@@ -16,16 +16,17 @@
     return lax.ppermute(block, axis, route)
 
 
-def from_x(block, distance):
-    count = lax.axis_size("aux")
-    z_len = count // X_LEN
-    route = [((i - distance * z_len) % count, i) for i in range(count)]
+def from_grid(block, dx, dz):
+    route = []
+    for x in range(X_LEN):
+        for z in range(Z_LEN):
+            source = (x - dx) % X_LEN * Z_LEN + (z - dz) % Z_LEN
+            route.append((source, x * Z_LEN + z))
     return lax.ppermute(block, "aux", route)
 
 
 def groups_along(which):
-    z_len = lax.axis_size("aux") // X_LEN
-    lines = [[x * z_len + z for z in range(z_len)] for x in range(X_LEN)]
+    lines = [[x * Z_LEN + z for z in range(Z_LEN)] for x in range(X_LEN)]
     return lines if which == "z" else [list(line) for line in zip(*lines)]
 
 
@@ -37,28 +38,36 @@
 
 
 def metric_kernel(me_ref, rows_ref, out_ref):
-    copies, _, kept = out_ref.shape
+    kept = out_ref.shape[1]
     side = rows_ref.shape[1] // X_LEN
-    my_x = me_ref[0] // copies
+    my_x = me_ref[0] // Z_LEN
     for k in range(kept // side):
         place = lax.rem(my_x + k, X_LEN)
-        block = rows_ref[:, pl.ds(pl.multiple_of(place * side, side), side)]
-        for copy in range(copies):
-            out_ref[copy, :, k * side:(k + 1) * side] = block
-
-
-def metric_copies(rows, me, copies):
-    count, cols = rows.shape
+        out_ref[:, k * side:(k + 1) * side] = (
+            rows_ref[:, pl.ds(pl.multiple_of(place * side, side), side)]
+        )
+
+
+def line_kernel(me_ref, *refs):
+    *piece_refs, line_ref, short_ref = refs
+    count = piece_refs[0].shape[0]
+    my_z = lax.rem(me_ref[0], Z_LEN)
+    for k, piece_ref in enumerate(piece_refs):
+        place = lax.rem(my_z + (Z_LEN - k), Z_LEN)
+        rows = pl.ds(pl.multiple_of(place * count, count), count)
+        line_ref[rows, :] = piece_ref[...]
+        short_ref[rows, :] = piece_ref[:, :short_ref.shape[1]]
+
+
+def in_vmem(kernel, shapes, me, *arrays):
+    whole = pl.BlockSpec(memory_space=pltpu.VMEM)
     return pl.pallas_call(
-        metric_kernel,
-        out_shape=jax.ShapeDtypeStruct((copies, count, 3 * cols // X_LEN), rows.dtype),
-        in_specs=[
-            pl.BlockSpec(memory_space=pltpu.SMEM),
-            pl.BlockSpec(memory_space=pltpu.VMEM),
-        ],
-        out_specs=pl.BlockSpec(memory_space=pltpu.VMEM),
+        kernel,
+        out_shape=[jax.ShapeDtypeStruct(shape, arrays[0].dtype) for shape in shapes],
+        in_specs=[pl.BlockSpec(memory_space=pltpu.SMEM)] + [whole] * len(arrays),
+        out_specs=[whole] * len(shapes),
         compiler_params=pltpu.CompilerParams(vmem_limit_bytes=4 << 20),
-    )(me, rows)
+    )(me, *arrays)
 
 
 BLOCKS = {
@@ -138,12 +147,20 @@
     def _():
         total_ref[...] = jnp.zeros_like(total_ref)
 
-    total = total_ref[...]
+    lefts, rights = [], []
     for fitted_ref, half_ref in zip(pairs[::2], pairs[1::2]):
         parts, width, depth, cols = half_ref.shape
         for w in range(width):
-            right = half_ref[:, w].reshape(parts * depth, cols)
-            total += jnp.dot(fitted_ref[w], right, preferred_element_type=jnp.float32)
+            lefts.append(fitted_ref[w])
+            rights.append(half_ref[:, w].reshape(parts * depth, cols))
+    total = total_ref[...]
+    for k in range(0, len(lefts), 2):
+        both = jnp.dot(
+            jnp.concatenate(lefts[k:k + 2], axis=0),
+            jnp.concatenate(rights[k:k + 2], axis=1),
+            preferred_element_type=jnp.float32,
+        )
+        total += both[:cols, :cols] + both[cols:, cols:]
     total_ref[...] = total
 
     @pl.when(step == pl.num_programs(0) - 1)
@@ -213,19 +230,18 @@
 
 def body(integrals, density, dens_cols, neighbours, metric):
     ints, rows = integrals[0], metric[0]
-    group = lax.axis_size("aux")
-    z_len = group // X_LEN
     cols = ints.shape[2]
+    count, side = rows.shape[0], rows.shape[1] // X_LEN
     me = lax.axis_index("aux")[None]
-    line = to_all(metric_copies(rows, me, z_len), "z")
-    line = line.reshape(-1, line.shape[2])
-    line, ints_out = lax.optimization_barrier((line, by_slot(ints)))
-    ints_moved = exchanged(ints_out)
-    short = line[:, :2 * rows.shape[1] // X_LEN]
-    parts = [line, from_x(line, -1), from_x(short, 2), from_x(short, 1)]
+    ints_moved = exchanged(by_slot(ints))
+    kept, = in_vmem(metric_kernel, [(count, 3 * side)], me, rows)
+    pieces = [kept] + [from_grid(kept, 0, k) for k in range(1, Z_LEN)]
     dense = local_density(density, dens_cols, neighbours)
     half = jnp.einsum("ls,plm->psm", dense, ints, preferred_element_type=jnp.float32)
     half_moved = exchanged(by_slot(half.astype(jnp.bfloat16)))
+    shapes = [(Z_LEN * count, 3 * side), (Z_LEN * count, 2 * side)]
+    line, short = in_vmem(line_kernel, shapes, me, *pieces)
+    parts = [line, from_grid(line, -1, 0), from_grid(short, 2, 0), from_grid(short, 1, 0)]
     most = 3 * ints_moved.shape[1] // 4
     rest = fit(parts, me, ints_moved, most, ints_moved.shape[1] - most)
     fitted = [
@@ -234,7 +250,7 @@
     ]
     shares = close(fitted, half_moved, 4)
     shares = jnp.sum(to_all(shares, "x"), axis=0).astype(jnp.bfloat16)
-    shares = jnp.broadcast_to(shares[None], (z_len, cols, cols))
+    shares = jnp.broadcast_to(shares[None], (Z_LEN, cols, cols))
     shares = to_all(shares, "z").astype(jnp.float32)
     return jnp.sum(shares, axis=0)[None]
 

time: 260 us -> 289 us (1.11)
  starting transfers between devices: 38 us -> 64.2 us
    ppermute x3 -> x10, waiting for transfers between devices: 21.6 us -> 85.1 us  [from_grid(): return lax.ppermute(block, 'aux', route)]
    all_to_all x2, waiting for transfers between devices: 129 us -> 75.8 us  [exchanged(): return lax.all_to_all(array, 'aux', split_axis=0, concat_axis=0, tiled=True)]
    ppermute x3 -> x10, starting transfers between devices: 11 us -> 39.2 us  [from_grid(): return lax.ppermute(block, 'aux', route)]
    all_to_all x1 -> x0, starting transfers between devices: 10.3 us -> none  [to_all(): lax.all_to_all(copies, 'aux', split_axis=0, concat_axis=0, tiled=True, ax...]
    all_to_all x2, starting transfers between devices: 10.3 us -> 18.7 us  [exchanged(): return lax.all_to_all(array, 'aux', split_axis=0, concat_axis=0, tiled=True)]
    all_to_all x1 -> x0, waiting for transfers between devices: 7.84 us -> none  [to_all(): lax.all_to_all(copies, 'aux', split_axis=0, concat_axis=0, tiled=True, ax...]
  transfers between devices with their start and end apart: 10 -> 16, of which waited for: 6 -> 7; matrix products, arithmetic and copies ran while one was open for 7% -> 4% of each run, Pallas kernels for 3% -> 3%
where the time goes in v7:
time: 289 us; the launch traced here: 288 us
  waiting for transfers between devices  164 us (57%)
  starting transfers between devices  64.2 us (22%)
  blocking collectives  26.3 us (9%)
  local copies, waits for them, and re-layouts  14.2 us (5%)
  Pallas kernels  13.3 us (5%)
  matrix products  5.11 us (2%)
    ppermute x10, waiting for transfers between devices, from_grid(): return lax.ppermute(block, 'aux', route)  85.1 us
    all_to_all x2, waiting for transfers between devices, exchanged(): return lax.all_to_all(array, 'aux', split_axis=0, concat_axis=0, tiled=True)  75.8 us
    ppermute x10, starting transfers between devices, from_grid(): return lax.ppermute(block, 'aux', route)  39.2 us
    all_to_all x2, blocking collectives, to_all(): lax.all_to_all(copies, 'aux', split_axis=0, concat_axis=0, tiled=True, ax...  26.3 us
    all_to_all x2, starting transfers between devices, exchanged(): return lax.all_to_all(array, 'aux', split_axis=0, concat_axis=0, tiled=True)  18.7 us
    pallas_call x2, Pallas kernels, fit(): pl.pallas_call(fit_kernel, out_shape=jax.ShapeDtypeStruct((slots, cols, r...  8.99 us
    transpose x1, local copies, waits for them, and re-layouts, by_slot(): return array.transpose(1, 0, 2).reshape(group, slots // group, count, cols)  6.87 us
    ppermute x4, starting transfers between devices, passed_along(): return lax.ppermute(block, axis, route)  6.35 us
  transfers between devices with their start and end apart: 16, of which 7 were waited for; matrix products, arithmetic and copies ran while one was open for 4% of the time, Pallas kernels for 3%

profile of v7, /device:TPU:48, one launch (start us, length us, event | category | flops | bytes accessed | tf_op | source)
XLA Modules:
  0.0 288.4 jit_solution(5414535133810237911)
XLA Ops:
  0.0 6.9 %copy.11 = bf16[512,32,128]{2,1,0:T(8,128)(2,1)} copy(bf16[512,32,128]{2,0,1:T(8,128)(2,1)} %bitcast.40) | data formatting | bytes 8388608 | tf_op jit(solution)/shard_map/transpose | solution.py:224
  6.9 13.4 %all-to-all-start = ((bf16[32,16,32,128]{3,2,1,0:T(8,128)(2,1)}), bf16[32,16,32,128]{3,2,1,0:T(8,128)(2,1)}, u32[]{:S(2)}, u32[]{:S(2)}) async-start(bf16[32,16,32,128]{3,2,1,0:T(8,128)(2,1)} %bitcast.39), calls=%async_computation | async-start | bytes 8388608 | tf_op jit(solution)/shard_map/all_to_all | solution.py:228
  20.3 0.5 collective-permute-start.12
  20.8 0.0 collective-permute-start.11
  20.8 2.6 collective-permute-start.10
  23.4 3.3 %collective-permute-start.13 = (bf16[1,4,128,128]{3,2,1,0:T(8,128)(2,1)S(1)}, bf16[1,4,128,128]{3,2,1,0:T(8,128)(2,1)S(1)}, u32[]{:S(2)}, u32[]{:S(2)}) collective-permute-start(bf16[1,4,128,128]{3,2,1,0:T(8,128)(2,1)S(1)} %copy-done.3), channel_id=1, source_target_pairs={{64,0},{96,32},{128,64},{160,96},{192,128},{224,160},{256,192},{28... | collective-permute-start | bytes 393224 | tf_op jit(solution)/shard_map/ppermute | solution.py:16
  26.7 0.1 copy.12
  26.8 0.2 dynamic-slice_reduce_fusion
  27.0 0.6 gather_fusion.1
  27.6 0.1 broadcast_select_fusion.1
  27.7 1.3 collective-permute-done.10
  28.9 0.0 collective-permute-done.11
  29.0 0.0 collective-permute-done.12
  29.0 1.9 collective-permute-done.13
  31.0 0.6 gather_fusion
  31.6 0.1 broadcast_select_fusion
  31.7 0.5 convolution_convert_fusion
  32.3 4.6 %fusion.2 = bf16[512,32,128]{2,0,1:T(8,128)(2,1)S(1)} fusion(bf16[1,32,512,128]{3,2,1,0:T(8,128)(2,1)} %param.5, bf16[64,8,4,128]{3,2,1,0:T(4,128)(2,1)S(1)} %bitcast.41), kind=kOutput, calls=%fused_computation.4 | convolution fusion | flops 2149580800 | bytes 8912896 | tf_op jit(solution)/shard_map/ls,plm->psm/dot_general | solution.py:240
  36.9 4.7 %copy.15 = bf16[512,32,128]{2,1,0:T(8,128)(2,1)} copy(bf16[512,32,128]{2,0,1:T(8,128)(2,1)S(1)} %fusion.2) | data formatting | bytes 8388608 | tf_op jit(solution)/shard_map/convert_element_type | solution.py:241
  41.5 75.8 %all-to-all-done.refs_4_ = bf16[32,16,32,128]{3,2,1,0:T(8,128)(2,1)} async-done(((bf16[32,16,32,128]{3,2,1,0:T(8,128)(2,1)}), bf16[32,16,32,128]{3,2,1,0:T(8,128)(2,1)}, u32[]{:S(2)}, u32[]{:S(2)}) %all-to-all-start) | async-done | bytes 4194336 | tf_op jit(solution)/shard_map/all_to_all | solution.py:228
  117.3 5.2 %all-to-all-start.1 = ((bf16[32,16,32,128]{3,2,1,0:T(8,128)(2,1)}), bf16[32,16,32,128]{3,2,1,0:T(8,128)(2,1)}, u32[]{:S(2)}, u32[]{:S(2)}) async-start(bf16[32,16,32,128]{3,2,1,0:T(8,128)(2,1)} %bitcast.38), calls=%async_computation.1 | async-start | bytes 8388608 | tf_op jit(solution)/shard_map/all_to_all | solution.py:228
  122.6 4.8 %collective-permute-start.6 = (bf16[32,768]{1,0:T(8,128)(2,1)S(1)}, bf16[32,768]{1,0:T(8,128)(2,1)S(1)}, u32[]{:S(2)}, u32[]{:S(2)}) collective-permute-start(bf16[32,768]{1,0:T(8,128)(2,1)S(1)} %shard_map.55.refs_0_), channel_id=1, source_target_pairs={{1,0},{2,1},{3,2},{4,3},{5,4},{6,5},{7,6},{0,7},{9,8},{10,9},{11,1... | collective-permute-start | bytes 147464 | tf_op jit(solution)/shard_map/ppermute | solution.py:25
  127.4 4.3 %collective-permute-start.5 = (bf16[32,768]{1,0:T(8,128)(2,1)S(1)}, bf16[32,768]{1,0:T(8,128)(2,1)S(1)}, u32[]{:S(2)}, u32[]{:S(2)}) collective-permute-start(bf16[32,768]{1,0:T(8,128)(2,1)S(1)} %shard_map.55.refs_0_), channel_id=1, source_target_pairs={{2,0},{3,1},{4,2},{5,3},{6,4},{7,5},{0,6},{1,7},{10,8},{11,9},{12,... | collective-permute-start | bytes 147464 | tf_op jit(solution)/shard_map/ppermute | solution.py:25
  131.7 3.4 %collective-permute-start.4 = (bf16[32,768]{1,0:T(8,128)(2,1)S(1)}, bf16[32,768]{1,0:T(8,128)(2,1)S(1)}, u32[]{:S(2)}, u32[]{:S(2)}) collective-permute-start(bf16[32,768]{1,0:T(8,128)(2,1)S(1)} %shard_map.55.refs_0_), channel_id=1, source_target_pairs={{3,0},{4,1},{5,2},{6,3},{7,4},{0,5},{1,6},{2,7},{11,8},{12,9},{13,... | collective-permute-start | bytes 147464 | tf_op jit(solution)/shard_map/ppermute | solution.py:25
  135.1 5.5 %collective-permute-start.3 = (bf16[32,768]{1,0:T(8,128)(2,1)S(1)}, bf16[32,768]{1,0:T(8,128)(2,1)S(1)}, u32[]{:S(2)}, u32[]{:S(2)}) collective-permute-start(bf16[32,768]{1,0:T(8,128)(2,1)S(1)} %shard_map.55.refs_0_), channel_id=1, source_target_pairs={{4,0},{5,1},{6,2},{7,3},{0,4},{1,5},{2,6},{3,7},{12,8},{13,9},{14,... | collective-permute-start | bytes 147464 | tf_op jit(solution)/shard_map/ppermute | solution.py:25
  140.6 2.2 collective-permute-start.2
  142.7 74.0 %collective-permute-done.6.refs_7_ = bf16[32,768]{1,0:T(8,128)(2,1)S(1)} collective-permute-done((bf16[32,768]{1,0:T(8,128)(2,1)S(1)}, bf16[32,768]{1,0:T(8,128)(2,1)S(1)}, u32[]{:S(2)}, u32[]{:S(2)}) %collective-permute-start.6) | collective-permute-done | bytes 49184 | tf_op jit(solution)/shard_map/ppermute | solution.py:25
  216.8 4.2 %collective-permute-start.1 = (bf16[32,768]{1,0:T(8,128)(2,1)S(1)}, bf16[32,768]{1,0:T(8,128)(2,1)S(1)}, u32[]{:S(2)}, u32[]{:S(2)}) collective-permute-start(bf16[32,768]{1,0:T(8,128)(2,1)S(1)} %shard_map.55.refs_0_), channel_id=1, source_target_pairs={{6,0},{7,1},{0,2},{1,3},{2,4},{3,5},{4,6},{5,7},{14,8},{15,9},{8,1... | collective-permute-start | bytes 147464 | tf_op jit(solution)/shard_map/ppermute | solution.py:25
  221.0 0.0 collective-permute-done.5.refs_6_
  221.0 4.2 %collective-permute-start = (bf16[32,768]{1,0:T(8,128)(2,1)S(1)}, bf16[32,768]{1,0:T(8,128)(2,1)S(1)}, u32[]{:S(2)}, u32[]{:S(2)}) collective-permute-start(bf16[32,768]{1,0:T(8,128)(2,1)S(1)} %shard_map.55.refs_0_), channel_id=1, source_target_pairs={{7,0},{0,1},{1,2},{2,3},{3,4},{4,5},{5,6},{6,7},{15,8},{8,9},{9,10... | collective-permute-start | bytes 147464 | tf_op jit(solution)/shard_map/ppermute | solution.py:25
  225.2 0.0 collective-permute-done.4.refs_5_
  225.2 0.0 collective-permute-done.3.refs_4_
  225.2 0.0 collective-permute-done.2.refs_3_
  225.2 1.1 collective-permute-done.1.refs_2_
  226.3 2.0 collective-permute-done.refs_1_
  228.2 0.1 shard_map.56
  228.3 4.7 %collective-permute-start.7 = (bf16[256,768]{1,0:T(8,128)(2,1)S(1)}, bf16[256,768]{1,0:T(8,128)(2,1)S(1)}, u32[]{:S(2)}, u32[]{:S(2)}) collective-permute-start(bf16[256,768]{1,0:T(8,128)(2,1)S(1)} %get-tuple-element.7.refs_0_), channel_id=1, source_target_pairs={{8,0},{9,1},{10,2},{11,3},{12,4},{13,5},{14,6},{15,7},{16,8},{17,9... | collective-permute-start | bytes 1179656 | tf_op jit(solution)/shard_map/ppermute | solution.py:25
  233.0 1.9 collective-permute-start.9
  234.9 4.1 %collective-permute-start.8 = (bf16[256,512]{1,0:T(8,128)(2,1)S(1)}, bf16[256,512]{1,0:T(8,128)(2,1)S(1)}, u32[]{:S(2)}, u32[]{:S(2)}) collective-permute-start(bf16[256,512]{1,0:T(8,128)(2,1)S(1)} %get-tuple-element.8), channel_id=1, source_target_pairs={{16,0},{17,1},{18,2},{19,3},{20,4},{21,5},{22,6},{23,7},{24,8},{25... | collective-permute-start | bytes 786440 | tf_op jit(solution)/shard_map/ppermute | solution.py:25
  239.0 8.0 %collective-permute-done.9.refs_3_ = bf16[256,512]{1,0:T(8,128)(2,1)S(1)} collective-permute-done((bf16[256,512]{1,0:T(8,128)(2,1)S(1)}, bf16[256,512]{1,0:T(8,128)(2,1)S(1)}, u32[]{:S(2)}, u32[]{:S(2)}) %collective-permute-start.9) | collective-permute-done | bytes 262176 | tf_op jit(solution)/shard_map/ppermute | solution.py:25
  247.1 0.0 collective-permute-done.8.refs_2_
  247.1 2.6 shard_map.58.refs_2_
  249.7 1.0 copy-done.1
  250.7 6.4 %shard_map.57.refs_0_ = bf16[12,128,1024]{2,1,0:T(8,128)(2,1)S(1)} custom-call(s32[1]{0:T(128)} %bitcast.me_ref, bf16[256,768]{1,0:T(8,128)(2,1)S(1)} %get-tuple-element.7.refs_0_, bf16[256,768]{1,0:T(8,128)(2,1)S(1)} %collective-permute-done.7.refs_1_, bf16[256,512]{1,0:T(8,128)(2,1)S(1)} %collective-permute-done.8.refs_2_, ...), custom_call_target="tpu_custom_call" | custom-call | flops 3221225472 | bytes 8388608 | tf_op jit(solution)/shard_map/pallas_call | solution.py:117
  257.1 4.2 %shard_map.59 = f32[4,128,128]{2,1,0:T(8,128)S(1)} custom-call(bf16[12,128,1024]{2,1,0:T(8,128)(2,1)S(1)} %shard_map.57.refs_0_, bf16[32,16,32,128]{3,2,1,0:T(8,128)(2,1)} %all-to-all-done.1.refs_1_.refs_3_, bf16[4,128,1024]{2,1,0:T(8,128)(2,1)} %copy-done.1, bf16[32,16,32,128]{3,2,1,0:T(8,128)(2,1)} %all-to-all-done.1.refs_1_.refs_3_), custom_call_target="tpu_custom_call" | custom-call | flops 536870912 | bytes 8388608 | tf_op jit(solution)/shard_map/pallas_call | solution.py:186
  261.3 9.1 %all_to_all.20 = f32[4,128,128]{2,1,0:T(8,128)S(1)} all-to-all(f32[4,128,128]{2,1,0:T(8,128)S(1)} %shard_map.59), channel_id=1, replica_groups={{0,8,16,24},{1,9,17,25},{2,10,18,26},{3,11,19,27},{4,12,20,28},{5,13,21..., dimensions={0} | all-to-all | bytes 524288 | tf_op jit(solution)/shard_map/all_to_all | solution.py:34
  270.5 17.2 %all_to_all.21 = bf16[8,128,128]{2,1,0:T(8,128)(2,1)S(1)} all-to-all(bf16[8,128,128]{2,1,0:T(8,128)(2,1)S(1)} %broadcast_in_dim.34), channel_id=1, replica_groups={{0,1,2,3,4,5,6,7},{8,9,10,11,12,13,14,15},{16,17,18,19,20,21,22,23},{24..., dimensions={0} | all-to-all | bytes 524288 | tf_op jit(solution)/shard_map/all_to_all | solution.py:34
  287.7 0.7 convert_reduce_fusion
  (23 shorter events, 0.2 us)
Async XLA Ops:
  0.0 26.8 %copy-start = (s32[16,4]{0,1:T(4,128)S(1)}, s32[16,4]{0,1:T(4,128)}, u32[]{:S(2)}) copy-start(s32[16,4]{0,1:T(4,128)} %param.8) | copy-start | bytes 772
  6.9 13.4 %copy-start.3 = (bf16[1,4,128,128]{3,2,1,0:T(8,128)(2,1)S(1)}, bf16[1,4,128,128]{3,2,1,0:T(8,128)(2,1)}, u32[]{:S(2)}) copy-start(bf16[1,4,128,128]{3,2,1,0:T(8,128)(2,1)} %param.6) | copy-start | bytes 393220
  6.9 19.8 %copy-start.4 = (s32[16,4]{0,1:T(4,128)S(1)}, s32[16,4]{0,1:T(4,128)}, u32[]{:S(2)}) copy-start(s32[16,4]{0,1:T(4,128)} %param.7) | copy-start | bytes 772
  6.9 110.4 %all-to-all-start = ((bf16[32,16,32,128]{3,2,1,0:T(8,128)(2,1)}), bf16[32,16,32,128]{3,2,1,0:T(8,128)(2,1)}, u32[]{:S(2)}, u32[]{:S(2)}) async-start(bf16[32,16,32,128]{3,2,1,0:T(8,128)(2,1)} %bitcast.39), calls=%async_computation | async-start | bytes 8388608 | tf_op jit(solution)/shard_map/all_to_all | solution.py:228
  20.3 8.7 %collective-permute-start.12 = (bf16[1,4,128,128]{3,2,1,0:T(8,128)(2,1)S(1)}, bf16[1,4,128,128]{3,2,1,0:T(8,128)(2,1)S(1)}, u32[]{:S(2)}, u32[]{:S(2)}) collective-permute-start(bf16[1,4,128,128]{3,2,1,0:T(8,128)(2,1)S(1)} %copy-done.3), channel_id=1, source_target_pairs={{32,0},{64,32},{96,64},{128,96},{160,128},{192,160},{224,192},{256... | collective-permute-start | bytes 393224 | tf_op jit(solution)/shard_map/ppermute | solution.py:16
  20.8 8.1 %collective-permute-start.11 = (bf16[1,4,128,128]{3,2,1,0:T(8,128)(2,1)S(1)}, bf16[1,4,128,128]{3,2,1,0:T(8,128)(2,1)S(1)}, u32[]{:S(2)}, u32[]{:S(2)}) collective-permute-start(bf16[1,4,128,128]{3,2,1,0:T(8,128)(2,1)S(1)} %copy-done.3), channel_id=1, source_target_pairs={{480,0},{0,32},{32,64},{64,96},{96,128},{128,160},{160,192},{192,2... | collective-permute-start | bytes 393224 | tf_op jit(solution)/shard_map/ppermute | solution.py:16
  20.8 8.1 %collective-permute-start.10 = (bf16[1,4,128,128]{3,2,1,0:T(8,128)(2,1)S(1)}, bf16[1,4,128,128]{3,2,1,0:T(8,128)(2,1)S(1)}, u32[]{:S(2)}, u32[]{:S(2)}) collective-permute-start(bf16[1,4,128,128]{3,2,1,0:T(8,128)(2,1)S(1)} %copy-done.3), channel_id=1, source_target_pairs={{448,0},{480,32},{0,64},{32,96},{64,128},{96,160},{128,192},{160,2... | collective-permute-start | bytes 393224 | tf_op jit(solution)/shard_map/ppermute | solution.py:16
  23.4 7.5 %collective-permute-start.13 = (bf16[1,4,128,128]{3,2,1,0:T(8,128)(2,1)S(1)}, bf16[1,4,128,128]{3,2,1,0:T(8,128)(2,1)S(1)}, u32[]{:S(2)}, u32[]{:S(2)}) collective-permute-start(bf16[1,4,128,128]{3,2,1,0:T(8,128)(2,1)S(1)} %copy-done.3), channel_id=1, source_target_pairs={{64,0},{96,32},{128,64},{160,96},{192,128},{224,160},{256,192},{28... | collective-permute-start | bytes 393224 | tf_op jit(solution)/shard_map/ppermute | solution.py:16
  117.3 5.2 %copy-start.2 = (bf16[1,32,1024]{2,1,0:T(8,128)(2,1)S(1)}, bf16[1,32,1024]{2,1,0:T(8,128)(2,1)}, u32[]{:S(2)}) copy-start(bf16[1,32,1024]{2,1,0:T(8,128)(2,1)} %param.9) | copy-start | bytes 196612
  117.3 139.8 %all-to-all-start.1 = ((bf16[32,16,32,128]{3,2,1,0:T(8,128)(2,1)}), bf16[32,16,32,128]{3,2,1,0:T(8,128)(2,1)}, u32[]{:S(2)}, u32[]{:S(2)}) async-start(bf16[32,16,32,128]{3,2,1,0:T(8,128)(2,1)} %bitcast.38), calls=%async_computation.1 | async-start | bytes 8388608 | tf_op jit(solution)/shard_map/all_to_all | solution.py:228
  122.6 94.2 %collective-permute-start.6 = (bf16[32,768]{1,0:T(8,128)(2,1)S(1)}, bf16[32,768]{1,0:T(8,128)(2,1)S(1)}, u32[]{:S(2)}, u32[]{:S(2)}) collective-permute-start(bf16[32,768]{1,0:T(8,128)(2,1)S(1)} %shard_map.55.refs_0_), channel_id=1, source_target_pairs={{1,0},{2,1},{3,2},{4,3},{5,4},{6,5},{7,6},{0,7},{9,8},{10,9},{11,1... | collective-permute-start | bytes 147464 | tf_op jit(solution)/shard_map/ppermute | solution.py:25
  127.4 93.5 %collective-permute-start.5 = (bf16[32,768]{1,0:T(8,128)(2,1)S(1)}, bf16[32,768]{1,0:T(8,128)(2,1)S(1)}, u32[]{:S(2)}, u32[]{:S(2)}) collective-permute-start(bf16[32,768]{1,0:T(8,128)(2,1)S(1)} %shard_map.55.refs_0_), channel_id=1, source_target_pairs={{2,0},{3,1},{4,2},{5,3},{6,4},{7,5},{0,6},{1,7},{10,8},{11,9},{12,... | collective-permute-start | bytes 147464 | tf_op jit(solution)/shard_map/ppermute | solution.py:25
  131.7 93.5 %collective-permute-start.4 = (bf16[32,768]{1,0:T(8,128)(2,1)S(1)}, bf16[32,768]{1,0:T(8,128)(2,1)S(1)}, u32[]{:S(2)}, u32[]{:S(2)}) collective-permute-start(bf16[32,768]{1,0:T(8,128)(2,1)S(1)} %shard_map.55.refs_0_), channel_id=1, source_target_pairs={{3,0},{4,1},{5,2},{6,3},{7,4},{0,5},{1,6},{2,7},{11,8},{12,9},{13,... | collective-permute-start | bytes 147464 | tf_op jit(solution)/shard_map/ppermute | solution.py:25
  135.1 90.1 %collective-permute-start.3 = (bf16[32,768]{1,0:T(8,128)(2,1)S(1)}, bf16[32,768]{1,0:T(8,128)(2,1)S(1)}, u32[]{:S(2)}, u32[]{:S(2)}) collective-permute-start(bf16[32,768]{1,0:T(8,128)(2,1)S(1)} %shard_map.55.refs_0_), channel_id=1, source_target_pairs={{4,0},{5,1},{6,2},{7,3},{0,4},{1,5},{2,6},{3,7},{12,8},{13,9},{14,... | collective-permute-start | bytes 147464 | tf_op jit(solution)/shard_map/ppermute | solution.py:25
  140.6 84.6 %collective-permute-start.2 = (bf16[32,768]{1,0:T(8,128)(2,1)S(1)}, bf16[32,768]{1,0:T(8,128)(2,1)S(1)}, u32[]{:S(2)}, u32[]{:S(2)}) collective-permute-start(bf16[32,768]{1,0:T(8,128)(2,1)S(1)} %shard_map.55.refs_0_), channel_id=1, source_target_pairs={{5,0},{6,1},{7,2},{0,3},{1,4},{2,5},{3,6},{4,7},{13,8},{14,9},{15,... | collective-permute-start | bytes 147464 | tf_op jit(solution)/shard_map/ppermute | solution.py:25
  216.8 9.5 %collective-permute-start.1 = (bf16[32,768]{1,0:T(8,128)(2,1)S(1)}, bf16[32,768]{1,0:T(8,128)(2,1)S(1)}, u32[]{:S(2)}, u32[]{:S(2)}) collective-permute-start(bf16[32,768]{1,0:T(8,128)(2,1)S(1)} %shard_map.55.refs_0_), channel_id=1, source_target_pairs={{6,0},{7,1},{0,2},{1,3},{2,4},{3,5},{4,6},{5,7},{14,8},{15,9},{8,1... | collective-permute-start | bytes 147464 | tf_op jit(solution)/shard_map/ppermute | solution.py:25
  221.0 7.2 %collective-permute-start = (bf16[32,768]{1,0:T(8,128)(2,1)S(1)}, bf16[32,768]{1,0:T(8,128)(2,1)S(1)}, u32[]{:S(2)}, u32[]{:S(2)}) collective-permute-start(bf16[32,768]{1,0:T(8,128)(2,1)S(1)} %shard_map.55.refs_0_), channel_id=1, source_target_pairs={{7,0},{0,1},{1,2},{2,3},{3,4},{4,5},{5,6},{6,7},{15,8},{8,9},{9,10... | collective-permute-start | bytes 147464 | tf_op jit(solution)/shard_map/ppermute | solution.py:25
  228.3 18.8 %collective-permute-start.7 = (bf16[256,768]{1,0:T(8,128)(2,1)S(1)}, bf16[256,768]{1,0:T(8,128)(2,1)S(1)}, u32[]{:S(2)}, u32[]{:S(2)}) collective-permute-start(bf16[256,768]{1,0:T(8,128)(2,1)S(1)} %get-tuple-element.7.refs_0_), channel_id=1, source_target_pairs={{8,0},{9,1},{10,2},{11,3},{12,4},{13,5},{14,6},{15,7},{16,8},{17,9... | collective-permute-start | bytes 1179656 | tf_op jit(solution)/shard_map/ppermute | solution.py:25
  233.0 14.0 %collective-permute-start.9 = (bf16[256,512]{1,0:T(8,128)(2,1)S(1)}, bf16[256,512]{1,0:T(8,128)(2,1)S(1)}, u32[]{:S(2)}, u32[]{:S(2)}) collective-permute-start(bf16[256,512]{1,0:T(8,128)(2,1)S(1)} %get-tuple-element.8), channel_id=1, source_target_pairs={{24,0},{25,1},{26,2},{27,3},{28,4},{29,5},{30,6},{31,7},{0,8},{1,9... | collective-permute-start | bytes 786440 | tf_op jit(solution)/shard_map/ppermute | solution.py:25
  234.9 12.1 %collective-permute-start.8 = (bf16[256,512]{1,0:T(8,128)(2,1)S(1)}, bf16[256,512]{1,0:T(8,128)(2,1)S(1)}, u32[]{:S(2)}, u32[]{:S(2)}) collective-permute-start(bf16[256,512]{1,0:T(8,128)(2,1)S(1)} %get-tuple-element.8), channel_id=1, source_target_pairs={{16,0},{17,1},{18,2},{19,3},{20,4},{21,5},{22,6},{23,7},{24,8},{25... | collective-permute-start | bytes 786440 | tf_op jit(solution)/shard_map/ppermute | solution.py:25
  249.7 1.0 copy-start.1

commit v8 on v7

--- a/solution.py
+++ b/solution.py
@@ -139,64 +139,80 @@
     )(me, *metric_parts, ints)
 
 
-def close_kernel(*refs):
-    *pairs, out_ref, total_ref = refs
-    step = pl.program_id(0)
-
-    @pl.when(step == 0)
-    def _():
-        total_ref[...] = jnp.zeros_like(total_ref)
-
-    lefts, rights = [], []
-    for fitted_ref, half_ref in zip(pairs[::2], pairs[1::2]):
-        parts, width, depth, cols = half_ref.shape
-        for w in range(width):
-            lefts.append(fitted_ref[w])
-            rights.append(half_ref[:, w].reshape(parts * depth, cols))
-    total = total_ref[...]
-    for k in range(0, len(lefts), 2):
-        both = jnp.dot(
-            jnp.concatenate(lefts[k:k + 2], axis=0),
-            jnp.concatenate(rights[k:k + 2], axis=1),
-            preferred_element_type=jnp.float32,
+def close_kernel(most_ref, rest_ref, half_ref, out_ref, half_buf, rest_buf, sems):
+    chunks, parts, width, depth, cols = half_buf.shape
+    copies = [
+        pltpu.make_async_copy(
+            half_ref.at[:, pl.ds(width * c, width)], half_buf.at[c], sems.at[c],
         )
-        total += both[:cols, :cols] + both[cols:, cols:]
-    total_ref[...] = total
-
-    @pl.when(step == pl.num_programs(0) - 1)
-    def _():
-        done = total_ref[...].T
-        for k in range(out_ref.shape[0]):
-            out_ref[k] = done
-
-
-def close(fitted_parts, half, steps):
+        for c in range(chunks)
+    ]
+    copies.append(pltpu.make_async_copy(rest_ref, rest_buf, sems.at[chunks]))
+    for copy in copies:
+        copy.start()
+    total = jnp.zeros((cols, cols), jnp.float32)
+    for c in range(chunks):
+        copies[c].wait()
+        if c == chunks - 1:
+            copies[chunks].wait()
+        for w in range(0, width, 2):
+            slots = (w, w + 1)
+            if c < chunks - 1:
+                lefts = [most_ref[width * c + v] for v in slots]
+            else:
+                lefts = [rest_buf[v] for v in slots]
+            rights = [half_buf[c, :, v].reshape(parts * depth, cols) for v in slots]
+            both = jnp.dot(
+                jnp.concatenate(lefts, axis=0), jnp.concatenate(rights, axis=1),
+                preferred_element_type=jnp.float32,
+            )
+            total += both[:cols, :cols] + both[cols:, cols:]
+    done = total.T
+    for k in range(out_ref.shape[0]):
+        out_ref[k] = done
+
+
+def close(most, rest, half):
     parts, slots, depth, cols = half.shape
-    rows = parts * depth
-    specs, operands, first = [], [], 0
-    for fitted in fitted_parts:
-        width = fitted.shape[0] // steps
-        specs.append(pl.BlockSpec((width, cols, rows), lambda i: (i, 0, 0)))
-        specs.append(pl.BlockSpec(
-            (parts, width, depth, cols),
-            lambda i, start=first // width: (0, i + start, 0, 0),
-        ))
-        operands += [fitted, half]
-        first += fitted.shape[0]
+    width = rest.shape[0]
+    chunks = slots // width
+    vmem, hbm = pltpu.VMEM, pltpu.HBM
     return pl.pallas_call(
         close_kernel,
         out_shape=jax.ShapeDtypeStruct((X_LEN, cols, cols), jnp.float32),
-        grid=(steps,),
-        in_specs=specs,
-        out_specs=pl.BlockSpec((X_LEN, cols, cols), lambda i: (0, 0, 0)),
-        scratch_shapes=[pltpu.VMEM((cols, cols), jnp.float32)],
-        compiler_params=pltpu.CompilerParams(vmem_limit_bytes=12 << 20),
+        in_specs=[pl.BlockSpec(memory_space=space) for space in (vmem, hbm, hbm)],
+        out_specs=pl.BlockSpec(memory_space=vmem),
+        scratch_shapes=[
+            pltpu.VMEM((chunks, parts, width, depth, cols), half.dtype),
+            pltpu.VMEM(rest.shape, rest.dtype),
+            pltpu.SemaphoreType.DMA((chunks + 1,)),
+        ],
+        compiler_params=pltpu.CompilerParams(vmem_limit_bytes=16 << 20),
         cost_estimate=pl.CostEstimate(
-            flops=2 * rows * slots * cols * cols,
-            bytes_accessed=4 * rows * slots * cols,
+            flops=2 * parts * depth * slots * cols * cols,
+            bytes_accessed=4 * parts * depth * slots * cols,
             transcendentals=0,
         ),
-    )(*operands)
+    )(most, *(pltpu.with_memory_space_constraint(x, hbm) for x in (rest, half)))
+
+
+def swap_kernel(in_ref, out_ref):
+    out_ref[...] = jnp.swapaxes(in_ref[...], 0, 1)
+
+
+def slot_major(array, width):
+    count, slots, cols = array.shape
+    return pl.pallas_call(
+        swap_kernel,
+        out_shape=pltpu.HBM((slots, count, cols), array.dtype),
+        grid=(slots // width,),
+        in_specs=[pl.BlockSpec((count, width, cols), lambda i: (0, i, 0))],
+        out_specs=pl.BlockSpec((width, count, cols), lambda i: (i, 0, 0)),
+        compiler_params=pltpu.CompilerParams(vmem_limit_bytes=8 << 20),
+        cost_estimate=pl.CostEstimate(
+            flops=0, bytes_accessed=4 * array.size, transcendentals=0,
+        ),
+    )(pltpu.with_memory_space_constraint(array, pltpu.HBM))
 
 
 def local_density(density, dens_cols, neighbours):
@@ -233,7 +249,9 @@
     cols = ints.shape[2]
     count, side = rows.shape[0], rows.shape[1] // X_LEN
     me = lax.axis_index("aux")[None]
-    ints_moved = exchanged(by_slot(ints))
+    ints_out = slot_major(ints, 64)
+    group = lax.axis_size("aux")
+    ints_moved = exchanged(ints_out.reshape(group, -1, count, cols))
     kept, = in_vmem(metric_kernel, [(count, 3 * side)], me, rows)
     pieces = [kept] + [from_grid(kept, 0, k) for k in range(1, Z_LEN)]
     dense = local_density(density, dens_cols, neighbours)
@@ -244,11 +262,7 @@
     parts = [line, from_grid(line, -1, 0), from_grid(short, 2, 0), from_grid(short, 1, 0)]
     most = 3 * ints_moved.shape[1] // 4
     rest = fit(parts, me, ints_moved, most, ints_moved.shape[1] - most)
-    fitted = [
-        fit(parts, me, ints_moved, 0, most),
-        pltpu.with_memory_space_constraint(rest, pltpu.HBM),
-    ]
-    shares = close(fitted, half_moved, 4)
+    shares = close(fit(parts, me, ints_moved, 0, most), rest, half_moved)
     shares = jnp.sum(to_all(shares, "x"), axis=0).astype(jnp.bfloat16)
     shares = jnp.broadcast_to(shares[None], (Z_LEN, cols, cols))
     shares = to_all(shares, "z").astype(jnp.float32)

time: 289 us -> 287 us (level)
  the two profiles are of different devices: /device:TPU:48 before, /device:TPU:32 now
where the time goes in v8:
time: 287 us; the launch traced here: 286 us
  waiting for transfers between devices  164 us (57%)
  starting transfers between devices  65.9 us (23%)
  blocking collectives  23.1 us (8%)
  Pallas kernels  19.3 us (7%)
  local copies, waits for them, and re-layouts  7.32 us (3%)
  matrix products  5.12 us (2%)
    ppermute x10, waiting for transfers between devices, from_grid(): return lax.ppermute(block, 'aux', route)  87.4 us
    all_to_all x2, waiting for transfers between devices, exchanged(): return lax.all_to_all(array, 'aux', split_axis=0, concat_axis=0, tiled=True)  74 us
    ppermute x10, starting transfers between devices, from_grid(): return lax.ppermute(block, 'aux', route)  38.4 us
    all_to_all x2, blocking collectives, to_all(): lax.all_to_all(copies, 'aux', split_axis=0, concat_axis=0, tiled=True, ax...  23.1 us
    all_to_all x2, starting transfers between devices, exchanged(): return lax.all_to_all(array, 'aux', split_axis=0, concat_axis=0, tiled=True)  18.7 us
    pallas_call x2, Pallas kernels, fit(): pl.pallas_call(fit_kernel, out_shape=jax.ShapeDtypeStruct((slots, cols, r...  8.98 us
    ppermute x4, starting transfers between devices, passed_along(): return lax.ppermute(block, axis, route)  8.79 us
    pallas_call x1, Pallas kernels, slot_major(): pl.pallas_call(swap_kernel, out_shape=pltpu.HBM((slots, count, cols), arr...  7.14 us
  transfers between devices with their start and end apart: 16, of which 8 were waited for; matrix products, arithmetic and copies ran while one was open for 4% of the time, Pallas kernels for 3%

profile of v8, /device:TPU:32, one launch (start us, length us, event | category | flops | bytes accessed | tf_op | source)
XLA Modules:
  0.0 285.9 jit_solution(8467396128433304469)
XLA Ops:
  0.0 7.1 %shard_map.57 = bf16[512,32,128]{2,1,0:T(8,128)(2,1)} custom-call(bf16[32,512,128]{2,1,0:T(8,128)(2,1)} %bitcast.36), custom_call_target="tpu_custom_call" | custom-call | bytes 8388608 | tf_op jit(solution)/shard_map/pallas_call | solution.py:205
  7.1 13.4 %all-to-all-start = ((bf16[32,16,32,128]{3,2,1,0:T(8,128)(2,1)}), bf16[32,16,32,128]{3,2,1,0:T(8,128)(2,1)}, u32[]{:S(2)}, u32[]{:S(2)}) async-start(bf16[32,16,32,128]{3,2,1,0:T(8,128)(2,1)} %bitcast.35), calls=%async_computation | async-start | bytes 8388608 | tf_op jit(solution)/shard_map/all_to_all | solution.py:244
  20.6 2.6 collective-permute-start.10
  23.2 0.0 collective-permute-start.11
  23.2 2.9 %collective-permute-start.12 = (bf16[1,4,128,128]{3,2,1,0:T(8,128)(2,1)S(1)}, bf16[1,4,128,128]{3,2,1,0:T(8,128)(2,1)S(1)}, u32[]{:S(2)}, u32[]{:S(2)}) collective-permute-start(bf16[1,4,128,128]{3,2,1,0:T(8,128)(2,1)S(1)} %copy-done.3), channel_id=1, source_target_pairs={{32,0},{64,32},{96,64},{128,96},{160,128},{192,160},{224,192},{256... | collective-permute-start | bytes 393224 | tf_op jit(solution)/shard_map/ppermute | solution.py:16
  26.2 3.2 %collective-permute-start.13 = (bf16[1,4,128,128]{3,2,1,0:T(8,128)(2,1)S(1)}, bf16[1,4,128,128]{3,2,1,0:T(8,128)(2,1)S(1)}, u32[]{:S(2)}, u32[]{:S(2)}) collective-permute-start(bf16[1,4,128,128]{3,2,1,0:T(8,128)(2,1)S(1)} %copy-done.3), channel_id=1, source_target_pairs={{64,0},{96,32},{128,64},{160,96},{192,128},{224,160},{256,192},{28... | collective-permute-start | bytes 393224 | tf_op jit(solution)/shard_map/ppermute | solution.py:16
  29.4 0.1 copy.10
  29.5 0.2 dynamic-slice_reduce_fusion
  29.7 0.6 gather_fusion.1
  30.3 0.1 broadcast_select_fusion.1
  30.4 0.0 collective-permute-done.10
  30.4 0.0 collective-permute-done.11
  30.5 0.0 collective-permute-done.12
  30.5 2.5 collective-permute-done.13
  33.0 0.6 gather_fusion
  33.7 0.1 broadcast_select_fusion
  33.8 0.5 convolution_convert_fusion.1
  34.4 4.6 %convolution_convert_fusion = bf16[512,32,128]{2,0,1:T(8,128)(2,1)S(1)} fusion(bf16[64,8,4,128]{3,2,1,0:T(4,128)(2,1)S(1)} %bitcast.37, bf16[1,32,512,128]{3,2,1,0:T(8,128)(2,1)} %param.5), kind=kOutput, calls=%fused_computation.2 | convolution fusion | flops 2149580800 | bytes 8912896 | tf_op jit(solution)/shard_map/ls,plm->psm/dot_general | solution.py:258
  38.9 4.7 %copy.13 = bf16[512,32,128]{2,1,0:T(8,128)(2,1)} copy(bf16[512,32,128]{2,0,1:T(8,128)(2,1)S(1)} %convolution_convert_fusion) | data formatting | bytes 8388608 | tf_op jit(solution)/shard_map/convert_element_type | solution.py:259
  43.6 74.0 %all-to-all-done.refs_4_ = bf16[32,16,32,128]{3,2,1,0:T(8,128)(2,1)} async-done(((bf16[32,16,32,128]{3,2,1,0:T(8,128)(2,1)}), bf16[32,16,32,128]{3,2,1,0:T(8,128)(2,1)}, u32[]{:S(2)}, u32[]{:S(2)}) %all-to-all-start) | async-done | bytes 4194336 | tf_op jit(solution)/shard_map/all_to_all | solution.py:244
  117.6 5.2 %all-to-all-start.1 = ((bf16[32,16,32,128]{3,2,1,0:T(8,128)(2,1)}), bf16[32,16,32,128]{3,2,1,0:T(8,128)(2,1)}, u32[]{:S(2)}, u32[]{:S(2)}) async-start(bf16[32,16,32,128]{3,2,1,0:T(8,128)(2,1)} %bitcast.34), calls=%async_computation.1 | async-start | bytes 8388608 | tf_op jit(solution)/shard_map/all_to_all | solution.py:244
  122.8 3.6 %collective-permute-start = (bf16[32,768]{1,0:T(8,128)(2,1)S(1)}, bf16[32,768]{1,0:T(8,128)(2,1)S(1)}, u32[]{:S(2)}, u32[]{:S(2)}) collective-permute-start(bf16[32,768]{1,0:T(8,128)(2,1)S(1)} %shard_map.55.refs_0_), channel_id=1, source_target_pairs={{7,0},{0,1},{1,2},{2,3},{3,4},{4,5},{5,6},{6,7},{15,8},{8,9},{9,10... | collective-permute-start | bytes 147464 | tf_op jit(solution)/shard_map/ppermute | solution.py:25
  126.5 4.3 %collective-permute-start.1 = (bf16[32,768]{1,0:T(8,128)(2,1)S(1)}, bf16[32,768]{1,0:T(8,128)(2,1)S(1)}, u32[]{:S(2)}, u32[]{:S(2)}) collective-permute-start(bf16[32,768]{1,0:T(8,128)(2,1)S(1)} %shard_map.55.refs_0_), channel_id=1, source_target_pairs={{6,0},{7,1},{0,2},{1,3},{2,4},{3,5},{4,6},{5,7},{14,8},{15,9},{8,1... | collective-permute-start | bytes 147464 | tf_op jit(solution)/shard_map/ppermute | solution.py:25
  130.8 4.6 %collective-permute-start.2 = (bf16[32,768]{1,0:T(8,128)(2,1)S(1)}, bf16[32,768]{1,0:T(8,128)(2,1)S(1)}, u32[]{:S(2)}, u32[]{:S(2)}) collective-permute-start(bf16[32,768]{1,0:T(8,128)(2,1)S(1)} %shard_map.55.refs_0_), channel_id=1, source_target_pairs={{5,0},{6,1},{7,2},{0,3},{1,4},{2,5},{3,6},{4,7},{13,8},{14,9},{15,... | collective-permute-start | bytes 147464 | tf_op jit(solution)/shard_map/ppermute | solution.py:25
  135.4 4.3 %collective-permute-start.3 = (bf16[32,768]{1,0:T(8,128)(2,1)S(1)}, bf16[32,768]{1,0:T(8,128)(2,1)S(1)}, u32[]{:S(2)}, u32[]{:S(2)}) collective-permute-start(bf16[32,768]{1,0:T(8,128)(2,1)S(1)} %shard_map.55.refs_0_), channel_id=1, source_target_pairs={{4,0},{5,1},{6,2},{7,3},{0,4},{1,5},{2,6},{3,7},{12,8},{13,9},{14,... | collective-permute-start | bytes 147464 | tf_op jit(solution)/shard_map/ppermute | solution.py:25
  139.6 4.6 %collective-permute-start.4 = (bf16[32,768]{1,0:T(8,128)(2,1)S(1)}, bf16[32,768]{1,0:T(8,128)(2,1)S(1)}, u32[]{:S(2)}, u32[]{:S(2)}) collective-permute-start(bf16[32,768]{1,0:T(8,128)(2,1)S(1)} %shard_map.55.refs_0_), channel_id=1, source_target_pairs={{3,0},{4,1},{5,2},{6,3},{7,4},{0,5},{1,6},{2,7},{11,8},{12,9},{13,... | collective-permute-start | bytes 147464 | tf_op jit(solution)/shard_map/ppermute | solution.py:25
  144.2 74.8 %collective-permute-done.refs_1_ = bf16[32,768]{1,0:T(8,128)(2,1)S(1)} collective-permute-done((bf16[32,768]{1,0:T(8,128)(2,1)S(1)}, bf16[32,768]{1,0:T(8,128)(2,1)S(1)}, u32[]{:S(2)}, u32[]{:S(2)}) %collective-permute-start) | collective-permute-done | bytes 49184 | tf_op jit(solution)/shard_map/ppermute | solution.py:25
  219.1 1.9 collective-permute-start.5
  221.0 0.8 collective-permute-done.1.refs_2_
  221.8 5.3 %collective-permute-start.6 = (bf16[32,768]{1,0:T(8,128)(2,1)S(1)}, bf16[32,768]{1,0:T(8,128)(2,1)S(1)}, u32[]{:S(2)}, u32[]{:S(2)}) collective-permute-start(bf16[32,768]{1,0:T(8,128)(2,1)S(1)} %shard_map.55.refs_0_), channel_id=1, source_target_pairs={{1,0},{2,1},{3,2},{4,3},{5,4},{6,5},{7,6},{0,7},{9,8},{10,9},{11,1... | collective-permute-start | bytes 147464 | tf_op jit(solution)/shard_map/ppermute | solution.py:25
  227.2 0.0 collective-permute-done.2.refs_3_
  227.2 0.7 collective-permute-done.3.refs_4_
  227.9 0.0 collective-permute-done.4.refs_5_
  227.9 0.0 collective-permute-done.5.refs_6_
  227.9 1.0 collective-permute-done.6.refs_7_
  228.9 0.1 shard_map.56
  229.0 4.2 %collective-permute-start.7 = (bf16[256,768]{1,0:T(8,128)(2,1)S(1)}, bf16[256,768]{1,0:T(8,128)(2,1)S(1)}, u32[]{:S(2)}, u32[]{:S(2)}) collective-permute-start(bf16[256,768]{1,0:T(8,128)(2,1)S(1)} %get-tuple-element.7.refs_0_), channel_id=1, source_target_pairs={{8,0},{9,1},{10,2},{11,3},{12,4},{13,5},{14,6},{15,7},{16,8},{17,9... | collective-permute-start | bytes 1179656 | tf_op jit(solution)/shard_map/ppermute | solution.py:25
  233.2 2.6 collective-permute-start.8
  235.8 3.0 %collective-permute-start.9 = (bf16[256,512]{1,0:T(8,128)(2,1)S(1)}, bf16[256,512]{1,0:T(8,128)(2,1)S(1)}, u32[]{:S(2)}, u32[]{:S(2)}) collective-permute-start(bf16[256,512]{1,0:T(8,128)(2,1)S(1)} %get-tuple-element.8), channel_id=1, source_target_pairs={{24,0},{25,1},{26,2},{27,3},{28,4},{29,5},{30,6},{31,7},{0,8},{1,9... | collective-permute-start | bytes 786440 | tf_op jit(solution)/shard_map/ppermute | solution.py:25
  238.9 6.9 %collective-permute-done.8.refs_2_ = bf16[256,512]{1,0:T(8,128)(2,1)S(1)} collective-permute-done((bf16[256,512]{1,0:T(8,128)(2,1)S(1)}, bf16[256,512]{1,0:T(8,128)(2,1)S(1)}, u32[]{:S(2)}, u32[]{:S(2)}) %collective-permute-start.8) | collective-permute-done | bytes 262176 | tf_op jit(solution)/shard_map/ppermute | solution.py:25
  245.8 3.1 %collective-permute-done.9.refs_3_ = bf16[256,512]{1,0:T(8,128)(2,1)S(1)} collective-permute-done((bf16[256,512]{1,0:T(8,128)(2,1)S(1)}, bf16[256,512]{1,0:T(8,128)(2,1)S(1)}, u32[]{:S(2)}, u32[]{:S(2)}) %collective-permute-start.9) | collective-permute-done | bytes 262176 | tf_op jit(solution)/shard_map/ppermute | solution.py:25
  248.9 2.6 shard_map.59.rest_ref
  251.5 1.0 copy-done.1
  252.6 6.4 %shard_map.58.most_ref = bf16[12,128,1024]{2,1,0:T(8,128)(2,1)S(1)} custom-call(s32[1]{0:T(128)} %bitcast.me_ref, bf16[256,768]{1,0:T(8,128)(2,1)S(1)} %get-tuple-element.7.refs_0_, bf16[256,768]{1,0:T(8,128)(2,1)S(1)} %collective-permute-done.7.refs_1_, bf16[256,512]{1,0:T(8,128)(2,1)S(1)} %collective-permute-done.8.refs_2_, ...), custom_call_target="tpu_custom_call" | custom-call | flops 3221225472 | bytes 8388608 | tf_op jit(solution)/shard_map/pallas_call | solution.py:117
  258.9 3.1 %shard_map.60 = f32[4,128,128]{2,1,0:T(8,128)S(1)} custom-call(bf16[12,128,1024]{2,1,0:T(8,128)(2,1)S(1)} %shard_map.58.most_ref, bf16[4,128,1024]{2,1,0:T(8,128)(2,1)} %copy-done.1, bf16[32,16,32,128]{3,2,1,0:T(8,128)(2,1)} %all-to-all-done.1.half_ref), custom_call_target="tpu_custom_call" | custom-call | flops 536870912 | bytes 8388608 | tf_op jit(solution)/shard_map/pallas_call | solution.py:180
  262.1 9.1 %all_to_all.20 = f32[4,128,128]{2,1,0:T(8,128)S(1)} all-to-all(f32[4,128,128]{2,1,0:T(8,128)S(1)} %shard_map.60), channel_id=1, replica_groups={{0,8,16,24},{1,9,17,25},{2,10,18,26},{3,11,19,27},{4,12,20,28},{5,13,21..., dimensions={0} | all-to-all | bytes 524288 | tf_op jit(solution)/shard_map/all_to_all | solution.py:34
  271.2 14.0 %all_to_all.21 = bf16[8,128,128]{2,1,0:T(8,128)(2,1)S(1)} all-to-all(bf16[8,128,128]{2,1,0:T(8,128)(2,1)S(1)} %broadcast_in_dim.34), channel_id=1, replica_groups={{0,1,2,3,4,5,6,7},{8,9,10,11,12,13,14,15},{16,17,18,19,20,21,22,23},{24..., dimensions={0} | all-to-all | bytes 524288 | tf_op jit(solution)/shard_map/all_to_all | solution.py:34
  285.2 0.7 convert_reduce_fusion
  (23 shorter events, 0.2 us)
Async XLA Ops:
  0.0 29.5 %copy-start = (s32[16,4]{0,1:T(4,128)S(1)}, s32[16,4]{0,1:T(4,128)}, u32[]{:S(2)}) copy-start(s32[16,4]{0,1:T(4,128)} %param.8) | copy-start | bytes 772
  7.1 13.4 %copy-start.3 = (bf16[1,4,128,128]{3,2,1,0:T(8,128)(2,1)S(1)}, bf16[1,4,128,128]{3,2,1,0:T(8,128)(2,1)}, u32[]{:S(2)}) copy-start(bf16[1,4,128,128]{3,2,1,0:T(8,128)(2,1)} %param.6) | copy-start | bytes 393220
  7.1 22.3 %copy-start.4 = (s32[16,4]{0,1:T(4,128)S(1)}, s32[16,4]{0,1:T(4,128)}, u32[]{:S(2)}) copy-start(s32[16,4]{0,1:T(4,128)} %param.7) | copy-start | bytes 772
  7.1 110.4 %all-to-all-start = ((bf16[32,16,32,128]{3,2,1,0:T(8,128)(2,1)}), bf16[32,16,32,128]{3,2,1,0:T(8,128)(2,1)}, u32[]{:S(2)}, u32[]{:S(2)}) async-start(bf16[32,16,32,128]{3,2,1,0:T(8,128)(2,1)} %bitcast.35), calls=%async_computation | async-start | bytes 8388608 | tf_op jit(solution)/shard_map/all_to_all | solution.py:244
  20.6 9.8 %collective-permute-start.10 = (bf16[1,4,128,128]{3,2,1,0:T(8,128)(2,1)S(1)}, bf16[1,4,128,128]{3,2,1,0:T(8,128)(2,1)S(1)}, u32[]{:S(2)}, u32[]{:S(2)}) collective-permute-start(bf16[1,4,128,128]{3,2,1,0:T(8,128)(2,1)S(1)} %copy-done.3), channel_id=1, source_target_pairs={{448,0},{480,32},{0,64},{32,96},{64,128},{96,160},{128,192},{160,2... | collective-permute-start | bytes 393224 | tf_op jit(solution)/shard_map/ppermute | solution.py:16
  23.2 7.2 %collective-permute-start.11 = (bf16[1,4,128,128]{3,2,1,0:T(8,128)(2,1)S(1)}, bf16[1,4,128,128]{3,2,1,0:T(8,128)(2,1)S(1)}, u32[]{:S(2)}, u32[]{:S(2)}) collective-permute-start(bf16[1,4,128,128]{3,2,1,0:T(8,128)(2,1)S(1)} %copy-done.3), channel_id=1, source_target_pairs={{480,0},{0,32},{32,64},{64,96},{96,128},{128,160},{160,192},{192,2... | collective-permute-start | bytes 393224 | tf_op jit(solution)/shard_map/ppermute | solution.py:16
  23.2 7.3 %collective-permute-start.12 = (bf16[1,4,128,128]{3,2,1,0:T(8,128)(2,1)S(1)}, bf16[1,4,128,128]{3,2,1,0:T(8,128)(2,1)S(1)}, u32[]{:S(2)}, u32[]{:S(2)}) collective-permute-start(bf16[1,4,128,128]{3,2,1,0:T(8,128)(2,1)S(1)} %copy-done.3), channel_id=1, source_target_pairs={{32,0},{64,32},{96,64},{128,96},{160,128},{192,160},{224,192},{256... | collective-permute-start | bytes 393224 | tf_op jit(solution)/shard_map/ppermute | solution.py:16
  26.2 6.8 %collective-permute-start.13 = (bf16[1,4,128,128]{3,2,1,0:T(8,128)(2,1)S(1)}, bf16[1,4,128,128]{3,2,1,0:T(8,128)(2,1)S(1)}, u32[]{:S(2)}, u32[]{:S(2)}) collective-permute-start(bf16[1,4,128,128]{3,2,1,0:T(8,128)(2,1)S(1)} %copy-done.3), channel_id=1, source_target_pairs={{64,0},{96,32},{128,64},{160,96},{192,128},{224,160},{256,192},{28... | collective-permute-start | bytes 393224 | tf_op jit(solution)/shard_map/ppermute | solution.py:16
  117.6 5.2 %copy-start.2 = (bf16[1,32,1024]{2,1,0:T(8,128)(2,1)S(1)}, bf16[1,32,1024]{2,1,0:T(8,128)(2,1)}, u32[]{:S(2)}) copy-start(bf16[1,32,1024]{2,1,0:T(8,128)(2,1)} %param.9) | copy-start | bytes 196612
  117.6 141.3 %all-to-all-start.1 = ((bf16[32,16,32,128]{3,2,1,0:T(8,128)(2,1)}), bf16[32,16,32,128]{3,2,1,0:T(8,128)(2,1)}, u32[]{:S(2)}, u32[]{:S(2)}) async-start(bf16[32,16,32,128]{3,2,1,0:T(8,128)(2,1)} %bitcast.34), calls=%async_computation.1 | async-start | bytes 8388608 | tf_op jit(solution)/shard_map/all_to_all | solution.py:244
  122.8 96.2 %collective-permute-start = (bf16[32,768]{1,0:T(8,128)(2,1)S(1)}, bf16[32,768]{1,0:T(8,128)(2,1)S(1)}, u32[]{:S(2)}, u32[]{:S(2)}) collective-permute-start(bf16[32,768]{1,0:T(8,128)(2,1)S(1)} %shard_map.55.refs_0_), channel_id=1, source_target_pairs={{7,0},{0,1},{1,2},{2,3},{3,4},{4,5},{5,6},{6,7},{15,8},{8,9},{9,10... | collective-permute-start | bytes 147464 | tf_op jit(solution)/shard_map/ppermute | solution.py:25
  126.5 95.4 %collective-permute-start.1 = (bf16[32,768]{1,0:T(8,128)(2,1)S(1)}, bf16[32,768]{1,0:T(8,128)(2,1)S(1)}, u32[]{:S(2)}, u32[]{:S(2)}) collective-permute-start(bf16[32,768]{1,0:T(8,128)(2,1)S(1)} %shard_map.55.refs_0_), channel_id=1, source_target_pairs={{6,0},{7,1},{0,2},{1,3},{2,4},{3,5},{4,6},{5,7},{14,8},{15,9},{8,1... | collective-permute-start | bytes 147464 | tf_op jit(solution)/shard_map/ppermute | solution.py:25
  130.8 96.4 %collective-permute-start.2 = (bf16[32,768]{1,0:T(8,128)(2,1)S(1)}, bf16[32,768]{1,0:T(8,128)(2,1)S(1)}, u32[]{:S(2)}, u32[]{:S(2)}) collective-permute-start(bf16[32,768]{1,0:T(8,128)(2,1)S(1)} %shard_map.55.refs_0_), channel_id=1, source_target_pairs={{5,0},{6,1},{7,2},{0,3},{1,4},{2,5},{3,6},{4,7},{13,8},{14,9},{15,... | collective-permute-start | bytes 147464 | tf_op jit(solution)/shard_map/ppermute | solution.py:25
  135.4 92.5 %collective-permute-start.3 = (bf16[32,768]{1,0:T(8,128)(2,1)S(1)}, bf16[32,768]{1,0:T(8,128)(2,1)S(1)}, u32[]{:S(2)}, u32[]{:S(2)}) collective-permute-start(bf16[32,768]{1,0:T(8,128)(2,1)S(1)} %shard_map.55.refs_0_), channel_id=1, source_target_pairs={{4,0},{5,1},{6,2},{7,3},{0,4},{1,5},{2,6},{3,7},{12,8},{13,9},{14,... | collective-permute-start | bytes 147464 | tf_op jit(solution)/shard_map/ppermute | solution.py:25
  139.6 88.3 %collective-permute-start.4 = (bf16[32,768]{1,0:T(8,128)(2,1)S(1)}, bf16[32,768]{1,0:T(8,128)(2,1)S(1)}, u32[]{:S(2)}, u32[]{:S(2)}) collective-permute-start(bf16[32,768]{1,0:T(8,128)(2,1)S(1)} %shard_map.55.refs_0_), channel_id=1, source_target_pairs={{3,0},{4,1},{5,2},{6,3},{7,4},{0,5},{1,6},{2,7},{11,8},{12,9},{13,... | collective-permute-start | bytes 147464 | tf_op jit(solution)/shard_map/ppermute | solution.py:25
  219.1 8.8 %collective-permute-start.5 = (bf16[32,768]{1,0:T(8,128)(2,1)S(1)}, bf16[32,768]{1,0:T(8,128)(2,1)S(1)}, u32[]{:S(2)}, u32[]{:S(2)}) collective-permute-start(bf16[32,768]{1,0:T(8,128)(2,1)S(1)} %shard_map.55.refs_0_), channel_id=1, source_target_pairs={{2,0},{3,1},{4,2},{5,3},{6,4},{7,5},{0,6},{1,7},{10,8},{11,9},{12,... | collective-permute-start | bytes 147464 | tf_op jit(solution)/shard_map/ppermute | solution.py:25
  221.8 7.1 %collective-permute-start.6 = (bf16[32,768]{1,0:T(8,128)(2,1)S(1)}, bf16[32,768]{1,0:T(8,128)(2,1)S(1)}, u32[]{:S(2)}, u32[]{:S(2)}) collective-permute-start(bf16[32,768]{1,0:T(8,128)(2,1)S(1)} %shard_map.55.refs_0_), channel_id=1, source_target_pairs={{1,0},{2,1},{3,2},{4,3},{5,4},{6,5},{7,6},{0,7},{9,8},{10,9},{11,1... | collective-permute-start | bytes 147464 | tf_op jit(solution)/shard_map/ppermute | solution.py:25
  229.0 19.9 %collective-permute-start.7 = (bf16[256,768]{1,0:T(8,128)(2,1)S(1)}, bf16[256,768]{1,0:T(8,128)(2,1)S(1)}, u32[]{:S(2)}, u32[]{:S(2)}) collective-permute-start(bf16[256,768]{1,0:T(8,128)(2,1)S(1)} %get-tuple-element.7.refs_0_), channel_id=1, source_target_pairs={{8,0},{9,1},{10,2},{11,3},{12,4},{13,5},{14,6},{15,7},{16,8},{17,9... | collective-permute-start | bytes 1179656 | tf_op jit(solution)/shard_map/ppermute | solution.py:25
  233.2 12.6 %collective-permute-start.8 = (bf16[256,512]{1,0:T(8,128)(2,1)S(1)}, bf16[256,512]{1,0:T(8,128)(2,1)S(1)}, u32[]{:S(2)}, u32[]{:S(2)}) collective-permute-start(bf16[256,512]{1,0:T(8,128)(2,1)S(1)} %get-tuple-element.8), channel_id=1, source_target_pairs={{16,0},{17,1},{18,2},{19,3},{20,4},{21,5},{22,6},{23,7},{24,8},{25... | collective-permute-start | bytes 786440 | tf_op jit(solution)/shard_map/ppermute | solution.py:25
  235.8 13.1 %collective-permute-start.9 = (bf16[256,512]{1,0:T(8,128)(2,1)S(1)}, bf16[256,512]{1,0:T(8,128)(2,1)S(1)}, u32[]{:S(2)}, u32[]{:S(2)}) collective-permute-start(bf16[256,512]{1,0:T(8,128)(2,1)S(1)} %get-tuple-element.8), channel_id=1, source_target_pairs={{24,0},{25,1},{26,2},{27,3},{28,4},{29,5},{30,6},{31,7},{0,8},{1,9... | collective-permute-start | bytes 786440 | tf_op jit(solution)/shard_map/ppermute | solution.py:25
  251.5 1.0 copy-start.1

commit v9 on v8

--- a/solution.py
+++ b/solution.py
@@ -150,36 +150,33 @@
     copies.append(pltpu.make_async_copy(rest_ref, rest_buf, sems.at[chunks]))
     for copy in copies:
         copy.start()
+    kept = most_ref.shape[0]
     total = jnp.zeros((cols, cols), jnp.float32)
     for c in range(chunks):
         copies[c].wait()
-        if c == chunks - 1:
+        slots = range(width * c, width * (c + 1))
+        if kept in slots:
             copies[chunks].wait()
-        for w in range(0, width, 2):
-            slots = (w, w + 1)
-            if c < chunks - 1:
-                lefts = [most_ref[width * c + v] for v in slots]
-            else:
-                lefts = [rest_buf[v] for v in slots]
-            rights = [half_buf[c, :, v].reshape(parts * depth, cols) for v in slots]
-            both = jnp.dot(
-                jnp.concatenate(lefts, axis=0), jnp.concatenate(rights, axis=1),
-                preferred_element_type=jnp.float32,
-            )
-            total += both[:cols, :cols] + both[cols:, cols:]
-    done = total.T
+        lefts = [most_ref[s] if s < kept else rest_buf[s - kept] for s in slots]
+        rights = [half_buf[c, :, v].reshape(parts * depth, cols) for v in range(width)]
+        both = jnp.dot(
+            jnp.concatenate(lefts, axis=0), jnp.concatenate(rights, axis=1),
+            preferred_element_type=jnp.float32,
+        )
+        total += both[:cols, :cols] + both[cols:, cols:]
+    done = total.T.astype(out_ref.dtype)
     for k in range(out_ref.shape[0]):
         out_ref[k] = done
 
 
 def close(most, rest, half):
     parts, slots, depth, cols = half.shape
-    width = rest.shape[0]
+    width = 2
     chunks = slots // width
     vmem, hbm = pltpu.VMEM, pltpu.HBM
     return pl.pallas_call(
         close_kernel,
-        out_shape=jax.ShapeDtypeStruct((X_LEN, cols, cols), jnp.float32),
+        out_shape=jax.ShapeDtypeStruct((Z_LEN, cols, cols), half.dtype),
         in_specs=[pl.BlockSpec(memory_space=space) for space in (vmem, hbm, hbm)],
         out_specs=pl.BlockSpec(memory_space=vmem),
         scratch_shapes=[
@@ -196,19 +193,38 @@
     )(most, *(pltpu.with_memory_space_constraint(x, hbm) for x in (rest, half)))
 
 
-def swap_kernel(in_ref, out_ref):
-    out_ref[...] = jnp.swapaxes(in_ref[...], 0, 1)
-
-
-def slot_major(array, width):
+def swap_kernel(in_ref, out_ref, in_buf, out_buf, in_sems, out_sems):
+    chunks, _, width, _ = in_buf.shape
+    reads, writes = [], []
+    for c in range(chunks):
+        slots = pl.ds(c * width, width)
+        reads.append(pltpu.make_async_copy(in_ref.at[:, slots], in_buf.at[c], in_sems.at[c]))
+        writes.append(pltpu.make_async_copy(out_buf.at[c], out_ref.at[slots], out_sems.at[c]))
+    for read in reads:
+        read.start()
+    for c in range(chunks):
+        reads[c].wait()
+        out_buf[c] = jnp.swapaxes(in_buf[c], 0, 1)
+        writes[c].start()
+    for write in writes:
+        write.wait()
+
+
+def slot_major(array, chunks):
     count, slots, cols = array.shape
+    width = slots // chunks
     return pl.pallas_call(
         swap_kernel,
         out_shape=pltpu.HBM((slots, count, cols), array.dtype),
-        grid=(slots // width,),
-        in_specs=[pl.BlockSpec((count, width, cols), lambda i: (0, i, 0))],
-        out_specs=pl.BlockSpec((width, count, cols), lambda i: (i, 0, 0)),
-        compiler_params=pltpu.CompilerParams(vmem_limit_bytes=8 << 20),
+        in_specs=[pl.BlockSpec(memory_space=pltpu.HBM)],
+        out_specs=pl.BlockSpec(memory_space=pltpu.HBM),
+        scratch_shapes=[
+            pltpu.VMEM((chunks, count, width, cols), array.dtype),
+            pltpu.VMEM((chunks, width, count, cols), array.dtype),
+            pltpu.SemaphoreType.DMA((chunks,)),
+            pltpu.SemaphoreType.DMA((chunks,)),
+        ],
+        compiler_params=pltpu.CompilerParams(vmem_limit_bytes=16 << 20),
         cost_estimate=pl.CostEstimate(
             flops=0, bytes_accessed=4 * array.size, transcendentals=0,
         ),
@@ -249,7 +265,7 @@
     cols = ints.shape[2]
     count, side = rows.shape[0], rows.shape[1] // X_LEN
     me = lax.axis_index("aux")[None]
-    ints_out = slot_major(ints, 64)
+    ints_out = slot_major(ints, 16)
     group = lax.axis_size("aux")
     ints_moved = exchanged(ints_out.reshape(group, -1, count, cols))
     kept, = in_vmem(metric_kernel, [(count, 3 * side)], me, rows)
@@ -263,10 +279,9 @@
     most = 3 * ints_moved.shape[1] // 4
     rest = fit(parts, me, ints_moved, most, ints_moved.shape[1] - most)
     shares = close(fit(parts, me, ints_moved, 0, most), rest, half_moved)
-    shares = jnp.sum(to_all(shares, "x"), axis=0).astype(jnp.bfloat16)
-    shares = jnp.broadcast_to(shares[None], (Z_LEN, cols, cols))
-    shares = to_all(shares, "z").astype(jnp.float32)
-    return jnp.sum(shares, axis=0)[None]
+    shares = jnp.sum(to_all(shares, "z").astype(jnp.float32), axis=0)
+    shares = jnp.broadcast_to(shares[None], (X_LEN, cols, cols))
+    return jnp.sum(to_all(shares, "x"), axis=0)[None]
 
 
 def solution(mesh):

time: 287 us -> 286 us (level)
  the two profiles are of different devices: /device:TPU:32 before, /device:TPU:56 now
where the time goes in v9:
time: 286 us; the launch traced here: 285 us
  waiting for transfers between devices  165 us (58%)
  starting transfers between devices  64.9 us (23%)
  blocking collectives  24.1 us (8%)
  Pallas kernels  17.5 us (6%)
  local copies, waits for them, and re-layouts  7.31 us (3%)
  matrix products  5.11 us (2%)
    ppermute x10, waiting for transfers between devices, from_grid(): return lax.ppermute(block, 'aux', route)  87.3 us
    all_to_all x2, waiting for transfers between devices, exchanged(): return lax.all_to_all(array, 'aux', split_axis=0, concat_axis=0, tiled=True)  74.4 us
    ppermute x10, starting transfers between devices, from_grid(): return lax.ppermute(block, 'aux', route)  38.6 us
    all_to_all x2, blocking collectives, to_all(): lax.all_to_all(copies, 'aux', split_axis=0, concat_axis=0, tiled=True, ax...  24.1 us
    all_to_all x2, starting transfers between devices, exchanged(): return lax.all_to_all(array, 'aux', split_axis=0, concat_axis=0, tiled=True)  18.7 us
    pallas_call x2, Pallas kernels, fit(): pl.pallas_call(fit_kernel, out_shape=jax.ShapeDtypeStruct((slots, cols, r...  8.98 us
    ppermute x4, starting transfers between devices, passed_along(): return lax.ppermute(block, axis, route)  7.58 us
  transfers between devices with their start and end apart: 16, of which 8 were waited for; matrix products, arithmetic and copies ran while one was open for 4% of the time, Pallas kernels for 3%

profile of v9, /device:TPU:56, one launch (start us, length us, event | category | flops | bytes accessed | tf_op | source)
XLA Modules:
  0.0 285.1 jit_solution(4968204535665098829)
XLA Ops:
  0.0 3.8 %shard_map.57 = bf16[512,32,128]{2,1,0:T(8,128)(2,1)} custom-call(bf16[32,512,128]{2,1,0:T(8,128)(2,1)} %bitcast.36), custom_call_target="tpu_custom_call" | custom-call | bytes 8388608 | tf_op jit(solution)/shard_map/pallas_call | solution.py:216
  3.8 0.0 copy-start.3
  3.9 0.0 copy-start.4
  3.9 13.4 %all-to-all-start = ((bf16[32,16,32,128]{3,2,1,0:T(8,128)(2,1)}), bf16[32,16,32,128]{3,2,1,0:T(8,128)(2,1)}, u32[]{:S(2)}, u32[]{:S(2)}) async-start(bf16[32,16,32,128]{3,2,1,0:T(8,128)(2,1)} %bitcast.35), calls=%async_computation | async-start | bytes 8388608 | tf_op jit(solution)/shard_map/all_to_all | solution.py:260
  17.3 1.9 collective-permute-start.10
  19.3 0.0 collective-permute-start.11
  19.3 1.7 collective-permute-start.12
  21.0 3.9 %collective-permute-start.13 = (bf16[1,4,128,128]{3,2,1,0:T(8,128)(2,1)S(1)}, bf16[1,4,128,128]{3,2,1,0:T(8,128)(2,1)S(1)}, u32[]{:S(2)}, u32[]{:S(2)}) collective-permute-start(bf16[1,4,128,128]{3,2,1,0:T(8,128)(2,1)S(1)} %copy-done.3), channel_id=1, source_target_pairs={{64,0},{96,32},{128,64},{160,96},{192,128},{224,160},{256,192},{28... | collective-permute-start | bytes 393224 | tf_op jit(solution)/shard_map/ppermute | solution.py:16
  25.0 0.1 copy.10
  25.0 0.2 dynamic-slice_reduce_fusion
  25.3 0.6 gather_fusion.1
  25.8 0.1 broadcast_select_fusion.1
  25.9 0.0 collective-permute-done.10
  25.9 0.0 collective-permute-done.11
  26.0 3.3 %collective-permute-done.13 = bf16[1,4,128,128]{3,2,1,0:T(8,128)(2,1)S(1)} collective-permute-done((bf16[1,4,128,128]{3,2,1,0:T(8,128)(2,1)S(1)}, bf16[1,4,128,128]{3,2,1,0:T(8,128)(2,1)S(1)}, u32[]{:S(2)}, u32[]{:S(2)}) %collective-permute-start.13) | collective-permute-done | bytes 131104 | tf_op jit(solution)/shard_map/ppermute | solution.py:16
  29.3 0.6 gather_fusion
  30.0 0.1 broadcast_select_fusion
  30.1 0.5 convolution_convert_fusion.1
  30.7 4.6 %convolution_convert_fusion = bf16[512,32,128]{2,0,1:T(8,128)(2,1)S(1)} fusion(bf16[64,8,4,128]{3,2,1,0:T(4,128)(2,1)S(1)} %bitcast.37, bf16[1,32,512,128]{3,2,1,0:T(8,128)(2,1)} %param.5), kind=kOutput, calls=%fused_computation.2 | convolution fusion | flops 2149580800 | bytes 8912896 | tf_op jit(solution)/shard_map/ls,plm->psm/dot_general | solution.py:274
  35.2 4.7 %copy.13 = bf16[512,32,128]{2,1,0:T(8,128)(2,1)} copy(bf16[512,32,128]{2,0,1:T(8,128)(2,1)S(1)} %convolution_convert_fusion) | data formatting | bytes 8388608 | tf_op jit(solution)/shard_map/convert_element_type | solution.py:275
  39.9 74.4 %all-to-all-done.refs_4_ = bf16[32,16,32,128]{3,2,1,0:T(8,128)(2,1)} async-done(((bf16[32,16,32,128]{3,2,1,0:T(8,128)(2,1)}), bf16[32,16,32,128]{3,2,1,0:T(8,128)(2,1)}, u32[]{:S(2)}, u32[]{:S(2)}) %all-to-all-start) | async-done | bytes 4194336 | tf_op jit(solution)/shard_map/all_to_all | solution.py:260
  114.3 5.2 %all-to-all-start.1 = ((bf16[32,16,32,128]{3,2,1,0:T(8,128)(2,1)}), bf16[32,16,32,128]{3,2,1,0:T(8,128)(2,1)}, u32[]{:S(2)}, u32[]{:S(2)}) async-start(bf16[32,16,32,128]{3,2,1,0:T(8,128)(2,1)} %bitcast.34), calls=%async_computation.1 | async-start | bytes 8388608 | tf_op jit(solution)/shard_map/all_to_all | solution.py:260
  119.6 3.6 %collective-permute-start = (bf16[32,768]{1,0:T(8,128)(2,1)S(1)}, bf16[32,768]{1,0:T(8,128)(2,1)S(1)}, u32[]{:S(2)}, u32[]{:S(2)}) collective-permute-start(bf16[32,768]{1,0:T(8,128)(2,1)S(1)} %shard_map.55.refs_0_), channel_id=1, source_target_pairs={{7,0},{0,1},{1,2},{2,3},{3,4},{4,5},{5,6},{6,7},{15,8},{8,9},{9,10... | collective-permute-start | bytes 147464 | tf_op jit(solution)/shard_map/ppermute | solution.py:25
  123.2 4.3 %collective-permute-start.1 = (bf16[32,768]{1,0:T(8,128)(2,1)S(1)}, bf16[32,768]{1,0:T(8,128)(2,1)S(1)}, u32[]{:S(2)}, u32[]{:S(2)}) collective-permute-start(bf16[32,768]{1,0:T(8,128)(2,1)S(1)} %shard_map.55.refs_0_), channel_id=1, source_target_pairs={{6,0},{7,1},{0,2},{1,3},{2,4},{3,5},{4,6},{5,7},{14,8},{15,9},{8,1... | collective-permute-start | bytes 147464 | tf_op jit(solution)/shard_map/ppermute | solution.py:25
  127.5 4.6 %collective-permute-start.2 = (bf16[32,768]{1,0:T(8,128)(2,1)S(1)}, bf16[32,768]{1,0:T(8,128)(2,1)S(1)}, u32[]{:S(2)}, u32[]{:S(2)}) collective-permute-start(bf16[32,768]{1,0:T(8,128)(2,1)S(1)} %shard_map.55.refs_0_), channel_id=1, source_target_pairs={{5,0},{6,1},{7,2},{0,3},{1,4},{2,5},{3,6},{4,7},{13,8},{14,9},{15,... | collective-permute-start | bytes 147464 | tf_op jit(solution)/shard_map/ppermute | solution.py:25
  132.1 4.3 %collective-permute-start.3 = (bf16[32,768]{1,0:T(8,128)(2,1)S(1)}, bf16[32,768]{1,0:T(8,128)(2,1)S(1)}, u32[]{:S(2)}, u32[]{:S(2)}) collective-permute-start(bf16[32,768]{1,0:T(8,128)(2,1)S(1)} %shard_map.55.refs_0_), channel_id=1, source_target_pairs={{4,0},{5,1},{6,2},{7,3},{0,4},{1,5},{2,6},{3,7},{12,8},{13,9},{14,... | collective-permute-start | bytes 147464 | tf_op jit(solution)/shard_map/ppermute | solution.py:25
  136.4 4.6 %collective-permute-start.4 = (bf16[32,768]{1,0:T(8,128)(2,1)S(1)}, bf16[32,768]{1,0:T(8,128)(2,1)S(1)}, u32[]{:S(2)}, u32[]{:S(2)}) collective-permute-start(bf16[32,768]{1,0:T(8,128)(2,1)S(1)} %shard_map.55.refs_0_), channel_id=1, source_target_pairs={{3,0},{4,1},{5,2},{6,3},{7,4},{0,5},{1,6},{2,7},{11,8},{12,9},{13,... | collective-permute-start | bytes 147464 | tf_op jit(solution)/shard_map/ppermute | solution.py:25
  141.0 74.8 %collective-permute-done.refs_1_ = bf16[32,768]{1,0:T(8,128)(2,1)S(1)} collective-permute-done((bf16[32,768]{1,0:T(8,128)(2,1)S(1)}, bf16[32,768]{1,0:T(8,128)(2,1)S(1)}, u32[]{:S(2)}, u32[]{:S(2)}) %collective-permute-start) | collective-permute-done | bytes 49184 | tf_op jit(solution)/shard_map/ppermute | solution.py:25
  215.8 1.9 collective-permute-start.5
  217.7 0.8 collective-permute-done.1.refs_2_
  218.6 5.3 %collective-permute-start.6 = (bf16[32,768]{1,0:T(8,128)(2,1)S(1)}, bf16[32,768]{1,0:T(8,128)(2,1)S(1)}, u32[]{:S(2)}, u32[]{:S(2)}) collective-permute-start(bf16[32,768]{1,0:T(8,128)(2,1)S(1)} %shard_map.55.refs_0_), channel_id=1, source_target_pairs={{1,0},{2,1},{3,2},{4,3},{5,4},{6,5},{7,6},{0,7},{9,8},{10,9},{11,1... | collective-permute-start | bytes 147464 | tf_op jit(solution)/shard_map/ppermute | solution.py:25
  223.9 0.0 collective-permute-done.2.refs_3_
  223.9 0.7 collective-permute-done.3.refs_4_
  224.6 1.0 collective-permute-done.6.refs_7_
  225.6 0.1 shard_map.56
  225.7 4.2 %collective-permute-start.7 = (bf16[256,768]{1,0:T(8,128)(2,1)S(1)}, bf16[256,768]{1,0:T(8,128)(2,1)S(1)}, u32[]{:S(2)}, u32[]{:S(2)}) collective-permute-start(bf16[256,768]{1,0:T(8,128)(2,1)S(1)} %get-tuple-element.7.refs_0_), channel_id=1, source_target_pairs={{8,0},{9,1},{10,2},{11,3},{12,4},{13,5},{14,6},{15,7},{16,8},{17,9... | collective-permute-start | bytes 1179656 | tf_op jit(solution)/shard_map/ppermute | solution.py:25
  230.0 2.6 collective-permute-start.8
  232.6 3.2 %collective-permute-start.9 = (bf16[256,512]{1,0:T(8,128)(2,1)S(1)}, bf16[256,512]{1,0:T(8,128)(2,1)S(1)}, u32[]{:S(2)}, u32[]{:S(2)}) collective-permute-start(bf16[256,512]{1,0:T(8,128)(2,1)S(1)} %get-tuple-element.8), channel_id=1, source_target_pairs={{24,0},{25,1},{26,2},{27,3},{28,4},{29,5},{30,6},{31,7},{0,8},{1,9... | collective-permute-start | bytes 786440 | tf_op jit(solution)/shard_map/ppermute | solution.py:25
  235.8 6.8 %collective-permute-done.8.refs_2_ = bf16[256,512]{1,0:T(8,128)(2,1)S(1)} collective-permute-done((bf16[256,512]{1,0:T(8,128)(2,1)S(1)}, bf16[256,512]{1,0:T(8,128)(2,1)S(1)}, u32[]{:S(2)}, u32[]{:S(2)}) %collective-permute-start.8) | collective-permute-done | bytes 262176 | tf_op jit(solution)/shard_map/ppermute | solution.py:25
  242.5 3.1 %collective-permute-done.9.refs_3_ = bf16[256,512]{1,0:T(8,128)(2,1)S(1)} collective-permute-done((bf16[256,512]{1,0:T(8,128)(2,1)S(1)}, bf16[256,512]{1,0:T(8,128)(2,1)S(1)}, u32[]{:S(2)}, u32[]{:S(2)}) %collective-permute-start.9) | collective-permute-done | bytes 262176 | tf_op jit(solution)/shard_map/ppermute | solution.py:25
  245.6 0.0 collective-permute-done.7.refs_1_
  245.6 2.6 shard_map.59.rest_ref
  248.3 1.0 copy-done.1
  249.3 6.4 %shard_map.58.most_ref = bf16[12,128,1024]{2,1,0:T(8,128)(2,1)S(1)} custom-call(s32[1]{0:T(128)} %bitcast.me_ref, bf16[256,768]{1,0:T(8,128)(2,1)S(1)} %get-tuple-element.7.refs_0_, bf16[256,768]{1,0:T(8,128)(2,1)S(1)} %collective-permute-done.7.refs_1_, bf16[256,512]{1,0:T(8,128)(2,1)S(1)} %collective-permute-done.8.refs_2_, ...), custom_call_target="tpu_custom_call" | custom-call | flops 3221225472 | bytes 8388608 | tf_op jit(solution)/shard_map/pallas_call | solution.py:117
  255.7 4.6 %shard_map.60 = bf16[8,128,128]{2,1,0:T(8,128)(2,1)S(1)} custom-call(bf16[12,128,1024]{2,1,0:T(8,128)(2,1)S(1)} %shard_map.58.most_ref, bf16[4,128,1024]{2,1,0:T(8,128)(2,1)} %copy-done.1, bf16[32,16,32,128]{3,2,1,0:T(8,128)(2,1)} %all-to-all-done.1.half_ref), custom_call_target="tpu_custom_call" | custom-call | flops 536870912 | bytes 8388608 | tf_op jit(solution)/shard_map/pallas_call | solution.py:177
  260.3 14.3 %all_to_all.20 = bf16[8,128,128]{2,1,0:T(8,128)(2,1)S(1)} all-to-all(bf16[8,128,128]{2,1,0:T(8,128)(2,1)S(1)} %shard_map.60), channel_id=1, replica_groups={{0,1,2,3,4,5,6,7},{8,9,10,11,12,13,14,15},{16,17,18,19,20,21,22,23},{24..., dimensions={0} | all-to-all | bytes 524288 | tf_op jit(solution)/shard_map/all_to_all | solution.py:34
  274.6 9.8 %all_to_all.21 = f32[4,128,128]{2,1,0:T(8,128)S(1)} all-to-all(f32[4,128,128]{2,1,0:T(8,128)S(1)} %broadcast_in_dim.34), channel_id=1, replica_groups={{0,8,16,24},{1,9,17,25},{2,10,18,26},{3,11,19,27},{4,12,20,28},{5,13,21..., dimensions={0} | all-to-all | bytes 524288 | tf_op jit(solution)/shard_map/all_to_all | solution.py:34
  284.4 0.6 reduce_sum.19
  (23 shorter events, 0.2 us)
Async XLA Ops:
  0.0 25.0 %copy-start = (s32[16,4]{0,1:T(4,128)S(1)}, s32[16,4]{0,1:T(4,128)}, u32[]{:S(2)}) copy-start(s32[16,4]{0,1:T(4,128)} %param.8) | copy-start | bytes 772
  3.8 13.5 %copy-start.3 = (bf16[1,4,128,128]{3,2,1,0:T(8,128)(2,1)S(1)}, bf16[1,4,128,128]{3,2,1,0:T(8,128)(2,1)}, u32[]{:S(2)}) copy-start(bf16[1,4,128,128]{3,2,1,0:T(8,128)(2,1)} %param.6) | copy-start | bytes 393220
  3.9 21.1 %copy-start.4 = (s32[16,4]{0,1:T(4,128)S(1)}, s32[16,4]{0,1:T(4,128)}, u32[]{:S(2)}) copy-start(s32[16,4]{0,1:T(4,128)} %param.7) | copy-start | bytes 772
  3.9 110.4 %all-to-all-start = ((bf16[32,16,32,128]{3,2,1,0:T(8,128)(2,1)}), bf16[32,16,32,128]{3,2,1,0:T(8,128)(2,1)}, u32[]{:S(2)}, u32[]{:S(2)}) async-start(bf16[32,16,32,128]{3,2,1,0:T(8,128)(2,1)} %bitcast.35), calls=%async_computation | async-start | bytes 8388608 | tf_op jit(solution)/shard_map/all_to_all | solution.py:260
  17.3 8.6 %collective-permute-start.10 = (bf16[1,4,128,128]{3,2,1,0:T(8,128)(2,1)S(1)}, bf16[1,4,128,128]{3,2,1,0:T(8,128)(2,1)S(1)}, u32[]{:S(2)}, u32[]{:S(2)}) collective-permute-start(bf16[1,4,128,128]{3,2,1,0:T(8,128)(2,1)S(1)} %copy-done.3), channel_id=1, source_target_pairs={{448,0},{480,32},{0,64},{32,96},{64,128},{96,160},{128,192},{160,2... | collective-permute-start | bytes 393224 | tf_op jit(solution)/shard_map/ppermute | solution.py:16
  19.3 6.7 %collective-permute-start.11 = (bf16[1,4,128,128]{3,2,1,0:T(8,128)(2,1)S(1)}, bf16[1,4,128,128]{3,2,1,0:T(8,128)(2,1)S(1)}, u32[]{:S(2)}, u32[]{:S(2)}) collective-permute-start(bf16[1,4,128,128]{3,2,1,0:T(8,128)(2,1)S(1)} %copy-done.3), channel_id=1, source_target_pairs={{480,0},{0,32},{32,64},{64,96},{96,128},{128,160},{160,192},{192,2... | collective-permute-start | bytes 393224 | tf_op jit(solution)/shard_map/ppermute | solution.py:16
  19.3 6.7 %collective-permute-start.12 = (bf16[1,4,128,128]{3,2,1,0:T(8,128)(2,1)S(1)}, bf16[1,4,128,128]{3,2,1,0:T(8,128)(2,1)S(1)}, u32[]{:S(2)}, u32[]{:S(2)}) collective-permute-start(bf16[1,4,128,128]{3,2,1,0:T(8,128)(2,1)S(1)} %copy-done.3), channel_id=1, source_target_pairs={{32,0},{64,32},{96,64},{128,96},{160,128},{192,160},{224,192},{256... | collective-permute-start | bytes 393224 | tf_op jit(solution)/shard_map/ppermute | solution.py:16
  21.0 8.3 %collective-permute-start.13 = (bf16[1,4,128,128]{3,2,1,0:T(8,128)(2,1)S(1)}, bf16[1,4,128,128]{3,2,1,0:T(8,128)(2,1)S(1)}, u32[]{:S(2)}, u32[]{:S(2)}) collective-permute-start(bf16[1,4,128,128]{3,2,1,0:T(8,128)(2,1)S(1)} %copy-done.3), channel_id=1, source_target_pairs={{64,0},{96,32},{128,64},{160,96},{192,128},{224,160},{256,192},{28... | collective-permute-start | bytes 393224 | tf_op jit(solution)/shard_map/ppermute | solution.py:16
  114.3 5.2 %copy-start.2 = (bf16[1,32,1024]{2,1,0:T(8,128)(2,1)S(1)}, bf16[1,32,1024]{2,1,0:T(8,128)(2,1)}, u32[]{:S(2)}) copy-start(bf16[1,32,1024]{2,1,0:T(8,128)(2,1)} %param.9) | copy-start | bytes 196612
  114.3 141.3 %all-to-all-start.1 = ((bf16[32,16,32,128]{3,2,1,0:T(8,128)(2,1)}), bf16[32,16,32,128]{3,2,1,0:T(8,128)(2,1)}, u32[]{:S(2)}, u32[]{:S(2)}) async-start(bf16[32,16,32,128]{3,2,1,0:T(8,128)(2,1)} %bitcast.34), calls=%async_computation.1 | async-start | bytes 8388608 | tf_op jit(solution)/shard_map/all_to_all | solution.py:260
  119.6 96.2 %collective-permute-start = (bf16[32,768]{1,0:T(8,128)(2,1)S(1)}, bf16[32,768]{1,0:T(8,128)(2,1)S(1)}, u32[]{:S(2)}, u32[]{:S(2)}) collective-permute-start(bf16[32,768]{1,0:T(8,128)(2,1)S(1)} %shard_map.55.refs_0_), channel_id=1, source_target_pairs={{7,0},{0,1},{1,2},{2,3},{3,4},{4,5},{5,6},{6,7},{15,8},{8,9},{9,10... | collective-permute-start | bytes 147464 | tf_op jit(solution)/shard_map/ppermute | solution.py:25
  123.2 95.4 %collective-permute-start.1 = (bf16[32,768]{1,0:T(8,128)(2,1)S(1)}, bf16[32,768]{1,0:T(8,128)(2,1)S(1)}, u32[]{:S(2)}, u32[]{:S(2)}) collective-permute-start(bf16[32,768]{1,0:T(8,128)(2,1)S(1)} %shard_map.55.refs_0_), channel_id=1, source_target_pairs={{6,0},{7,1},{0,2},{1,3},{2,4},{3,5},{4,6},{5,7},{14,8},{15,9},{8,1... | collective-permute-start | bytes 147464 | tf_op jit(solution)/shard_map/ppermute | solution.py:25
  127.5 96.4 %collective-permute-start.2 = (bf16[32,768]{1,0:T(8,128)(2,1)S(1)}, bf16[32,768]{1,0:T(8,128)(2,1)S(1)}, u32[]{:S(2)}, u32[]{:S(2)}) collective-permute-start(bf16[32,768]{1,0:T(8,128)(2,1)S(1)} %shard_map.55.refs_0_), channel_id=1, source_target_pairs={{5,0},{6,1},{7,2},{0,3},{1,4},{2,5},{3,6},{4,7},{13,8},{14,9},{15,... | collective-permute-start | bytes 147464 | tf_op jit(solution)/shard_map/ppermute | solution.py:25
  132.1 92.5 %collective-permute-start.3 = (bf16[32,768]{1,0:T(8,128)(2,1)S(1)}, bf16[32,768]{1,0:T(8,128)(2,1)S(1)}, u32[]{:S(2)}, u32[]{:S(2)}) collective-permute-start(bf16[32,768]{1,0:T(8,128)(2,1)S(1)} %shard_map.55.refs_0_), channel_id=1, source_target_pairs={{4,0},{5,1},{6,2},{7,3},{0,4},{1,5},{2,6},{3,7},{12,8},{13,9},{14,... | collective-permute-start | bytes 147464 | tf_op jit(solution)/shard_map/ppermute | solution.py:25
  136.4 88.3 %collective-permute-start.4 = (bf16[32,768]{1,0:T(8,128)(2,1)S(1)}, bf16[32,768]{1,0:T(8,128)(2,1)S(1)}, u32[]{:S(2)}, u32[]{:S(2)}) collective-permute-start(bf16[32,768]{1,0:T(8,128)(2,1)S(1)} %shard_map.55.refs_0_), channel_id=1, source_target_pairs={{3,0},{4,1},{5,2},{6,3},{7,4},{0,5},{1,6},{2,7},{11,8},{12,9},{13,... | collective-permute-start | bytes 147464 | tf_op jit(solution)/shard_map/ppermute | solution.py:25
  215.8 8.8 %collective-permute-start.5 = (bf16[32,768]{1,0:T(8,128)(2,1)S(1)}, bf16[32,768]{1,0:T(8,128)(2,1)S(1)}, u32[]{:S(2)}, u32[]{:S(2)}) collective-permute-start(bf16[32,768]{1,0:T(8,128)(2,1)S(1)} %shard_map.55.refs_0_), channel_id=1, source_target_pairs={{2,0},{3,1},{4,2},{5,3},{6,4},{7,5},{0,6},{1,7},{10,8},{11,9},{12,... | collective-permute-start | bytes 147464 | tf_op jit(solution)/shard_map/ppermute | solution.py:25
  218.6 7.1 %collective-permute-start.6 = (bf16[32,768]{1,0:T(8,128)(2,1)S(1)}, bf16[32,768]{1,0:T(8,128)(2,1)S(1)}, u32[]{:S(2)}, u32[]{:S(2)}) collective-permute-start(bf16[32,768]{1,0:T(8,128)(2,1)S(1)} %shard_map.55.refs_0_), channel_id=1, source_target_pairs={{1,0},{2,1},{3,2},{4,3},{5,4},{6,5},{7,6},{0,7},{9,8},{10,9},{11,1... | collective-permute-start | bytes 147464 | tf_op jit(solution)/shard_map/ppermute | solution.py:25
  225.7 19.9 %collective-permute-start.7 = (bf16[256,768]{1,0:T(8,128)(2,1)S(1)}, bf16[256,768]{1,0:T(8,128)(2,1)S(1)}, u32[]{:S(2)}, u32[]{:S(2)}) collective-permute-start(bf16[256,768]{1,0:T(8,128)(2,1)S(1)} %get-tuple-element.7.refs_0_), channel_id=1, source_target_pairs={{8,0},{9,1},{10,2},{11,3},{12,4},{13,5},{14,6},{15,7},{16,8},{17,9... | collective-permute-start | bytes 1179656 | tf_op jit(solution)/shard_map/ppermute | solution.py:25
  230.0 12.6 %collective-permute-start.8 = (bf16[256,512]{1,0:T(8,128)(2,1)S(1)}, bf16[256,512]{1,0:T(8,128)(2,1)S(1)}, u32[]{:S(2)}, u32[]{:S(2)}) collective-permute-start(bf16[256,512]{1,0:T(8,128)(2,1)S(1)} %get-tuple-element.8), channel_id=1, source_target_pairs={{16,0},{17,1},{18,2},{19,3},{20,4},{21,5},{22,6},{23,7},{24,8},{25... | collective-permute-start | bytes 786440 | tf_op jit(solution)/shard_map/ppermute | solution.py:25
  232.6 13.1 %collective-permute-start.9 = (bf16[256,512]{1,0:T(8,128)(2,1)S(1)}, bf16[256,512]{1,0:T(8,128)(2,1)S(1)}, u32[]{:S(2)}, u32[]{:S(2)}) collective-permute-start(bf16[256,512]{1,0:T(8,128)(2,1)S(1)} %get-tuple-element.8), channel_id=1, source_target_pairs={{24,0},{25,1},{26,2},{27,3},{28,4},{29,5},{30,6},{31,7},{0,8},{1,9... | collective-permute-start | bytes 786440 | tf_op jit(solution)/shard_map/ppermute | solution.py:25
  248.3 1.0 copy-start.1

commit v10 on v8

--- a/solution.py
+++ b/solution.py
@@ -196,19 +196,38 @@
     )(most, *(pltpu.with_memory_space_constraint(x, hbm) for x in (rest, half)))
 
 
-def swap_kernel(in_ref, out_ref):
-    out_ref[...] = jnp.swapaxes(in_ref[...], 0, 1)
-
-
-def slot_major(array, width):
+def swap_kernel(in_ref, out_ref, in_buf, out_buf, in_sems, out_sems):
+    chunks, _, width, _ = in_buf.shape
+    reads, writes = [], []
+    for c in range(chunks):
+        slots = pl.ds(c * width, width)
+        reads.append(pltpu.make_async_copy(in_ref.at[:, slots], in_buf.at[c], in_sems.at[c]))
+        writes.append(pltpu.make_async_copy(out_buf.at[c], out_ref.at[slots], out_sems.at[c]))
+    for read in reads:
+        read.start()
+    for c in range(chunks):
+        reads[c].wait()
+        out_buf[c] = jnp.swapaxes(in_buf[c], 0, 1)
+        writes[c].start()
+    for write in writes:
+        write.wait()
+
+
+def slot_major(array, chunks):
     count, slots, cols = array.shape
+    width = slots // chunks
     return pl.pallas_call(
         swap_kernel,
         out_shape=pltpu.HBM((slots, count, cols), array.dtype),
-        grid=(slots // width,),
-        in_specs=[pl.BlockSpec((count, width, cols), lambda i: (0, i, 0))],
-        out_specs=pl.BlockSpec((width, count, cols), lambda i: (i, 0, 0)),
-        compiler_params=pltpu.CompilerParams(vmem_limit_bytes=8 << 20),
+        in_specs=[pl.BlockSpec(memory_space=pltpu.HBM)],
+        out_specs=pl.BlockSpec(memory_space=pltpu.HBM),
+        scratch_shapes=[
+            pltpu.VMEM((chunks, count, width, cols), array.dtype),
+            pltpu.VMEM((chunks, width, count, cols), array.dtype),
+            pltpu.SemaphoreType.DMA((chunks,)),
+            pltpu.SemaphoreType.DMA((chunks,)),
+        ],
+        compiler_params=pltpu.CompilerParams(vmem_limit_bytes=16 << 20),
         cost_estimate=pl.CostEstimate(
             flops=0, bytes_accessed=4 * array.size, transcendentals=0,
         ),
@@ -249,7 +268,7 @@
     cols = ints.shape[2]
     count, side = rows.shape[0], rows.shape[1] // X_LEN
     me = lax.axis_index("aux")[None]
-    ints_out = slot_major(ints, 64)
+    ints_out = slot_major(ints, 4)
     group = lax.axis_size("aux")
     ints_moved = exchanged(ints_out.reshape(group, -1, count, cols))
     kept, = in_vmem(metric_kernel, [(count, 3 * side)], me, rows)

time: 287 us -> 283 us (0.986)
  Pallas kernels: 19.3 us -> 15.8 us
    pallas_call x1, Pallas kernels: 7.14 us -> 3.64 us  [slot_major(): pl.pallas_call(swap_kernel, out_shape=pltpu.HBM((slots, count, cols), arr...]
where the time goes in v10:
time: 283 us; the launch traced here: 282 us
  waiting for transfers between devices  164 us (58%)
  starting transfers between devices  65.9 us (23%)
  blocking collectives  23.1 us (8%)
  Pallas kernels  15.8 us (6%)
  local copies, waits for them, and re-layouts  7.32 us (3%)
  matrix products  5.11 us (2%)
    ppermute x10, waiting for transfers between devices, from_grid(): return lax.ppermute(block, 'aux', route)  87.4 us
    all_to_all x2, waiting for transfers between devices, exchanged(): return lax.all_to_all(array, 'aux', split_axis=0, concat_axis=0, tiled=True)  74 us
    ppermute x10, starting transfers between devices, from_grid(): return lax.ppermute(block, 'aux', route)  38.4 us
    all_to_all x2, blocking collectives, to_all(): lax.all_to_all(copies, 'aux', split_axis=0, concat_axis=0, tiled=True, ax...  23.1 us
    all_to_all x2, starting transfers between devices, exchanged(): return lax.all_to_all(array, 'aux', split_axis=0, concat_axis=0, tiled=True)  18.7 us
    pallas_call x2, Pallas kernels, fit(): pl.pallas_call(fit_kernel, out_shape=jax.ShapeDtypeStruct((slots, cols, r...  8.98 us
    ppermute x4, starting transfers between devices, passed_along(): return lax.ppermute(block, axis, route)  8.79 us
  transfers between devices with their start and end apart: 16, of which 8 were waited for; matrix products, arithmetic and copies ran while one was open for 4% of the time, Pallas kernels for 3%

profile of v10, /device:TPU:32, one launch (start us, length us, event | category | flops | bytes accessed | tf_op | source)
XLA Modules:
  0.0 282.4 jit_solution(15515858679430789485)
XLA Ops:
  0.0 3.6 %shard_map.57 = bf16[512,32,128]{2,1,0:T(8,128)(2,1)} custom-call(bf16[32,512,128]{2,1,0:T(8,128)(2,1)} %bitcast.36), custom_call_target="tpu_custom_call" | custom-call | bytes 8388608 | tf_op jit(solution)/shard_map/pallas_call | solution.py:219
  3.6 0.0 copy-start.3
  3.7 0.0 copy-start.4
  3.7 13.4 %all-to-all-start = ((bf16[32,16,32,128]{3,2,1,0:T(8,128)(2,1)}), bf16[32,16,32,128]{3,2,1,0:T(8,128)(2,1)}, u32[]{:S(2)}, u32[]{:S(2)}) async-start(bf16[32,16,32,128]{3,2,1,0:T(8,128)(2,1)} %bitcast.35), calls=%async_computation | async-start | bytes 8388608 | tf_op jit(solution)/shard_map/all_to_all | solution.py:263
  17.1 2.6 collective-permute-start.10
  19.7 0.0 collective-permute-start.11
  19.8 2.9 %collective-permute-start.12 = (bf16[1,4,128,128]{3,2,1,0:T(8,128)(2,1)S(1)}, bf16[1,4,128,128]{3,2,1,0:T(8,128)(2,1)S(1)}, u32[]{:S(2)}, u32[]{:S(2)}) collective-permute-start(bf16[1,4,128,128]{3,2,1,0:T(8,128)(2,1)S(1)} %copy-done.3), channel_id=1, source_target_pairs={{32,0},{64,32},{96,64},{128,96},{160,128},{192,160},{224,192},{256... | collective-permute-start | bytes 393224 | tf_op jit(solution)/shard_map/ppermute | solution.py:16
  22.7 3.2 %collective-permute-start.13 = (bf16[1,4,128,128]{3,2,1,0:T(8,128)(2,1)S(1)}, bf16[1,4,128,128]{3,2,1,0:T(8,128)(2,1)S(1)}, u32[]{:S(2)}, u32[]{:S(2)}) collective-permute-start(bf16[1,4,128,128]{3,2,1,0:T(8,128)(2,1)S(1)} %copy-done.3), channel_id=1, source_target_pairs={{64,0},{96,32},{128,64},{160,96},{192,128},{224,160},{256,192},{28... | collective-permute-start | bytes 393224 | tf_op jit(solution)/shard_map/ppermute | solution.py:16
  26.0 0.1 copy.10
  26.0 0.2 dynamic-slice_reduce_fusion
  26.3 0.6 gather_fusion.1
  26.8 0.1 broadcast_select_fusion.1
  27.0 2.5 collective-permute-done.13
  29.6 0.6 gather_fusion
  30.2 0.1 broadcast_select_fusion
  30.3 0.5 convolution_convert_fusion.1
  30.9 4.6 %convolution_convert_fusion = bf16[512,32,128]{2,0,1:T(8,128)(2,1)S(1)} fusion(bf16[64,8,4,128]{3,2,1,0:T(4,128)(2,1)S(1)} %bitcast.37, bf16[1,32,512,128]{3,2,1,0:T(8,128)(2,1)} %param.5), kind=kOutput, calls=%fused_computation.2 | convolution fusion | flops 2149580800 | bytes 8912896 | tf_op jit(solution)/shard_map/ls,plm->psm/dot_general | solution.py:277
  35.5 4.7 %copy.13 = bf16[512,32,128]{2,1,0:T(8,128)(2,1)} copy(bf16[512,32,128]{2,0,1:T(8,128)(2,1)S(1)} %convolution_convert_fusion) | data formatting | bytes 8388608 | tf_op jit(solution)/shard_map/convert_element_type | solution.py:278
  40.1 74.0 %all-to-all-done.refs_4_ = bf16[32,16,32,128]{3,2,1,0:T(8,128)(2,1)} async-done(((bf16[32,16,32,128]{3,2,1,0:T(8,128)(2,1)}), bf16[32,16,32,128]{3,2,1,0:T(8,128)(2,1)}, u32[]{:S(2)}, u32[]{:S(2)}) %all-to-all-start) | async-done | bytes 4194336 | tf_op jit(solution)/shard_map/all_to_all | solution.py:263
  114.1 5.2 %all-to-all-start.1 = ((bf16[32,16,32,128]{3,2,1,0:T(8,128)(2,1)}), bf16[32,16,32,128]{3,2,1,0:T(8,128)(2,1)}, u32[]{:S(2)}, u32[]{:S(2)}) async-start(bf16[32,16,32,128]{3,2,1,0:T(8,128)(2,1)} %bitcast.34), calls=%async_computation.1 | async-start | bytes 8388608 | tf_op jit(solution)/shard_map/all_to_all | solution.py:263
  119.4 3.6 %collective-permute-start = (bf16[32,768]{1,0:T(8,128)(2,1)S(1)}, bf16[32,768]{1,0:T(8,128)(2,1)S(1)}, u32[]{:S(2)}, u32[]{:S(2)}) collective-permute-start(bf16[32,768]{1,0:T(8,128)(2,1)S(1)} %shard_map.55.refs_0_), channel_id=1, source_target_pairs={{7,0},{0,1},{1,2},{2,3},{3,4},{4,5},{5,6},{6,7},{15,8},{8,9},{9,10... | collective-permute-start | bytes 147464 | tf_op jit(solution)/shard_map/ppermute | solution.py:25
  123.0 4.3 %collective-permute-start.1 = (bf16[32,768]{1,0:T(8,128)(2,1)S(1)}, bf16[32,768]{1,0:T(8,128)(2,1)S(1)}, u32[]{:S(2)}, u32[]{:S(2)}) collective-permute-start(bf16[32,768]{1,0:T(8,128)(2,1)S(1)} %shard_map.55.refs_0_), channel_id=1, source_target_pairs={{6,0},{7,1},{0,2},{1,3},{2,4},{3,5},{4,6},{5,7},{14,8},{15,9},{8,1... | collective-permute-start | bytes 147464 | tf_op jit(solution)/shard_map/ppermute | solution.py:25
  127.3 4.6 %collective-permute-start.2 = (bf16[32,768]{1,0:T(8,128)(2,1)S(1)}, bf16[32,768]{1,0:T(8,128)(2,1)S(1)}, u32[]{:S(2)}, u32[]{:S(2)}) collective-permute-start(bf16[32,768]{1,0:T(8,128)(2,1)S(1)} %shard_map.55.refs_0_), channel_id=1, source_target_pairs={{5,0},{6,1},{7,2},{0,3},{1,4},{2,5},{3,6},{4,7},{13,8},{14,9},{15,... | collective-permute-start | bytes 147464 | tf_op jit(solution)/shard_map/ppermute | solution.py:25
  131.9 4.3 %collective-permute-start.3 = (bf16[32,768]{1,0:T(8,128)(2,1)S(1)}, bf16[32,768]{1,0:T(8,128)(2,1)S(1)}, u32[]{:S(2)}, u32[]{:S(2)}) collective-permute-start(bf16[32,768]{1,0:T(8,128)(2,1)S(1)} %shard_map.55.refs_0_), channel_id=1, source_target_pairs={{4,0},{5,1},{6,2},{7,3},{0,4},{1,5},{2,6},{3,7},{12,8},{13,9},{14,... | collective-permute-start | bytes 147464 | tf_op jit(solution)/shard_map/ppermute | solution.py:25
  136.2 4.6 %collective-permute-start.4 = (bf16[32,768]{1,0:T(8,128)(2,1)S(1)}, bf16[32,768]{1,0:T(8,128)(2,1)S(1)}, u32[]{:S(2)}, u32[]{:S(2)}) collective-permute-start(bf16[32,768]{1,0:T(8,128)(2,1)S(1)} %shard_map.55.refs_0_), channel_id=1, source_target_pairs={{3,0},{4,1},{5,2},{6,3},{7,4},{0,5},{1,6},{2,7},{11,8},{12,9},{13,... | collective-permute-start | bytes 147464 | tf_op jit(solution)/shard_map/ppermute | solution.py:25
  140.8 74.8 %collective-permute-done.refs_1_ = bf16[32,768]{1,0:T(8,128)(2,1)S(1)} collective-permute-done((bf16[32,768]{1,0:T(8,128)(2,1)S(1)}, bf16[32,768]{1,0:T(8,128)(2,1)S(1)}, u32[]{:S(2)}, u32[]{:S(2)}) %collective-permute-start) | collective-permute-done | bytes 49184 | tf_op jit(solution)/shard_map/ppermute | solution.py:25
  215.6 1.9 collective-permute-start.5
  217.5 0.8 collective-permute-done.1.refs_2_
  218.4 5.3 %collective-permute-start.6 = (bf16[32,768]{1,0:T(8,128)(2,1)S(1)}, bf16[32,768]{1,0:T(8,128)(2,1)S(1)}, u32[]{:S(2)}, u32[]{:S(2)}) collective-permute-start(bf16[32,768]{1,0:T(8,128)(2,1)S(1)} %shard_map.55.refs_0_), channel_id=1, source_target_pairs={{1,0},{2,1},{3,2},{4,3},{5,4},{6,5},{7,6},{0,7},{9,8},{10,9},{11,1... | collective-permute-start | bytes 147464 | tf_op jit(solution)/shard_map/ppermute | solution.py:25
  223.7 0.7 collective-permute-done.3.refs_4_
  224.4 0.0 collective-permute-done.4.refs_5_
  224.4 0.0 collective-permute-done.5.refs_6_
  224.4 1.0 collective-permute-done.6.refs_7_
  225.4 0.1 shard_map.56
  225.5 4.2 %collective-permute-start.7 = (bf16[256,768]{1,0:T(8,128)(2,1)S(1)}, bf16[256,768]{1,0:T(8,128)(2,1)S(1)}, u32[]{:S(2)}, u32[]{:S(2)}) collective-permute-start(bf16[256,768]{1,0:T(8,128)(2,1)S(1)} %get-tuple-element.7.refs_0_), channel_id=1, source_target_pairs={{8,0},{9,1},{10,2},{11,3},{12,4},{13,5},{14,6},{15,7},{16,8},{17,9... | collective-permute-start | bytes 1179656 | tf_op jit(solution)/shard_map/ppermute | solution.py:25
  229.8 2.6 collective-permute-start.8
  232.4 3.0 %collective-permute-start.9 = (bf16[256,512]{1,0:T(8,128)(2,1)S(1)}, bf16[256,512]{1,0:T(8,128)(2,1)S(1)}, u32[]{:S(2)}, u32[]{:S(2)}) collective-permute-start(bf16[256,512]{1,0:T(8,128)(2,1)S(1)} %get-tuple-element.8), channel_id=1, source_target_pairs={{24,0},{25,1},{26,2},{27,3},{28,4},{29,5},{30,6},{31,7},{0,8},{1,9... | collective-permute-start | bytes 786440 | tf_op jit(solution)/shard_map/ppermute | solution.py:25
  235.4 6.9 %collective-permute-done.8.refs_2_ = bf16[256,512]{1,0:T(8,128)(2,1)S(1)} collective-permute-done((bf16[256,512]{1,0:T(8,128)(2,1)S(1)}, bf16[256,512]{1,0:T(8,128)(2,1)S(1)}, u32[]{:S(2)}, u32[]{:S(2)}) %collective-permute-start.8) | collective-permute-done | bytes 262176 | tf_op jit(solution)/shard_map/ppermute | solution.py:25
  242.3 3.1 %collective-permute-done.9.refs_3_ = bf16[256,512]{1,0:T(8,128)(2,1)S(1)} collective-permute-done((bf16[256,512]{1,0:T(8,128)(2,1)S(1)}, bf16[256,512]{1,0:T(8,128)(2,1)S(1)}, u32[]{:S(2)}, u32[]{:S(2)}) %collective-permute-start.9) | collective-permute-done | bytes 262176 | tf_op jit(solution)/shard_map/ppermute | solution.py:25
  245.4 0.0 collective-permute-done.7.refs_1_
  245.4 2.6 shard_map.59.rest_ref
  248.1 1.0 copy-done.1
  249.1 6.4 %shard_map.58.most_ref = bf16[12,128,1024]{2,1,0:T(8,128)(2,1)S(1)} custom-call(s32[1]{0:T(128)} %bitcast.me_ref, bf16[256,768]{1,0:T(8,128)(2,1)S(1)} %get-tuple-element.7.refs_0_, bf16[256,768]{1,0:T(8,128)(2,1)S(1)} %collective-permute-done.7.refs_1_, bf16[256,512]{1,0:T(8,128)(2,1)S(1)} %collective-permute-done.8.refs_2_, ...), custom_call_target="tpu_custom_call" | custom-call | flops 3221225472 | bytes 8388608 | tf_op jit(solution)/shard_map/pallas_call | solution.py:117
  255.5 0.0 all-to-all-done.1.half_ref
  255.5 3.1 %shard_map.60 = f32[4,128,128]{2,1,0:T(8,128)S(1)} custom-call(bf16[12,128,1024]{2,1,0:T(8,128)(2,1)S(1)} %shard_map.58.most_ref, bf16[4,128,1024]{2,1,0:T(8,128)(2,1)} %copy-done.1, bf16[32,16,32,128]{3,2,1,0:T(8,128)(2,1)} %all-to-all-done.1.half_ref), custom_call_target="tpu_custom_call" | custom-call | flops 536870912 | bytes 8388608 | tf_op jit(solution)/shard_map/pallas_call | solution.py:180
  258.6 9.1 %all_to_all.20 = f32[4,128,128]{2,1,0:T(8,128)S(1)} all-to-all(f32[4,128,128]{2,1,0:T(8,128)S(1)} %shard_map.60), channel_id=1, replica_groups={{0,8,16,24},{1,9,17,25},{2,10,18,26},{3,11,19,27},{4,12,20,28},{5,13,21..., dimensions={0} | all-to-all | bytes 524288 | tf_op jit(solution)/shard_map/all_to_all | solution.py:34
  267.7 14.0 %all_to_all.21 = bf16[8,128,128]{2,1,0:T(8,128)(2,1)S(1)} all-to-all(bf16[8,128,128]{2,1,0:T(8,128)(2,1)S(1)} %broadcast_in_dim.34), channel_id=1, replica_groups={{0,1,2,3,4,5,6,7},{8,9,10,11,12,13,14,15},{16,17,18,19,20,21,22,23},{24..., dimensions={0} | all-to-all | bytes 524288 | tf_op jit(solution)/shard_map/all_to_all | solution.py:34
  281.8 0.7 convert_reduce_fusion
  (23 shorter events, 0.2 us)
Async XLA Ops:
  0.0 26.0 %copy-start = (s32[16,4]{0,1:T(4,128)S(1)}, s32[16,4]{0,1:T(4,128)}, u32[]{:S(2)}) copy-start(s32[16,4]{0,1:T(4,128)} %param.8) | copy-start | bytes 772
  3.6 13.5 %copy-start.3 = (bf16[1,4,128,128]{3,2,1,0:T(8,128)(2,1)S(1)}, bf16[1,4,128,128]{3,2,1,0:T(8,128)(2,1)}, u32[]{:S(2)}) copy-start(bf16[1,4,128,128]{3,2,1,0:T(8,128)(2,1)} %param.6) | copy-start | bytes 393220
  3.7 22.3 %copy-start.4 = (s32[16,4]{0,1:T(4,128)S(1)}, s32[16,4]{0,1:T(4,128)}, u32[]{:S(2)}) copy-start(s32[16,4]{0,1:T(4,128)} %param.7) | copy-start | bytes 772
  3.7 110.4 %all-to-all-start = ((bf16[32,16,32,128]{3,2,1,0:T(8,128)(2,1)}), bf16[32,16,32,128]{3,2,1,0:T(8,128)(2,1)}, u32[]{:S(2)}, u32[]{:S(2)}) async-start(bf16[32,16,32,128]{3,2,1,0:T(8,128)(2,1)} %bitcast.35), calls=%async_computation | async-start | bytes 8388608 | tf_op jit(solution)/shard_map/all_to_all | solution.py:263
  17.1 9.8 %collective-permute-start.10 = (bf16[1,4,128,128]{3,2,1,0:T(8,128)(2,1)S(1)}, bf16[1,4,128,128]{3,2,1,0:T(8,128)(2,1)S(1)}, u32[]{:S(2)}, u32[]{:S(2)}) collective-permute-start(bf16[1,4,128,128]{3,2,1,0:T(8,128)(2,1)S(1)} %copy-done.3), channel_id=1, source_target_pairs={{448,0},{480,32},{0,64},{32,96},{64,128},{96,160},{128,192},{160,2... | collective-permute-start | bytes 393224 | tf_op jit(solution)/shard_map/ppermute | solution.py:16
  19.7 7.2 %collective-permute-start.11 = (bf16[1,4,128,128]{3,2,1,0:T(8,128)(2,1)S(1)}, bf16[1,4,128,128]{3,2,1,0:T(8,128)(2,1)S(1)}, u32[]{:S(2)}, u32[]{:S(2)}) collective-permute-start(bf16[1,4,128,128]{3,2,1,0:T(8,128)(2,1)S(1)} %copy-done.3), channel_id=1, source_target_pairs={{480,0},{0,32},{32,64},{64,96},{96,128},{128,160},{160,192},{192,2... | collective-permute-start | bytes 393224 | tf_op jit(solution)/shard_map/ppermute | solution.py:16
  19.8 7.3 %collective-permute-start.12 = (bf16[1,4,128,128]{3,2,1,0:T(8,128)(2,1)S(1)}, bf16[1,4,128,128]{3,2,1,0:T(8,128)(2,1)S(1)}, u32[]{:S(2)}, u32[]{:S(2)}) collective-permute-start(bf16[1,4,128,128]{3,2,1,0:T(8,128)(2,1)S(1)} %copy-done.3), channel_id=1, source_target_pairs={{32,0},{64,32},{96,64},{128,96},{160,128},{192,160},{224,192},{256... | collective-permute-start | bytes 393224 | tf_op jit(solution)/shard_map/ppermute | solution.py:16
  22.7 6.8 %collective-permute-start.13 = (bf16[1,4,128,128]{3,2,1,0:T(8,128)(2,1)S(1)}, bf16[1,4,128,128]{3,2,1,0:T(8,128)(2,1)S(1)}, u32[]{:S(2)}, u32[]{:S(2)}) collective-permute-start(bf16[1,4,128,128]{3,2,1,0:T(8,128)(2,1)S(1)} %copy-done.3), channel_id=1, source_target_pairs={{64,0},{96,32},{128,64},{160,96},{192,128},{224,160},{256,192},{28... | collective-permute-start | bytes 393224 | tf_op jit(solution)/shard_map/ppermute | solution.py:16
  114.1 5.2 %copy-start.2 = (bf16[1,32,1024]{2,1,0:T(8,128)(2,1)S(1)}, bf16[1,32,1024]{2,1,0:T(8,128)(2,1)}, u32[]{:S(2)}) copy-start(bf16[1,32,1024]{2,1,0:T(8,128)(2,1)} %param.9) | copy-start | bytes 196612
  114.1 141.3 %all-to-all-start.1 = ((bf16[32,16,32,128]{3,2,1,0:T(8,128)(2,1)}), bf16[32,16,32,128]{3,2,1,0:T(8,128)(2,1)}, u32[]{:S(2)}, u32[]{:S(2)}) async-start(bf16[32,16,32,128]{3,2,1,0:T(8,128)(2,1)} %bitcast.34), calls=%async_computation.1 | async-start | bytes 8388608 | tf_op jit(solution)/shard_map/all_to_all | solution.py:263
  119.4 96.2 %collective-permute-start = (bf16[32,768]{1,0:T(8,128)(2,1)S(1)}, bf16[32,768]{1,0:T(8,128)(2,1)S(1)}, u32[]{:S(2)}, u32[]{:S(2)}) collective-permute-start(bf16[32,768]{1,0:T(8,128)(2,1)S(1)} %shard_map.55.refs_0_), channel_id=1, source_target_pairs={{7,0},{0,1},{1,2},{2,3},{3,4},{4,5},{5,6},{6,7},{15,8},{8,9},{9,10... | collective-permute-start | bytes 147464 | tf_op jit(solution)/shard_map/ppermute | solution.py:25
  123.0 95.4 %collective-permute-start.1 = (bf16[32,768]{1,0:T(8,128)(2,1)S(1)}, bf16[32,768]{1,0:T(8,128)(2,1)S(1)}, u32[]{:S(2)}, u32[]{:S(2)}) collective-permute-start(bf16[32,768]{1,0:T(8,128)(2,1)S(1)} %shard_map.55.refs_0_), channel_id=1, source_target_pairs={{6,0},{7,1},{0,2},{1,3},{2,4},{3,5},{4,6},{5,7},{14,8},{15,9},{8,1... | collective-permute-start | bytes 147464 | tf_op jit(solution)/shard_map/ppermute | solution.py:25
  127.3 96.4 %collective-permute-start.2 = (bf16[32,768]{1,0:T(8,128)(2,1)S(1)}, bf16[32,768]{1,0:T(8,128)(2,1)S(1)}, u32[]{:S(2)}, u32[]{:S(2)}) collective-permute-start(bf16[32,768]{1,0:T(8,128)(2,1)S(1)} %shard_map.55.refs_0_), channel_id=1, source_target_pairs={{5,0},{6,1},{7,2},{0,3},{1,4},{2,5},{3,6},{4,7},{13,8},{14,9},{15,... | collective-permute-start | bytes 147464 | tf_op jit(solution)/shard_map/ppermute | solution.py:25
  131.9 92.5 %collective-permute-start.3 = (bf16[32,768]{1,0:T(8,128)(2,1)S(1)}, bf16[32,768]{1,0:T(8,128)(2,1)S(1)}, u32[]{:S(2)}, u32[]{:S(2)}) collective-permute-start(bf16[32,768]{1,0:T(8,128)(2,1)S(1)} %shard_map.55.refs_0_), channel_id=1, source_target_pairs={{4,0},{5,1},{6,2},{7,3},{0,4},{1,5},{2,6},{3,7},{12,8},{13,9},{14,... | collective-permute-start | bytes 147464 | tf_op jit(solution)/shard_map/ppermute | solution.py:25
  136.2 88.3 %collective-permute-start.4 = (bf16[32,768]{1,0:T(8,128)(2,1)S(1)}, bf16[32,768]{1,0:T(8,128)(2,1)S(1)}, u32[]{:S(2)}, u32[]{:S(2)}) collective-permute-start(bf16[32,768]{1,0:T(8,128)(2,1)S(1)} %shard_map.55.refs_0_), channel_id=1, source_target_pairs={{3,0},{4,1},{5,2},{6,3},{7,4},{0,5},{1,6},{2,7},{11,8},{12,9},{13,... | collective-permute-start | bytes 147464 | tf_op jit(solution)/shard_map/ppermute | solution.py:25
  215.6 8.8 %collective-permute-start.5 = (bf16[32,768]{1,0:T(8,128)(2,1)S(1)}, bf16[32,768]{1,0:T(8,128)(2,1)S(1)}, u32[]{:S(2)}, u32[]{:S(2)}) collective-permute-start(bf16[32,768]{1,0:T(8,128)(2,1)S(1)} %shard_map.55.refs_0_), channel_id=1, source_target_pairs={{2,0},{3,1},{4,2},{5,3},{6,4},{7,5},{0,6},{1,7},{10,8},{11,9},{12,... | collective-permute-start | bytes 147464 | tf_op jit(solution)/shard_map/ppermute | solution.py:25
  218.4 7.1 %collective-permute-start.6 = (bf16[32,768]{1,0:T(8,128)(2,1)S(1)}, bf16[32,768]{1,0:T(8,128)(2,1)S(1)}, u32[]{:S(2)}, u32[]{:S(2)}) collective-permute-start(bf16[32,768]{1,0:T(8,128)(2,1)S(1)} %shard_map.55.refs_0_), channel_id=1, source_target_pairs={{1,0},{2,1},{3,2},{4,3},{5,4},{6,5},{7,6},{0,7},{9,8},{10,9},{11,1... | collective-permute-start | bytes 147464 | tf_op jit(solution)/shard_map/ppermute | solution.py:25
  225.5 19.9 %collective-permute-start.7 = (bf16[256,768]{1,0:T(8,128)(2,1)S(1)}, bf16[256,768]{1,0:T(8,128)(2,1)S(1)}, u32[]{:S(2)}, u32[]{:S(2)}) collective-permute-start(bf16[256,768]{1,0:T(8,128)(2,1)S(1)} %get-tuple-element.7.refs_0_), channel_id=1, source_target_pairs={{8,0},{9,1},{10,2},{11,3},{12,4},{13,5},{14,6},{15,7},{16,8},{17,9... | collective-permute-start | bytes 1179656 | tf_op jit(solution)/shard_map/ppermute | solution.py:25
  229.8 12.6 %collective-permute-start.8 = (bf16[256,512]{1,0:T(8,128)(2,1)S(1)}, bf16[256,512]{1,0:T(8,128)(2,1)S(1)}, u32[]{:S(2)}, u32[]{:S(2)}) collective-permute-start(bf16[256,512]{1,0:T(8,128)(2,1)S(1)} %get-tuple-element.8), channel_id=1, source_target_pairs={{16,0},{17,1},{18,2},{19,3},{20,4},{21,5},{22,6},{23,7},{24,8},{25... | collective-permute-start | bytes 786440 | tf_op jit(solution)/shard_map/ppermute | solution.py:25
  232.4 13.1 %collective-permute-start.9 = (bf16[256,512]{1,0:T(8,128)(2,1)S(1)}, bf16[256,512]{1,0:T(8,128)(2,1)S(1)}, u32[]{:S(2)}, u32[]{:S(2)}) collective-permute-start(bf16[256,512]{1,0:T(8,128)(2,1)S(1)} %get-tuple-element.8), channel_id=1, source_target_pairs={{24,0},{25,1},{26,2},{27,3},{28,4},{29,5},{30,6},{31,7},{0,8},{1,9... | collective-permute-start | bytes 786440 | tf_op jit(solution)/shard_map/ppermute | solution.py:25
  248.1 1.0 copy-start.1
